TPU v7x, 32 devices: a whole 2x2x4 slice. The times are simulated.
32 devices in a mesh: lat: 8 (over y, x, core), chan: 4 (over z).
Axes of the slice: x: 2, y: 2, z: 4, core: 2. Of those that a mesh axis runs over, the one named last changes fastest.
Arguments:
- state: bfloat16 [256, 64, 1440], P('chan', 'lat'), may hold values from -6 to 6
- kernel: bfloat16 [3, 3, 256, 256], replicated, may hold values from -0.125 to 0.125
- bias: float32 [256], P('chan'), may hold values from -3 to 3
- innovations: float32 [256, 8, 8, 1024], P('chan', 'lat'), may hold values from -6 to 6
- interp: bfloat16 [4, 8, 8, 1024], P(None, 'lat'), may hold values from 0 to 1
- cells: int32 [8, 8, 1024], P('lat'), may hold values from 0 to 90719, as said below
- counts: int32 [8, 8], P('lat'), may hold values from 1 to 1024, as said below
Outputs:
- grad_state: bfloat16 [256, 64, 1440], P('chan', 'lat')
- departures: float32 [256, 8, 8, 1024], P('chan', 'lat')
Inputs may be any that keep to these rules, and one draw needn't show every extreme that they name: `cells`: every observation of slab d has its first corner in rows 8 d to 8 d + 6. `counts`: in every draw some slab receives 1024 used slots from every instrument shard.
All inputs are finite; a program needn't handle non-finite values.
Results may differ from a plain program's by a relative error of at most 0.023.
Values may be sent and summed in bfloat16 or wider, within the bound.
No kernel may reach another device: no remote copies, remote signals or barrier semaphores. Data moves between devices by JAX's collectives and lax.ppermute only.
A program may use at most 256 MiB of HBM per device.

v0:
```python
import jax
import jax.numpy as jnp
from jax import lax
from jax.sharding import PartitionSpec as P

KERNEL_SPACING = 8


def extended(block, sides, width):
    for axis, dim in sides:
        count = lax.axis_size(axis)
        forward = [(i, i + 1) for i in range(count - 1)]
        backward = [(target, source) for source, target in forward]
        low = lax.ppermute(
            lax.slice_in_dim(block, block.shape[dim] - width, None, axis=dim), axis, forward
        )
        high = lax.ppermute(lax.slice_in_dim(block, 0, width, axis=dim), axis, backward)
        block = jnp.concatenate([low, block, high], axis=dim)
    return block


def gelu_value(value):
    return 0.5 * value * (1.0 + jax.scipy.special.erf(value * 0.7071067811865476))


def gelu_slope(value):
    return (
        0.5 * (1.0 + jax.scipy.special.erf(value * 0.7071067811865476))
        + value * jnp.exp(-0.5 * value * value) * 0.3989422804014327
    )


def tap_stack(padded_field, direction_sign, row_count):
    field_pieces = []
    for row_offset in range(3):
        for column_offset in range(3):
            start_offset = KERNEL_SPACING + direction_sign * (row_offset - 1) * KERNEL_SPACING
            part = lax.slice_in_dim(padded_field, start_offset, start_offset + row_count, axis=1)
            field_pieces.append(
                jnp.roll(part, -direction_sign * (column_offset - 1) * KERNEL_SPACING, axis=2)
            )
    stacked = jnp.stack(field_pieces)
    return stacked.reshape(9 * padded_field.shape[0], row_count * padded_field.shape[2])


def channel_mix(grid_field, kernel_t, direction_sign):
    group, row_count, width = grid_field.shape
    total_channels = kernel_t.shape[0]
    owner = lax.axis_index("chan")
    padded_field = extended(grid_field, (("lat", 1),), KERNEL_SPACING)
    stacked = tap_stack(padded_field, direction_sign, row_count)
    local_weights = lax.dynamic_slice_in_dim(kernel_t, owner * group, group, 3).reshape(
        total_channels, 9 * group
    )
    return lax.psum_scatter(
        jnp.dot(local_weights, stacked, preferred_element_type=jnp.float32)
        .reshape(group * lax.axis_size("chan"), row_count, width)
        .astype(jnp.bfloat16),
        "chan",
        scatter_dimension=0,
        tiled=True,
    ).astype(jnp.float32)


def shards(state, kernel, bias, innovations, interp, cells, counts):
    group, row_count, width = state.shape
    forward_kernel = jnp.transpose(kernel, (2, 0, 1, 3))
    backward_kernel = jnp.transpose(kernel, (3, 0, 1, 2))
    pre = channel_mix(state, forward_kernel, 1) + bias[:, None, None]
    hidden = gelu_value(pre)
    flat_hidden = hidden.reshape(group, row_count * width)
    slots = jnp.arange(innovations.shape[3], dtype=jnp.int32)
    mask = (slots[None, :] < counts[0][:, None]).astype(jnp.float32)
    masked_values = innovations * mask[None, None]
    masked_weights = interp.astype(jnp.float32) * mask[None, None]
    got_values, got_weights = (
        lax.all_to_all(
            masked_values.astype(jnp.bfloat16), "lat", split_axis=2, concat_axis=1, tiled=True
        ).astype(masked_values.dtype),
        lax.all_to_all(
            masked_weights.astype(jnp.bfloat16), "lat", split_axis=2, concat_axis=1, tiled=True
        ).astype(masked_weights.dtype),
    )
    got_cells = lax.all_to_all(cells, "lat", split_axis=1, concat_axis=0, tiled=True)
    local_cells = got_cells - lax.axis_index("lat") * row_count * width
    row_index = local_cells // width
    col_index = local_cells % width
    corner_one = row_index * width + (col_index + 1) % width
    corners = [local_cells, corner_one, local_cells + width, corner_one + width]
    model = jnp.zeros(got_values.shape, jnp.float32)
    for which in range(4):
        model = model + got_weights[which][None] * jnp.take(flat_hidden, corners[which], axis=1)
    local_departures = model - got_values
    departures = lax.all_to_all(
        local_departures.astype(jnp.bfloat16), "lat", split_axis=1, concat_axis=2, tiled=True
    ).astype(local_departures.dtype)
    grad_hidden = jnp.zeros((group, row_count * width), jnp.float32)
    for which in range(4):
        grad_hidden = grad_hidden.at[:, corners[which].reshape(-1)].add(
            (got_weights[which][None] * local_departures).reshape(group, -1)
        )
    grad_pre = (grad_hidden.reshape(pre.shape) * gelu_slope(pre)).astype(jnp.bfloat16)
    grad_state = channel_mix(grad_pre, backward_kernel, -1).astype(jnp.bfloat16)
    return (grad_state, departures)


def solution(mesh):
    return jax.shard_map(
        shards,
        mesh=mesh,
        in_specs=(
            P("chan", "lat", None),
            P(),
            P("chan"),
            P("chan", "lat", None, None),
            P(None, "lat", None, None),
            P("lat", None, None),
            P("lat", None),
        ),
        out_specs=(P("chan", "lat", None), P("chan", "lat", None, None)),
        check_vma=False,
    )
```

profile of v0, /device:TPU:0, one launch (start us, length us, event | category | flops | bytes accessed | tf_op | source)
XLA Modules:
  0.0 894.1 jit_solution(1340920264573949839)
XLA Ops:
  7.2 3.6 collective-permute-start
  10.9 1.3 collective-permute-start.1
  14.4 1.1 fusion.56
  15.5 2.9 fusion.58
  19.5 1.8 fusion.26
  21.4 2.7 bitcast_dynamic-update-slice_fusion.5
  24.0 1.3 fusion.27
  25.3 1.9 fusion.28
  27.3 1.2 bitcast_dynamic-update-slice_fusion.4
  28.5 1.4 fusion.29
  29.9 2.9 fusion.54
  32.9 1.1 fusion.55
  34.0 1.9 fusion.30
  35.8 2.7 bitcast_dynamic-update-slice_fusion.3
  38.5 1.3 fusion.31
  39.9 27.0 %reshape.416 = bf16[576,11520]{1,0:T(8,128)(2,1)} reshape(bf16[9,64,8,1440]{3,2,1,0:T(8,128)(2,1)} %fusion.31) | data formatting | bytes 26542080 | tf_op jit(solution)/shard_map/reshape | solution.py:43
  66.9 28.0 %dot_general.15 = bf16[8,1440,576]{1,0,2:T(8,128)(2,1)} reshape(bf16[11520,576]{0,1:T(8,128)(2,1)} %bitcast.220) | data formatting | bytes 26542080 | tf_op jit(solution)/shard_map/dot_general | solution.py:56
  94.8 24.5 %fusion.4 = bf16[256,8,1440]{2,0,1:T(8,128)(2,1)} fusion(bf16[256,576,1]{0,1,2:T(8,128)(2,1)S(1)} %bitcast.234, bf16[8,1440,576]{1,0,2:T(8,128)(2,1)} %dot_general.15), kind=kOutput, calls=%fused_computation.12 | convolution fusion | flops 3400335360 | bytes 19464192 | tf_op jit(solution)/shard_map/dot_general | solution.py:56
  120.7 33.1 %all-to-all-start = ((s32[1,8,1024]{2,0,1:T(1,128)}), s32[1,8,1024]{2,0,1:T(1,128)S(1)}, u32[]{:S(2)}, u32[]{:S(2)}) async-start(s32[1,8,1024]{2,0,1:T(1,128)} %copy.92), calls=%async_computation | async-start | bytes 65536 | tf_op jit(solution)/shard_map/all_to_all | solution.py:84
  153.9 2.1 fusion.25
  156.7 1.9 all-to-all-done
  158.6 3.4 all-to-all-start.1
  164.1 1.1 compare_select_fusion.5
  167.0 4.3 all-to-all-start.2
  171.3 89.6 %reduce-scatter.3.cloned.1.call-done = bf16[64,8,1440]{2,0,1:T(8,128)(2,1)} async-done(((bf16[256,8,1440]{2,0,1:T(8,128)(2,1)}), bf16[64,8,1440]{2,0,1:T(8,128)(2,1)}) %reduce-scatter.3.cloned.1.call-update) | async-done | bytes 1474576 | tf_op jit(solution)/shard_map/reduce_scatter | solution.py:55
  260.9 3.7 multiply_multiply_fusion.1
  264.6 5.7 copy.124
  270.2 30.6 %gather_fusion.2 = f32[8192,64]{1,0:T(8,128)} fusion(f32[64,11520]{0,1:T(8,128)} %bitcast.215, s32[8192]{0:T(1024)S(1)} %get-tuple-element.69), kind=kCustom, calls=%fused_computation.2.clone | custom fusion | bytes 4227072 | tf_op jit(solution)/shard_map/jit(_take)/gather | solution.py:92
  300.8 2.8 copy.103
  303.6 33.3 %gather_fusion.3 = f32[8192,64]{1,0:T(8,128)} fusion(f32[64,11520]{0,1:T(8,128)} %bitcast.216, s32[8192]{0:T(1024)} %get-tuple-element.68), kind=kCustom, calls=%fused_computation.3.clone | custom fusion | bytes 4227072 | tf_op jit(solution)/shard_map/jit(_take)/gather | solution.py:92
  336.9 3.8 copy.105
  340.7 33.3 %gather_fusion.1 = f32[8192,64]{1,0:T(8,128)} fusion(f32[64,11520]{0,1:T(8,128)} %bitcast.217, s32[8192]{0:T(1024)} %get-tuple-element.70), kind=kCustom, calls=%fused_computation.1.clone | custom fusion | bytes 4227072 | tf_op jit(solution)/shard_map/jit(_take)/gather | solution.py:92
  373.9 3.8 copy.101
  377.7 30.6 %gather_fusion = f32[8192,64]{1,0:T(8,128)} fusion(f32[64,11520]{0,1:T(8,128)} %bitcast.218, s32[8192]{0:T(1024)S(1)} %get-tuple-element.71), kind=kCustom, calls=%fused_computation.clone | custom fusion | bytes 4227072 | tf_op jit(solution)/shard_map/jit(_take)/gather | solution.py:92
  408.3 3.8 copy.99
  412.1 5.7 convert_bitcast_fusion
  417.8 2.9 broadcast_multiply_fusion
  420.9 2.7 copy.108
  423.6 1.7 copy.131
  425.4 2.8 copy.110
  428.2 1.7 copy.132
  429.9 2.8 copy.112
  432.7 1.7 copy.133
  434.5 2.8 copy.114
  437.3 47.2 %scatter_custom_fusion = f32[64,11520]{0,1:T(8,128)} fusion(s32[8192]{0:T(1024)} %bitcast.244, f32[8192,64]{1,0:T(8,128)} %copy.108, f32[]{:T(128)} %constant.32.clone.1), kind=kCustom, calls=%fused_computation.24 | custom fusion | flops 524288 | bytes 2949632 | tf_op jit(solution)/shard_map/scatter-add | solution.py:99
  484.4 45.1 %scatter_fusion = f32[64,11520]{0,1:T(8,128)} fusion(f32[64,11520]{0,1:T(8,128)} %scatter_custom_fusion, s32[8192]{0:T(1024)S(1)} %bitcast.239, f32[8192,64]{1,0:T(8,128)} %copy.110), kind=kCustom, calls=%fused_computation.5 | custom fusion | flops 524288 | bytes 6324224 | tf_op jit(solution)/shard_map/scatter-add | solution.py:99
  529.5 45.2 %scatter_fusion.1 = f32[64,11520]{0,1:T(8,128)} fusion(f32[64,11520]{0,1:T(8,128)} %scatter_fusion, s32[8192]{0:T(1024)S(1)} %bitcast.238, f32[8192,64]{1,0:T(8,128)} %copy.112), kind=kCustom, calls=%fused_computation.6 | custom fusion | flops 524288 | bytes 6324224 | tf_op jit(solution)/shard_map/scatter-add | solution.py:99
  574.7 45.1 %scatter_fusion.2 = f32[64,11520]{0,1:T(8,128)} fusion(f32[64,11520]{0,1:T(8,128)} %scatter_fusion.1, s32[8192]{0:T(1024)S(1)} %bitcast.237, f32[8192,64]{1,0:T(8,128)} %copy.114), kind=kCustom, calls=%fused_computation.7 | custom fusion | flops 524288 | bytes 6324224 | tf_op jit(solution)/shard_map/scatter-add | solution.py:99
  619.8 6.1 copy.116
  625.9 3.1 fusion.15
  629.0 1.3 collective-permute-start.2
  630.3 3.1 collective-permute-start.3
  633.6 1.2 fusion.51
  634.8 1.2 fusion.53
  638.2 1.2 fusion.49
  640.6 21.6 %copy.117 = bf16[9,64,8,1440]{3,2,1,0:T(8,128)(2,1)} copy(bf16[9,64,8,1440]{3,1,2,0:T(8,128)(2,1)S(1)} %fusion.37) | data formatting | bytes 26542080 | tf_op jit(solution)/shard_map/stack | solution.py:42
  662.3 26.8 %reshape.423 = bf16[576,11520]{1,0:T(8,128)(2,1)} reshape(bf16[9,64,8,1440]{3,2,1,0:T(8,128)(2,1)} %copy.117) | data formatting | bytes 26542080 | tf_op jit(solution)/shard_map/reshape | solution.py:43
  689.1 27.9 %dot_general.18 = bf16[8,1440,576]{1,0,2:T(8,128)(2,1)} reshape(bf16[11520,576]{0,1:T(8,128)(2,1)} %bitcast.221) | data formatting | bytes 26542080 | tf_op jit(solution)/shard_map/dot_general | solution.py:56
  717.0 24.7 %fusion.7 = bf16[256,8,1440]{2,0,1:T(8,128)(2,1)} fusion(bf16[256,576,1]{0,1,2:T(8,128)(2,1)S(1)} %bitcast.235, bf16[8,1440,576]{1,0,2:T(8,128)(2,1)} %dot_general.18), kind=kOutput, calls=%fused_computation.13 | convolution fusion | flops 3400335360 | bytes 19464192 | tf_op jit(solution)/shard_map/dot_general | solution.py:56
  741.7 1.2 copy-done.3
  742.9 49.0 %all_to_all.16 = bf16[64,8,1,1024]{3,0,2,1:T(8,128)(2,1)S(1)} all-to-all(bf16[64,8,1,1024]{3,0,2,1:T(8,128)(2,1)S(1)} %copy-done.3), channel_id=1, replica_groups=mesh['lat'=8,'chan'=4] {'lat'}, dimensions={1} | all-to-all | bytes 2097152 | tf_op jit(solution)/shard_map/all_to_all | solution.py:94
  792.2 2.5 copy.121
  794.7 88.7 %reduce-scatter.5.cloned.1.call-done = bf16[64,8,1440]{2,0,1:T(8,128)(2,1)} async-done(((bf16[256,8,1440]{2,0,1:T(8,128)(2,1)}), bf16[64,8,1440]{2,0,1:T(8,128)(2,1)}) %reduce-scatter.5.cloned.1.call-update) | async-done | bytes 1474576 | tf_op jit(solution)/shard_map/reduce_scatter | solution.py:55
  883.4 3.4 copy.120
  (67 shorter events, 13.3 us)
Async XLA Ops:
  7.2 5.0 copy-start
  7.2 7.3 copy-start.1
  7.2 253.7 %reduce-scatter.3.cloned.1.call-start = ((), (), s32[]{:S(2)}) async-start(), calls=%async_computation.6 | async-start | bytes 7864320 | tf_op jit(solution)/shard_map/reduce_scatter | solution.py:55
  7.2 8.3 collective-permute-start
  10.9 19.1 %collective-permute-start.1 = (bf16[64,8,1440]{2,1,0:T(8,128)(2,1)}, bf16[64,8,1440]{2,1,0:T(8,128)(2,1)}, u32[]{:S(2)}, u32[]{:S(2)}) collective-permute-start(bf16[64,8,1440]{2,1,0:T(8,128)(2,1)} %param.9), channel_id=1, source_target_pairs={{4,0},{8,4},{12,8},{16,12},{20,16},{24,20},{28,24},{5,1},{9,5},{13... | collective-permute-start | bytes 4423688 | tf_op jit(solution)/shard_map/ppermute | solution.py:17
  66.9 28.0 %copy-start.5 = (bf16[256,3,3,64]{0,3,2,1:T(8,128)(2,1)S(1)}, bf16[256,3,3,64]{0,3,2,1:T(8,128)(2,1)}, u32[]{:S(2)}) copy-start(bf16[256,3,3,64]{0,3,2,1:T(8,128)(2,1)} %copy.95) | copy-start | bytes 884740
  119.3 0.8 copy-start.9
  119.3 34.5 %copy-start.12 = (s32[1,8]{1,0:T(1,128)S(1)}, s32[1,8]{1,0:T(1,128)}, u32[]{:S(2)}) copy-start(s32[1,8]{1,0:T(1,128)} %param.15) | copy-start | bytes 100
  119.3 34.5 %copy-start.4 = (f32[64,1,8,1024]{3,2,1,0:T(8,128)S(1)}, f32[64,1,8,1024]{3,2,1,0:T(8,128)}, u32[]{:S(2)}) copy-start(f32[64,1,8,1024]{3,2,1,0:T(8,128)} %param.12) | copy-start | bytes 6291460
  120.1 35.9 %copy-start.6 = (bf16[4,1,8,1024]{3,2,1,0:T(8,128)(2,1)S(1)}, bf16[4,1,8,1024]{3,2,1,0:T(8,128)(2,1)}, u32[]{:S(2)}) copy-start(bf16[4,1,8,1024]{3,2,1,0:T(8,128)(2,1)} %param.13) | copy-start | bytes 196612
  120.7 37.9 %all-to-all-start = ((s32[1,8,1024]{2,0,1:T(1,128)}), s32[1,8,1024]{2,0,1:T(1,128)S(1)}, u32[]{:S(2)}, u32[]{:S(2)}) async-start(s32[1,8,1024]{2,0,1:T(1,128)} %copy.92), calls=%async_computation | async-start | bytes 65536 | tf_op jit(solution)/shard_map/all_to_all | solution.py:84
  156.0 104.8 %copy-start.10 = (f32[64]{0:T(128)S(1)}, f32[64]{0:T(128)}, u32[]{:S(2)}) copy-start(f32[64]{0:T(128)} %param.11) | copy-start | bytes 772
  158.6 8.3 all-to-all-start.1
  167.0 245.2 %all-to-all-start.2 = ((bf16[64,1,8,1024]{3,0,1,2:T(8,128)(2,1)}), bf16[64,1,8,1024]{3,0,1,2:T(8,128)(2,1)}, u32[]{:S(2)}, u32[]{:S(2)}) async-start(bf16[64,1,8,1024]{3,0,1,2:T(8,128)(2,1)} %fusion.25), calls=%async_computation.3 | async-start | bytes 2097152 | tf_op jit(solution)/shard_map/all_to_all | solution.py:77
  171.2 712.2 %reduce-scatter.5.cloned.1.call-start = ((), (), s32[]{:S(2)}) async-start(), calls=%async_computation.7 | async-start | bytes 7864320 | tf_op jit(solution)/shard_map/reduce_scatter | solution.py:55
  408.3 3.8 copy-start.7
  408.3 3.8 copy-start.8
  619.8 6.1 copy-start.2
  619.8 6.1 copy-start.11
  629.0 5.8 collective-permute-start.2
  630.3 7.9 collective-permute-start.3
  741.7 1.2 copy-start.3
Sparse Core Ops, SparseCore 0:
  119.5 141.3 reduce-scatter.2
  741.8 141.5 reduce-scatter.4
where the time goes:
time: 904 us; the launch traced here: 894 us
  local copies, waits for them, and re-layouts  333 us (37%)
  other arithmetic  217 us (24%)
  waiting for transfers between devices  181 us (20%)
  starting transfers between devices  50.1 us (6%)
  matrix products  49.2 us (5%)
  blocking collectives  49 us (5%)
  between operations  14.8 us (2%)
    scatter-add x4, other arithmetic, shards(): grad_hidden.at[:, corners[which].reshape(-1)]  183 us
    reduce_scatter x2, waiting for transfers between devices, channel_mix(): lax.psum_scatter(jnp.dot(local_weights, stacked, preferred_element_type=j...  178 us
    gather x8, local copies, waits for them, and re-layouts, shards(): jnp.take(flat_hidden, corners[which], axis=1)  142 us
    dot_general x2, local copies, waits for them, and re-layouts, channel_mix(): jnp.dot(local_weights, stacked, preferred_element_type=jnp.float32)  55.9 us
    reshape x2, local copies, waits for them, and re-layouts, tap_stack(): stacked.reshape(9 * padded_field.shape[0], row_count * padded_field.shape...  53.8 us
    dot_general x2, matrix products, channel_mix(): jnp.dot(local_weights, stacked, preferred_element_type=jnp.float32)  49.2 us
    all_to_all x1, blocking collectives, shards(): lax.all_to_all(local_departures.astype(jnp.bfloat16), 'lat', split_axis=1...  49 us
    all_to_all x1, starting transfers between devices, shards(): lax.all_to_all(cells, 'lat', split_axis=1, concat_axis=0, tiled=True)  33.1 us
  transfers between devices with their start and end apart: 9, of which 4 were waited for; matrix products, arithmetic and copies ran while one was open for 21% of the time, Pallas kernels for 0%

commit v1 on v0

v1 whole, which is shorter than its diff:
```python
import functools

import jax
import jax.numpy as jnp
from jax import lax
from jax.experimental import pallas as pl
from jax.experimental.pallas import tpu as pltpu
from jax.sharding import PartitionSpec as P

SPACING = 8
LANES = 128
STEP = 120
TOGETHER = 4
OBS = 256

VMEM = pl.BlockSpec(memory_space=pltpu.VMEM)
SMEM = pl.BlockSpec(memory_space=pltpu.SMEM)
PARAMS = pltpu.CompilerParams(vmem_limit_bytes=56 * 1024 * 1024)


def padded_width(width):
    return -(-(width + 3 * SPACING) // LANES) * LANES


def lane_iota(shape):
    return lax.broadcasted_iota(jnp.int32, shape, len(shape) - 1)


def wrapped_tail(first, tail, rem):
    lane = lane_iota(tail.shape)
    head = pltpu.roll(first, rem, 1)
    end = pltpu.roll(tail, LANES - rem, 1)
    out = jnp.where(lane < rem, tail, jnp.where(lane < rem + 2 * SPACING, head, 0.0))
    return jnp.where(lane >= LANES - SPACING, end, out)


def split_rows_kernel(parts, rounds, place_ref, state_ref, *refs):
    outs, rows_ref = refs[:-1], refs[-1]
    group, rows, width = state_ref.shape
    wide = outs[0].shape[1]
    main = width // LANES * LANES
    rem = width - main
    place = place_ref[0]
    tiles = wide // LANES
    for tile in range(tiles):
        size = min(LANES, width - tile * LANES)
        part = state_ref[:, :, tile * LANES:tile * LANES + size].astype(jnp.float32)
        rows_ref[tile, :, :size] = part.reshape(group * rows, size)
    for turn in range(rounds):
        for k in range(parts):
            row = turn * parts + (place ^ k)
            out = outs[turn * parts + k]
            strips = [rows_ref[tile, pl.ds(row, group, stride=rows), :] for tile in range(tiles)]
            for tile in range(tiles - 1):
                out[:, tile * LANES:(tile + 1) * LANES] = strips[tile].astype(jnp.bfloat16)
            out[:, main:] = wrapped_tail(strips[0], strips[-1], rem).astype(jnp.bfloat16)


def split_rows(place, state, parts, wide):
    group, rows, width = state.shape
    rounds = rows // parts
    return pl.pallas_call(
        functools.partial(split_rows_kernel, parts, rounds),
        out_shape=[jax.ShapeDtypeStruct((group, wide), jnp.bfloat16)] * rows,
        in_specs=[SMEM, VMEM],
        out_specs=[VMEM] * rows,
        scratch_shapes=[pltpu.VMEM((wide // LANES, group * rows, LANES), jnp.float32)],
        compiler_params=PARAMS,
        name="split_rows",
    )(place, state)


def join_rows_kernel(parts, rounds, place_ref, *refs):
    pieces, out_ref, rows_ref = refs[:-2], refs[-2], refs[-1]
    group, rows, width = out_ref.shape
    place = place_ref[0]
    for turn in range(rounds):
        for k in range(parts):
            row = turn * parts + (place ^ k)
            piece = pieces[turn * parts + k]
            for tile in range(rows_ref.shape[0]):
                part = piece[:, tile * LANES:(tile + 1) * LANES].astype(jnp.float32)
                rows_ref[tile, pl.ds(row, group, stride=rows), :] = part
    for tile in range(rows_ref.shape[0]):
        size = min(LANES, width - tile * LANES)
        part = rows_ref[tile, :, :size].reshape(group, rows, size)
        out_ref[:, :, tile * LANES:tile * LANES + size] = part.astype(jnp.bfloat16)


def join_rows(place, pieces, parts, width):
    group, wide = pieces[0].shape
    rows = len(pieces)
    return pl.pallas_call(
        functools.partial(join_rows_kernel, parts, rows // parts),
        out_shape=jax.ShapeDtypeStruct((group, rows, width), jnp.bfloat16),
        in_specs=[SMEM] + [VMEM] * rows,
        out_specs=VMEM,
        scratch_shapes=[pltpu.VMEM((wide // LANES, group * rows, LANES), jnp.float32)],
        compiler_params=PARAMS,
        name="join_rows",
    )(place, *pieces)


def assemble_kernel(place_ref, *refs):
    pieces, out_ref = refs[:-1], refs[-1]
    group = pieces[0].shape[0]
    for k, piece in enumerate(pieces):
        start = pl.multiple_of((place_ref[0] ^ k) * group, group)
        out_ref[pl.ds(start, group), :] = piece[...]


def assemble(place, pieces):
    group, wide = pieces[0].shape
    return pl.pallas_call(
        assemble_kernel,
        out_shape=jax.ShapeDtypeStruct((group * len(pieces), wide), jnp.bfloat16),
        in_specs=[SMEM] + [VMEM] * len(pieces),
        out_specs=VMEM,
        compiler_params=PARAMS,
        name="assemble",
    )(place, *pieces)


def conv_kernel(place_ref, weights_ref, below_ref, here_ref, above_ref, *refs):
    outs, sums_ref = refs[:-1], refs[-1]
    group, wide = outs[0].shape
    total = here_ref.shape[0]
    columns = 2 * LANES

    @pl.loop(0, wide // columns)
    def _(tile):
        at = pl.ds(pl.multiple_of(tile * columns, columns), columns)
        part = jnp.dot(weights_ref[1], here_ref[:, at], preferred_element_type=jnp.float32)
        part += jnp.dot(weights_ref[0], below_ref[:, at], preferred_element_type=jnp.float32)
        part += jnp.dot(weights_ref[2], above_ref[:, at], preferred_element_type=jnp.float32)
        sums_ref[:, at] = part

    for k, out in enumerate(outs):
        start = (place_ref[0] ^ k) * group
        left = sums_ref[pl.ds(pl.multiple_of(start, group), group), :]
        middle = sums_ref[pl.ds(pl.multiple_of(start + total, group), group), :]
        right = sums_ref[pl.ds(pl.multiple_of(start + 2 * total, group), group), :]
        mixed = middle + pltpu.roll(left, SPACING, 1) + pltpu.roll(right, wide - SPACING, 1)
        out[...] = mixed.astype(jnp.bfloat16)


def conv(place, weights, below, here, above, parts):
    total, wide = here.shape
    group = total // parts
    return pl.pallas_call(
        conv_kernel,
        out_shape=[jax.ShapeDtypeStruct((group, wide), jnp.bfloat16)] * parts,
        in_specs=[SMEM] + [VMEM] * 4,
        out_specs=[VMEM] * parts,
        scratch_shapes=[pltpu.VMEM((3 * total, wide), jnp.float32)],
        compiler_params=PARAMS,
        cost_estimate=pl.CostEstimate(
            flops=18 * total * total * wide, bytes_accessed=8 * total * wide + 18 * total * total, transcendentals=0
        ),
        name="conv",
    )(place, weights, below, here, above)


def pack_obs_kernel(width, place_ref, counts_ref, values_ref, weights_ref, cells_ref, *refs):
    outs, tiles_ref = refs[:-1], refs[-1]
    slabs = len(outs)
    group = values_ref.shape[0] // slabs
    slots = values_ref.shape[1]
    blocks = -(-width // STEP)
    for tile in range(slots // LANES):
        tiles_ref[tile] = values_ref[:, tile * LANES:(tile + 1) * LANES]
    for k, out in enumerate(outs):
        slab = place_ref[0] ^ k
        used = lane_iota((1, slots)) < counts_ref[0, slab]
        values = jnp.concatenate(
            [tiles_ref[tile, pl.ds(slab, group, stride=slabs), :] for tile in range(slots // LANES)], axis=1
        )
        out[:group, :] = jnp.where(used, values, 0.0).astype(jnp.bfloat16)
        weights = jnp.where(used, weights_ref[slab], 0.0)
        local = (cells_ref[slab] - slab * (SPACING * width)).astype(jnp.float32)
        row = jnp.clip(jnp.floor((local + 0.5) * (1.0 / width)), 0.0, SPACING - 2.0)
        column = local - row * width
        block = jnp.clip(jnp.floor((column + 0.5) * (1.0 / STEP)), 0.0, blocks - 1.0)
        tail = jnp.concatenate(
            [weights, row * blocks + block, column - block * STEP, jnp.zeros((10, slots), jnp.float32)], axis=0
        )
        out[group:, :] = tail.astype(jnp.bfloat16)


def pack_obs(place, counts, values, weights, cells, width):
    group, slabs, slots = values.shape
    return pl.pallas_call(
        functools.partial(pack_obs_kernel, width),
        out_shape=[jax.ShapeDtypeStruct((group + 16, slots), jnp.bfloat16)] * slabs,
        in_specs=[SMEM, SMEM, VMEM, VMEM, VMEM],
        out_specs=[VMEM] * slabs,
        scratch_shapes=[pltpu.VMEM((slots // LANES, group * slabs, LANES), jnp.float32)],
        compiler_params=PARAMS,
        name="pack_obs",
    )(place, counts, values.reshape(group * slabs, slots), weights, cells)


def unpack_obs_kernel(place_ref, *refs):
    pieces, out_ref, tiles_ref = refs[:-2], refs[-2], refs[-1]
    slabs = len(pieces)
    group = out_ref.shape[0] // slabs
    for k, piece in enumerate(pieces):
        slab = place_ref[0] ^ k
        for tile in range(tiles_ref.shape[0]):
            part = piece[:, tile * LANES:(tile + 1) * LANES].astype(jnp.float32)
            tiles_ref[tile, pl.ds(slab, group, stride=slabs), :] = part
    for tile in range(tiles_ref.shape[0]):
        out_ref[:, tile * LANES:(tile + 1) * LANES] = tiles_ref[tile]


def unpack_obs(place, pieces):
    group, slots = pieces[0].shape
    slabs = len(pieces)
    return pl.pallas_call(
        unpack_obs_kernel,
        out_shape=jax.ShapeDtypeStruct((group * slabs, slots), jnp.float32),
        in_specs=[SMEM] + [VMEM] * slabs,
        out_specs=VMEM,
        scratch_shapes=[pltpu.VMEM((slots // LANES, group * slabs, LANES), jnp.float32)],
        compiler_params=PARAMS,
        name="unpack_obs",
    )(place, *pieces)


def gelu_value(value):
    return 0.5 * value * (1.0 + lax.erf(value * 0.7071067811865476))


def gelu_slope(value):
    return (
        0.5 * (1.0 + lax.erf(value * 0.7071067811865476))
        + value * jnp.exp(-0.5 * value * value) * 0.3989422804014327
    )


def observe_kernel(parts, rounds, slabs, width, place_ref, bias_ref, *refs):
    rows = parts * rounds
    mixed, obs = refs[:rows], refs[rows:rows + slabs]
    grads = refs[rows + slabs:2 * rows + slabs]
    departures = refs[2 * rows + slabs:2 * rows + 2 * slabs]
    pre_ref, table_ref, found_ref, row_ref = refs[2 * rows + 2 * slabs:]
    group, wide = mixed[0].shape
    slots = obs[0].shape[1]
    blocks = -(-width // STEP)
    tiles = wide // LANES
    place = place_ref[0]
    rem = width % LANES
    last = width // LANES
    lane = lane_iota((group, LANES))
    bias = bias_ref[...]

    for turn in range(rounds):
        for k in range(parts):
            row = turn * parts + (place ^ k)
            pre_ref[row] = mixed[turn * parts + k][...].astype(jnp.float32) + bias

    @pl.loop(0, rows)
    def _(row):
        row_ref[...] = gelu_value(pre_ref[row])
        for j in range(blocks):
            tile, shift = divmod(j * STEP, LANES)
            block = row_ref[:, tile * LANES:(tile + 1) * LANES]
            if shift:
                after = row_ref[:, (tile + 1) * LANES:(tile + 2) * LANES]
                block = jnp.where(
                    lane < LANES - shift,
                    pltpu.roll(block, LANES - shift, 1),
                    pltpu.roll(after, LANES - shift, 1),
                )
            block = block.astype(jnp.bfloat16)

            @pl.when(row < rows - 1)
            def _():
                at = pl.multiple_of((row * blocks + j) * group, group)
                table_ref[pl.ds(at, group), :LANES] = block

            @pl.when(row > 0)
            def _():
                at = pl.multiple_of(((row - 1) * blocks + j) * group, group)
                table_ref[pl.ds(at, group), LANES:] = block

    found_ref[...] = jnp.zeros_like(found_ref)
    steps = (rows - 1) * blocks // TOGETHER
    high = TOGETHER * group
    lo_iota = lax.broadcasted_iota(jnp.int32, (LANES, OBS), 0)
    for s in range(slabs):
        @pl.loop(0, slots // OBS)
        def _(sub):
            at = pl.ds(pl.multiple_of(sub * OBS, OBS), OBS)
            side = obs[s][group:, at].astype(jnp.float32)
            which = side[4:5].astype(jnp.int32)
            low = side[5:6].astype(jnp.int32)
            first, second = lo_iota == low, lo_iota == low + 1
            spread = jnp.concatenate(
                [
                    jnp.where(first, side[0:1], jnp.where(second, side[1:2], 0.0)),
                    jnp.where(first, side[2:3], jnp.where(second, side[3:4], 0.0)),
                ],
                axis=0,
            ).astype(jnp.bfloat16)
            whole = jnp.broadcast_to(which, (group, OBS))

            def gather(step, model):
                start = pl.multiple_of(step * high, high)
                part = jnp.dot(table_ref[pl.ds(start, high), :], spread, preferred_element_type=jnp.float32)
                for i in range(TOGETHER):
                    model = jnp.where(whole == step * TOGETHER + i, part[i * group:(i + 1) * group], model)
                return model

            model = lax.fori_loop(0, steps, gather, jnp.zeros((group, OBS), jnp.float32))
            departure = model - obs[s][:group, at].astype(jnp.float32)
            departures[s][:, at] = departure.astype(jnp.bfloat16)

            @pl.loop(0, steps)
            def _(step):
                start = pl.multiple_of(step * high, high)
                chosen = jnp.concatenate(
                    [jnp.where(whole == step * TOGETHER + i, departure, 0.0) for i in range(TOGETHER)], axis=0
                ).astype(jnp.bfloat16)
                found_ref[pl.ds(start, high), :] += lax.dot_general(
                    chosen, spread, (((1,), (1,)), ((), ())), preferred_element_type=jnp.float32
                )

    for turn in range(rounds):
        for k in range(parts):
            row = turn * parts + (place ^ k)
            out = grads[turn * parts + k]
            sums = [jnp.zeros((group, LANES), jnp.float32) for _ in range(tiles)]
            upper = pl.multiple_of(jnp.minimum(row, rows - 2) * (blocks * group), group)
            lower = pl.multiple_of(jnp.maximum(row - 1, 0) * (blocks * group), group)
            has_upper = row < rows - 1
            has_lower = row > 0
            for j in range(blocks):
                tile, shift = divmod(j * STEP, LANES)
                top = found_ref[pl.ds(upper + j * group, group), :LANES]
                low = found_ref[pl.ds(lower + j * group, group), LANES:]
                block = jnp.where(has_upper, top, 0.0) + jnp.where(has_lower, low, 0.0)
                if shift:
                    block = pltpu.roll(block, shift, 1)
                    sums[tile] += jnp.where(lane >= shift, block, 0.0)
                    sums[tile + 1] += jnp.where(lane < shift, block, 0.0)
                else:
                    sums[tile] += block
            sums[0] += jnp.where(lane == 0, pltpu.roll(sums[last], LANES - rem, 1), 0.0)
            for tile in range(tiles):
                at = slice(tile * LANES, (tile + 1) * LANES)
                sums[tile] *= gelu_slope(pre_ref[row, :, at])
                if tile < last:
                    out[:, at] = sums[tile].astype(jnp.bfloat16)
            out[:, last * LANES:] = wrapped_tail(sums[0], sums[last], rem).astype(jnp.bfloat16)


def observe(place, bias, mixed, obs, parts, width):
    group, wide = mixed[0].shape
    rows, slabs = len(mixed), len(obs)
    slots = obs[0].shape[1]
    blocks = -(-width // STEP)
    found = (rows - 1) * blocks * group
    results = pl.pallas_call(
        functools.partial(observe_kernel, parts, rows // parts, slabs, width),
        out_shape=[jax.ShapeDtypeStruct((group, wide), jnp.bfloat16)] * rows
        + [jax.ShapeDtypeStruct((group, slots), jnp.bfloat16)] * slabs,
        in_specs=[SMEM] + [VMEM] * (1 + rows + slabs),
        out_specs=[VMEM] * (rows + slabs),
        scratch_shapes=[
            pltpu.VMEM((rows, group, wide), jnp.float32),
            pltpu.VMEM((found, 2 * LANES), jnp.bfloat16),
            pltpu.VMEM((found, 2 * LANES), jnp.float32),
            pltpu.VMEM((group, wide), jnp.float32),
        ],
        compiler_params=PARAMS,
        name="observe",
    )(place, bias, *mixed, *obs)
    return results[:rows], results[rows:]


def swap(piece, axis, k):
    if k == 0:
        return piece
    return lax.ppermute(piece, axis, [(i, i ^ k) for i in range(lax.axis_size(axis))])


def mix(place, weights, pieces, parts):
    count = lax.axis_size("lat")
    forward = [(i, i + 1) for i in range(count - 1)]
    backward = [(i + 1, i) for i in range(count - 1)]
    results = []
    for turn in range(len(pieces) // parts):
        own = pieces[turn * parts:(turn + 1) * parts]
        here = assemble(place, [swap(own[k], "chan", k) for k in range(parts)])
        below = lax.ppermute(here, "lat", forward)
        above = lax.ppermute(here, "lat", backward)
        mixed = conv(place, weights, below, here, above, parts)
        results += [swap(mixed[k], "chan", k) for k in range(parts)]
    return results


def shards(state, kernel, bias, innovations, interp, cells, counts):
    group, rows, width = state.shape
    parts, slabs = lax.axis_size("chan"), lax.axis_size("lat")
    wide = padded_width(width)
    total = kernel.shape[2]
    chan_place = lax.axis_index("chan").reshape(1)
    lat_place = lax.axis_index("lat").reshape(1)
    forward_weights = kernel.reshape(3, 3 * total, total)
    backward_weights = jnp.transpose(kernel[::-1, ::-1], (0, 1, 3, 2)).reshape(3, 3 * total, total)

    mixed = mix(chan_place, forward_weights, split_rows(chan_place, state, parts, wide), parts)

    interp_rows = jnp.transpose(interp[:, 0], (1, 0, 2)).astype(jnp.float32)
    packed = pack_obs(
        lat_place, counts, innovations[:, 0], interp_rows, cells[0][:, None, :], width
    )
    obs = [swap(packed[k], "lat", k) for k in range(slabs)]

    grads, departures = observe(chan_place, bias[:, None], mixed, obs, parts, width)
    returned = [swap(departures[k], "lat", k) for k in range(slabs)]
    departures_out = unpack_obs(lat_place, returned).reshape(innovations.shape)
    grad_state = join_rows(chan_place, mix(chan_place, backward_weights, grads, parts), parts, width)
    return grad_state, departures_out


def solution(mesh):
    return jax.shard_map(
        shards,
        mesh=mesh,
        in_specs=(
            P("chan", "lat", None),
            P(),
            P("chan"),
            P("chan", "lat", None, None),
            P(None, "lat", None, None),
            P("lat", None, None),
            P("lat", None),
        ),
        out_specs=(P("chan", "lat", None), P("chan", "lat", None, None)),
        check_vma=False,
    )
```

time: 904 us -> 553 us (0.61)
  Pallas kernels: 0 us -> 343 us
  local copies, waits for them, and re-layouts: 333 us -> 10.7 us
  other arithmetic: 217 us -> 0 us
  waiting for transfers between devices: 181 us -> 78.9 us
  starting transfers between devices: 50.1 us -> 116 us
  matrix products: 49.2 us -> 0 us
  blocking collectives: 49 us -> 0 us
  between operations: 14.8 us -> 1.11 us
    pallas_call x0 -> x13, Pallas kernels: none -> 343 us  [the longest x1 295 us: observe(): pl.pallas_call(functools.partial(observe_kernel, parts, rows // parts, sl...]
    scatter-add x4 -> x0, other arithmetic: 183 us -> none  [shards(): grad_hidden.at[:, corners[which].reshape(-1)]]
    reduce_scatter x2 -> x0, waiting for transfers between devices: 178 us -> none  [channel_mix(): lax.psum_scatter(jnp.dot(local_weights, stacked, preferred_element_type=j...]
    gather x8 -> x0, local copies, waits for them, and re-layouts: 142 us -> none  [shards(): jnp.take(flat_hidden, corners[which], axis=1)]
    ppermute x4 -> x46, starting transfers between devices: 9.34 us -> 116 us  [the longest x38 96.3 us: swap(): lax.ppermute(piece, axis, [(i, i ^ k) for i in range(lax.axis_size(axis))])]
    ppermute x4 -> x46, waiting for transfers between devices: 0.01 us -> 78.9 us  [the longest x38 78.9 us: swap(): lax.ppermute(piece, axis, [(i, i ^ k) for i in range(lax.axis_size(axis))])]
    reshape x8 -> x0, local copies, waits for them, and re-layouts: 76.8 us -> none  [the longest x2 53.8 us: tap_stack(): stacked.reshape(9 * padded_field.shape[0], row_count * padded_field.shape...]
    dot_general x2 -> x0, local copies, waits for them, and re-layouts: 55.9 us -> none  [channel_mix(): jnp.dot(local_weights, stacked, preferred_element_type=jnp.float32)]
  transfers between devices with their start and end apart: 9 -> 46, of which waited for: 4 -> 13; matrix products, arithmetic and copies ran while one was open for 21% -> 1% of each run, Pallas kernels for 0% -> 8%
where the time goes in v1:
time: 553 us; the launch traced here: 550 us
  Pallas kernels  343 us (62%)
  starting transfers between devices  116 us (21%)
  waiting for transfers between devices  78.9 us (14%)
  local copies, waits for them, and re-layouts  10.7 us (2%)
    pallas_call x1, Pallas kernels, observe(): pl.pallas_call(functools.partial(observe_kernel, parts, rows // parts, sl...  295 us
    ppermute x38, starting transfers between devices, swap(): lax.ppermute(piece, axis, [(i, i ^ k) for i in range(lax.axis_size(axis))])  96.3 us
    ppermute x38, waiting for transfers between devices, swap(): lax.ppermute(piece, axis, [(i, i ^ k) for i in range(lax.axis_size(axis))])  78.9 us
    pallas_call x4, Pallas kernels, conv(): pl.pallas_call(conv_kernel, out_shape=[jax.ShapeDtypeStruct((group, wide)...  26 us
    ppermute x4, starting transfers between devices, mix(): below = lax.ppermute(here, 'lat', forward)  14.4 us
  transfers between devices with their start and end apart: 46, of which 13 were waited for; matrix products, arithmetic and copies ran while one was open for 1% of the time, Pallas kernels for 8%

profile of v1, /device:TPU:0, one launch (start us, length us, event | category | flops | bytes accessed | tf_op | source)
XLA Modules:
  0.0 550.1 jit_solution(4315623258966220979)
XLA Ops:
  0.6 3.2 split_rows.1
  3.8 3.0 collective-permute-start.8
  6.8 2.6 collective-permute-start.9
  9.4 0.9 collective-permute-start
  10.3 3.5 collective-permute-start.1
  13.8 2.4 collective-permute-done.8.refs_1_
  16.2 4.6 collective-permute-start.2
  20.8 3.4 collective-permute-done.9.refs_2_
  25.0 2.1 assemble.5.here_ref
  27.1 1.4 collective-permute-start.12
  28.5 3.9 collective-permute-start.11
  32.5 8.6 %collective-permute-done.1.refs_2_ = bf16[64,1536]{1,0:T(8,128)(2,1)S(1)} collective-permute-done((bf16[64,1536]{1,0:T(8,128)(2,1)}, bf16[64,1536]{1,0:T(8,128)(2,1)S(1)}, u32[]{:S(2)}, u32[]{:S(2)}) %collective-permute-start.1) | collective-permute-done | bytes 196640 | tf_op jit(solution)/shard_map/ppermute | solution.py:385
  41.8 2.1 assemble.4.here_ref
  44.0 1.3 collective-permute-start.4
  45.3 3.3 collective-permute-start.3
  49.9 3.3 pack_obs.1
  53.2 1.1 collective-permute-start.16
  54.2 0.9 copy-done.45
  55.1 1.5 collective-permute-start.17
  56.7 6.5 %conv.5 = (bf16[64,1536]{1,0:T(8,128)(2,1)}, bf16[64,1536]{1,0:T(8,128)(2,1)}, bf16[64,1536]{1,0:T(8,128)(2,1)}, bf16[64,1536]{1,0:T(8,128)(2,1)}) custom-call(s32[1]{0:T(128)} %bitcast.place_ref, bf16[3,768,256]{2,1,0:T(8,128)(2,1)} %bitcast.21, bf16[256,1536]{1,0:T(8,128)(2,1)} %collective-permute-done.11.below_ref, bf16[256,1536]{1,0:T(8,128)(2,1)} %assemble.5.here_ref, ...), custom_call_target="tpu_custom_call" | custom-call | flops 1811939328 | bytes 4325376 | tf_op jit(solution)/shard_map/conv/pallas_call | solution.py:150
  63.2 8.0 %collective-permute-start.13 = (bf16[64,1536]{1,0:T(8,128)(2,1)}, bf16[64,1536]{1,0:T(8,128)(2,1)S(1)}, u32[]{:S(2)}, u32[]{:S(2)}) collective-permute-start(bf16[64,1536]{1,0:T(8,128)(2,1)} %get-tuple-element.63), channel_id=1, source_target_pairs={{0,1},{1,0},{2,3},{3,2},{4,5},{5,4},{6,7},{7,6},{8,9},{9,8},{10,11... | collective-permute-start | bytes 589832 | tf_op jit(solution)/shard_map/ppermute | solution.py:385
  71.2 2.3 collective-permute-start.19
  73.7 2.6 collective-permute-start.21
  77.2 6.4 %conv.4 = (bf16[64,1536]{1,0:T(8,128)(2,1)}, bf16[64,1536]{1,0:T(8,128)(2,1)}, bf16[64,1536]{1,0:T(8,128)(2,1)}, bf16[64,1536]{1,0:T(8,128)(2,1)}) custom-call(s32[1]{0:T(128)} %bitcast.place_ref, bf16[3,768,256]{2,1,0:T(8,128)(2,1)} %bitcast.22, bf16[256,1536]{1,0:T(8,128)(2,1)} %copy-done.43, bf16[256,1536]{1,0:T(8,128)(2,1)} %assemble.4.here_ref, ...), custom_call_target="tpu_custom_call" | custom-call | flops 1811939328 | bytes 4325376 | tf_op jit(solution)/shard_map/conv/pallas_call | solution.py:150
  83.6 2.0 collective-permute-done.19.refs_12_
  85.6 10.7 %collective-permute-start.14 = (bf16[64,1536]{1,0:T(8,128)(2,1)S(1)}, bf16[64,1536]{1,0:T(8,128)(2,1)S(1)}, u32[]{:S(2)}, u32[]{:S(2)}) collective-permute-start(bf16[64,1536]{1,0:T(8,128)(2,1)S(1)} %copy-done.51), channel_id=1, source_target_pairs={{0,2},{1,3},{2,0},{3,1},{4,6},{5,7},{6,4},{7,5},{8,10},{9,11},{10,... | collective-permute-start | bytes 589832 | tf_op jit(solution)/shard_map/ppermute | solution.py:385
  96.3 1.4 collective-permute-start.15
  97.7 3.4 collective-permute-start.5
  101.1 2.4 collective-permute-start.7
  104.2 5.4 collective-permute-done.14.refs_6_
  109.6 3.2 collective-permute-done.5.refs_1_
  112.8 13.6 %collective-permute-done.6.refs_2_ = bf16[64,1536]{1,0:T(8,128)(2,1)S(1)} collective-permute-done((bf16[64,1536]{1,0:T(8,128)(2,1)}, bf16[64,1536]{1,0:T(8,128)(2,1)S(1)}, u32[]{:S(2)}, u32[]{:S(2)}) %collective-permute-start.6) | collective-permute-done | bytes 196640 | tf_op jit(solution)/shard_map/ppermute | solution.py:385
  127.1 295.1 %observe.1 = (bf16[64,1536]{1,0:T(8,128)(2,1)}, bf16[64,1536]{1,0:T(8,128)(2,1)}, bf16[64,1536]{1,0:T(8,128)(2,1)}, bf16[64,1536]{1,0:T(8,128)(2,1)}, bf16[64,15...) custom-call(s32[1]{0:T(128)} %bitcast.place_ref, ...), custom_call_target="tpu_custom_call" | custom-call | tf_op jit(solution)/shard_map/observe/pallas_call | solution.py:364
  422.3 4.8 collective-permute-start.31
  427.1 2.4 collective-permute-start.33
  429.5 1.0 collective-permute-start.23
  430.6 0.9 collective-permute-start.24
  431.5 4.5 collective-permute-done.31.refs_1_
  435.9 2.3 collective-permute-start.25
  438.2 6.2 %collective-permute-done.32.refs_2_ = bf16[64,1536]{1,0:T(8,128)(2,1)S(1)} collective-permute-done((bf16[64,1536]{1,0:T(8,128)(2,1)}, bf16[64,1536]{1,0:T(8,128)(2,1)S(1)}, u32[]{:S(2)}, u32[]{:S(2)}) %collective-permute-start.32) | collective-permute-done | bytes 196640 | tf_op jit(solution)/shard_map/ppermute | solution.py:385
  445.1 2.2 assemble.7.here_ref
  447.3 1.4 collective-permute-start.35
  448.7 3.9 collective-permute-start.34
  452.7 8.6 %collective-permute-done.24.refs_2_ = bf16[64,1536]{1,0:T(8,128)(2,1)S(1)} collective-permute-done((bf16[64,1536]{1,0:T(8,128)(2,1)}, bf16[64,1536]{1,0:T(8,128)(2,1)S(1)}, u32[]{:S(2)}, u32[]{:S(2)}) %collective-permute-start.24) | collective-permute-done | bytes 196640 | tf_op jit(solution)/shard_map/ppermute | solution.py:385
  462.0 2.1 assemble.6.here_ref
  464.2 1.3 collective-permute-start.27
  465.4 3.3 collective-permute-start.26
  468.9 1.5 copy.9
  470.4 1.1 collective-permute-start.39
  471.5 1.5 collective-permute-start.40
  473.1 6.5 %conv.7 = (bf16[64,1536]{1,0:T(8,128)(2,1)}, bf16[64,1536]{1,0:T(8,128)(2,1)}, bf16[64,1536]{1,0:T(8,128)(2,1)}, bf16[64,1536]{1,0:T(8,128)(2,1)}) custom-call(s32[1]{0:T(128)} %bitcast.place_ref, bf16[3,768,256]{2,1,0:T(8,128)(2,1)} %bitcast.23, bf16[256,1536]{1,0:T(8,128)(2,1)} %collective-permute-done.34.below_ref, bf16[256,1536]{1,0:T(8,128)(2,1)} %assemble.7.here_ref, ...), custom_call_target="tpu_custom_call" | custom-call | flops 1811939328 | bytes 4325376 | tf_op jit(solution)/shard_map/conv/pallas_call | solution.py:150
  479.7 11.9 %collective-permute-start.36 = (bf16[64,1536]{1,0:T(8,128)(2,1)}, bf16[64,1536]{1,0:T(8,128)(2,1)S(1)}, u32[]{:S(2)}, u32[]{:S(2)}) collective-permute-start(bf16[64,1536]{1,0:T(8,128)(2,1)} %get-tuple-element.87), channel_id=1, source_target_pairs={{0,1},{1,0},{2,3},{3,2},{4,5},{5,4},{6,7},{7,6},{8,9},{9,8},{10,11... | collective-permute-start | bytes 589832 | tf_op jit(solution)/shard_map/ppermute | solution.py:385
  491.6 2.3 collective-permute-start.42
  494.0 2.7 collective-permute-start.44
  497.5 6.5 %conv.6 = (bf16[64,1536]{1,0:T(8,128)(2,1)}, bf16[64,1536]{1,0:T(8,128)(2,1)}, bf16[64,1536]{1,0:T(8,128)(2,1)}, bf16[64,1536]{1,0:T(8,128)(2,1)}) custom-call(s32[1]{0:T(128)} %bitcast.place_ref, bf16[3,768,256]{2,1,0:T(8,128)(2,1)} %bitcast.24, bf16[256,1536]{1,0:T(8,128)(2,1)} %copy-done.46, bf16[256,1536]{1,0:T(8,128)(2,1)} %assemble.6.here_ref, ...), custom_call_target="tpu_custom_call" | custom-call | flops 1811939328 | bytes 4325376 | tf_op jit(solution)/shard_map/conv/pallas_call | solution.py:150
  504.1 10.6 %collective-permute-start.37 = (bf16[64,1536]{1,0:T(8,128)(2,1)S(1)}, bf16[64,1536]{1,0:T(8,128)(2,1)S(1)}, u32[]{:S(2)}, u32[]{:S(2)}) collective-permute-start(bf16[64,1536]{1,0:T(8,128)(2,1)S(1)} %copy-done.49), channel_id=1, source_target_pairs={{0,2},{1,3},{2,0},{3,1},{4,6},{5,7},{6,4},{7,5},{8,10},{9,11},{10,... | collective-permute-start | bytes 589832 | tf_op jit(solution)/shard_map/ppermute | solution.py:385
  514.7 2.0 collective-permute-start.38
  517.3 1.9 collective-permute-start.29
  519.1 2.0 collective-permute-start.30
  521.1 3.4 unpack_obs.1
  524.5 4.3 collective-permute-done.37.refs_6_
  528.8 1.7 collective-permute-done.28.refs_1_
  530.5 15.1 %collective-permute-done.29.refs_2_ = bf16[64,1536]{1,0:T(8,128)(2,1)S(1)} collective-permute-done((bf16[64,1536]{1,0:T(8,128)(2,1)}, bf16[64,1536]{1,0:T(8,128)(2,1)S(1)}, u32[]{:S(2)}, u32[]{:S(2)}) %collective-permute-start.29) | collective-permute-done | bytes 196640 | tf_op jit(solution)/shard_map/ppermute | solution.py:385
  546.4 3.7 join_rows.1
  (166 shorter events, 9.2 us)
Async XLA Ops:
  3.8 12.4 %collective-permute-start.8 = (bf16[64,1536]{1,0:T(8,128)(2,1)}, bf16[64,1536]{1,0:T(8,128)(2,1)S(1)}, u32[]{:S(2)}, u32[]{:S(2)}) collective-permute-start(bf16[64,1536]{1,0:T(8,128)(2,1)} %get-tuple-element.59), channel_id=1, source_target_pairs={{0,1},{1,0},{2,3},{3,2},{4,5},{5,4},{6,7},{7,6},{8,9},{9,8},{10,11... | collective-permute-start | bytes 589832 | tf_op jit(solution)/shard_map/ppermute | solution.py:385
  6.8 17.4 %collective-permute-start.9 = (bf16[64,1536]{1,0:T(8,128)(2,1)}, bf16[64,1536]{1,0:T(8,128)(2,1)S(1)}, u32[]{:S(2)}, u32[]{:S(2)}) collective-permute-start(bf16[64,1536]{1,0:T(8,128)(2,1)} %get-tuple-element.60), channel_id=1, source_target_pairs={{0,2},{1,3},{2,0},{3,1},{4,6},{5,7},{6,4},{7,5},{8,10},{9,11},{10,... | collective-permute-start | bytes 589832 | tf_op jit(solution)/shard_map/ppermute | solution.py:385
  9.4 14.8 %collective-permute-start.10 = (bf16[64,1536]{1,0:T(8,128)(2,1)}, bf16[64,1536]{1,0:T(8,128)(2,1)S(1)}, u32[]{:S(2)}, u32[]{:S(2)}) collective-permute-start(bf16[64,1536]{1,0:T(8,128)(2,1)} %get-tuple-element.61), channel_id=1, source_target_pairs={{0,3},{1,2},{2,1},{3,0},{4,7},{5,6},{6,5},{7,4},{8,11},{9,10},{10,... | collective-permute-start | bytes 589832 | tf_op jit(solution)/shard_map/ppermute | solution.py:385
  9.4 23.1 %collective-permute-start = (bf16[64,1536]{1,0:T(8,128)(2,1)}, bf16[64,1536]{1,0:T(8,128)(2,1)S(1)}, u32[]{:S(2)}, u32[]{:S(2)}) collective-permute-start(bf16[64,1536]{1,0:T(8,128)(2,1)} %get-tuple-element.51), channel_id=1, source_target_pairs={{0,1},{1,0},{2,3},{3,2},{4,5},{5,4},{6,7},{7,6},{8,9},{9,8},{10,11... | collective-permute-start | bytes 589832 | tf_op jit(solution)/shard_map/ppermute | solution.py:385
  10.3 30.8 %collective-permute-start.1 = (bf16[64,1536]{1,0:T(8,128)(2,1)}, bf16[64,1536]{1,0:T(8,128)(2,1)S(1)}, u32[]{:S(2)}, u32[]{:S(2)}) collective-permute-start(bf16[64,1536]{1,0:T(8,128)(2,1)} %get-tuple-element.52), channel_id=1, source_target_pairs={{0,2},{1,3},{2,0},{3,1},{4,6},{5,7},{6,4},{7,5},{8,10},{9,11},{10,... | collective-permute-start | bytes 589832 | tf_op jit(solution)/shard_map/ppermute | solution.py:385
  16.2 24.9 %collective-permute-start.2 = (bf16[64,1536]{1,0:T(8,128)(2,1)}, bf16[64,1536]{1,0:T(8,128)(2,1)S(1)}, u32[]{:S(2)}, u32[]{:S(2)}) collective-permute-start(bf16[64,1536]{1,0:T(8,128)(2,1)} %get-tuple-element.53), channel_id=1, source_target_pairs={{0,3},{1,2},{2,1},{3,0},{4,7},{5,6},{6,5},{7,4},{8,11},{9,10},{10,... | collective-permute-start | bytes 589832 | tf_op jit(solution)/shard_map/ppermute | solution.py:385
  27.1 21.4 %copy-start.40 = (s32[1,8,1024]{2,1,0:T(8,128)S(1)}, s32[1,8,1024]{2,1,0:T(8,128)}, u32[]{:S(2)}) copy-start(s32[1,8,1024]{2,1,0:T(8,128)} %param.12) | copy-start | bytes 98308
  27.1 22.1 %copy-start.39 = (bf16[4,1,8,1024]{3,2,1,0:T(8,128)(2,1)S(1)}, bf16[4,1,8,1024]{3,2,1,0:T(8,128)(2,1)}, u32[]{:S(2)}) copy-start(bf16[4,1,8,1024]{3,2,1,0:T(8,128)(2,1)} %param.11) | copy-start | bytes 196612
  27.1 27.1 %collective-permute-start.12 = (bf16[256,1536]{1,0:T(8,128)(2,1)}, bf16[256,1536]{1,0:T(8,128)(2,1)S(1)}, u32[]{:S(2)}, u32[]{:S(2)}) collective-permute-start(bf16[256,1536]{1,0:T(8,128)(2,1)} %assemble.5.here_ref), channel_id=1, source_target_pairs={{4,0},{8,4},{12,8},{16,12},{20,16},{24,20},{28,24},{5,1},{9,5},{13... | collective-permute-start | bytes 2359304 | tf_op jit(solution)/shard_map/ppermute | solution.py:397
  28.5 28.1 %collective-permute-start.11 = (bf16[256,1536]{1,0:T(8,128)(2,1)}, bf16[256,1536]{1,0:T(8,128)(2,1)}, u32[]{:S(2)}, u32[]{:S(2)}) collective-permute-start(bf16[256,1536]{1,0:T(8,128)(2,1)} %assemble.5.here_ref), channel_id=1, source_target_pairs={{0,4},{4,8},{8,12},{12,16},{16,20},{20,24},{24,28},{1,5},{5,9},{9,... | collective-permute-start | bytes 2359304 | tf_op jit(solution)/shard_map/ppermute | solution.py:396
  44.0 29.7 %collective-permute-start.4 = (bf16[256,1536]{1,0:T(8,128)(2,1)}, bf16[256,1536]{1,0:T(8,128)(2,1)S(1)}, u32[]{:S(2)}, u32[]{:S(2)}) collective-permute-start(bf16[256,1536]{1,0:T(8,128)(2,1)} %assemble.4.here_ref), channel_id=1, source_target_pairs={{4,0},{8,4},{12,8},{16,12},{20,16},{24,20},{28,24},{5,1},{9,5},{13... | collective-permute-start | bytes 2359304 | tf_op jit(solution)/shard_map/ppermute | solution.py:397
  45.3 31.0 %collective-permute-start.3 = (bf16[256,1536]{1,0:T(8,128)(2,1)}, bf16[256,1536]{1,0:T(8,128)(2,1)S(1)}, u32[]{:S(2)}, u32[]{:S(2)}) collective-permute-start(bf16[256,1536]{1,0:T(8,128)(2,1)} %assemble.4.here_ref), channel_id=1, source_target_pairs={{0,4},{4,8},{8,12},{12,16},{16,20},{20,24},{24,28},{1,5},{5,9},{9,... | collective-permute-start | bytes 2359304 | tf_op jit(solution)/shard_map/ppermute | solution.py:396
  53.2 10.0 %collective-permute-start.16 = (bf16[80,1024]{1,0:T(8,128)(2,1)}, bf16[80,1024]{1,0:T(8,128)(2,1)S(1)}, u32[]{:S(2)}, u32[]{:S(2)}) collective-permute-start(bf16[80,1024]{1,0:T(8,128)(2,1)} %get-tuple-element.67), channel_id=1, source_target_pairs={{0,4},{4,0},{8,12},{12,8},{16,20},{20,16},{24,28},{28,24},{1,5},{5... | collective-permute-start | bytes 491528 | tf_op jit(solution)/shard_map/ppermute | solution.py:385
  55.1 16.1 %collective-permute-start.17 = (bf16[80,1024]{1,0:T(8,128)(2,1)}, bf16[80,1024]{1,0:T(8,128)(2,1)S(1)}, u32[]{:S(2)}, u32[]{:S(2)}) collective-permute-start(bf16[80,1024]{1,0:T(8,128)(2,1)} %get-tuple-element.68), channel_id=1, source_target_pairs={{0,8},{4,12},{8,0},{12,4},{16,24},{20,28},{24,16},{28,20},{1,9},{5... | collective-permute-start | bytes 491528 | tf_op jit(solution)/shard_map/ppermute | solution.py:385
  56.6 16.9 %collective-permute-start.18 = (bf16[80,1024]{1,0:T(8,128)(2,1)}, bf16[80,1024]{1,0:T(8,128)(2,1)S(1)}, u32[]{:S(2)}, u32[]{:S(2)}) collective-permute-start(bf16[80,1024]{1,0:T(8,128)(2,1)} %get-tuple-element.69), channel_id=1, source_target_pairs={{0,12},{4,8},{8,4},{12,0},{16,28},{20,24},{24,20},{28,16},{1,13},{... | collective-permute-start | bytes 491528 | tf_op jit(solution)/shard_map/ppermute | solution.py:385
  56.7 19.6 %copy-start.52 = (bf16[80,1024]{1,0:T(8,128)(2,1)S(1)}, bf16[80,1024]{1,0:T(8,128)(2,1)}, u32[]{:S(2)}) copy-start(bf16[80,1024]{1,0:T(8,128)(2,1)} %get-tuple-element.73) | copy-start | bytes 491524
  63.2 20.4 %copy-start.25 = (bf16[80,1024]{1,0:T(8,128)(2,1)}, bf16[80,1024]{1,0:T(8,128)(2,1)S(1)}, u32[]{:S(2)}) copy-start(bf16[80,1024]{1,0:T(8,128)(2,1)S(1)} %collective-permute-done.16.refs_9_) | copy-start | bytes 491524
  63.2 37.9 %collective-permute-start.13 = (bf16[64,1536]{1,0:T(8,128)(2,1)}, bf16[64,1536]{1,0:T(8,128)(2,1)S(1)}, u32[]{:S(2)}, u32[]{:S(2)}) collective-permute-start(bf16[64,1536]{1,0:T(8,128)(2,1)} %get-tuple-element.63), channel_id=1, source_target_pairs={{0,1},{1,0},{2,3},{3,2},{4,5},{5,4},{6,7},{7,6},{8,9},{9,8},{10,11... | collective-permute-start | bytes 589832 | tf_op jit(solution)/shard_map/ppermute | solution.py:385
  71.2 14.3 %collective-permute-start.19 = (bf16[80,1024]{1,0:T(8,128)(2,1)S(1)}, bf16[80,1024]{1,0:T(8,128)(2,1)S(1)}, u32[]{:S(2)}, u32[]{:S(2)}) collective-permute-start(bf16[80,1024]{1,0:T(8,128)(2,1)S(1)} %copy-done.55), channel_id=1, source_target_pairs={{0,16},{4,20},{8,24},{12,28},{16,0},{20,4},{24,8},{28,12},{1,17},{... | collective-permute-start | bytes 491528 | tf_op jit(solution)/shard_map/ppermute | solution.py:385
  73.5 22.8 %collective-permute-start.20 = (bf16[80,1024]{1,0:T(8,128)(2,1)S(1)}, bf16[80,1024]{1,0:T(8,128)(2,1)S(1)}, u32[]{:S(2)}, u32[]{:S(2)}) collective-permute-start(bf16[80,1024]{1,0:T(8,128)(2,1)S(1)} %copy-done.54), channel_id=1, source_target_pairs={{0,20},{4,16},{8,28},{12,24},{16,4},{20,0},{24,12},{28,8},{1,21},{... | collective-permute-start | bytes 491528 | tf_op jit(solution)/shard_map/ppermute | solution.py:385
  73.7 24.0 %collective-permute-start.21 = (bf16[80,1024]{1,0:T(8,128)(2,1)S(1)}, bf16[80,1024]{1,0:T(8,128)(2,1)S(1)}, u32[]{:S(2)}, u32[]{:S(2)}) collective-permute-start(bf16[80,1024]{1,0:T(8,128)(2,1)S(1)} %copy-done.53), channel_id=1, source_target_pairs={{0,24},{4,28},{8,16},{12,20},{16,8},{20,12},{24,0},{28,4},{1,25},{... | collective-permute-start | bytes 491528 | tf_op jit(solution)/shard_map/ppermute | solution.py:385
  76.3 20.0 %copy-start.50 = (bf16[64,1536]{1,0:T(8,128)(2,1)S(1)}, bf16[64,1536]{1,0:T(8,128)(2,1)}, u32[]{:S(2)}) copy-start(bf16[64,1536]{1,0:T(8,128)(2,1)} %get-tuple-element.65) | copy-start | bytes 589828
  76.3 27.2 %copy-start.41 = (f32[64]{0:T(128)S(1)}, f32[64]{0:T(128)}, u32[]{:S(2)}) copy-start(f32[64]{0:T(128)} %param.9) | copy-start | bytes 772
  76.3 24.8 %collective-permute-start.22 = (bf16[80,1024]{1,0:T(8,128)(2,1)S(1)}, bf16[80,1024]{1,0:T(8,128)(2,1)S(1)}, u32[]{:S(2)}, u32[]{:S(2)}) collective-permute-start(bf16[80,1024]{1,0:T(8,128)(2,1)S(1)} %copy-done.52), channel_id=1, source_target_pairs={{0,28},{4,24},{8,20},{12,16},{16,12},{20,8},{24,4},{28,0},{1,29},{... | collective-permute-start | bytes 491528 | tf_op jit(solution)/shard_map/ppermute | solution.py:385
  85.6 40.8 %copy-start.28 = (bf16[80,1024]{1,0:T(8,128)(2,1)}, bf16[80,1024]{1,0:T(8,128)(2,1)S(1)}, u32[]{:S(2)}) copy-start(bf16[80,1024]{1,0:T(8,128)(2,1)S(1)} %collective-permute-done.19.refs_12_) | copy-start | bytes 491524
  85.6 24.0 %collective-permute-start.14 = (bf16[64,1536]{1,0:T(8,128)(2,1)S(1)}, bf16[64,1536]{1,0:T(8,128)(2,1)S(1)}, u32[]{:S(2)}, u32[]{:S(2)}) collective-permute-start(bf16[64,1536]{1,0:T(8,128)(2,1)S(1)} %copy-done.51), channel_id=1, source_target_pairs={{0,2},{1,3},{2,0},{3,1},{4,6},{5,7},{6,4},{7,5},{8,10},{9,11},{10,... | collective-permute-start | bytes 589832 | tf_op jit(solution)/shard_map/ppermute | solution.py:385
  96.3 30.1 %copy-start.29 = (bf16[80,1024]{1,0:T(8,128)(2,1)}, bf16[80,1024]{1,0:T(8,128)(2,1)S(1)}, u32[]{:S(2)}) copy-start(bf16[80,1024]{1,0:T(8,128)(2,1)S(1)} %collective-permute-done.20.refs_13_) | copy-start | bytes 491524
  96.3 13.3 %collective-permute-start.15 = (bf16[64,1536]{1,0:T(8,128)(2,1)S(1)}, bf16[64,1536]{1,0:T(8,128)(2,1)S(1)}, u32[]{:S(2)}, u32[]{:S(2)}) collective-permute-start(bf16[64,1536]{1,0:T(8,128)(2,1)S(1)} %copy-done.50), channel_id=1, source_target_pairs={{0,3},{1,2},{2,1},{3,0},{4,7},{5,6},{6,5},{7,4},{8,11},{9,10},{10,... | collective-permute-start | bytes 589832 | tf_op jit(solution)/shard_map/ppermute | solution.py:385
  97.7 28.7 %copy-start.30 = (bf16[80,1024]{1,0:T(8,128)(2,1)}, bf16[80,1024]{1,0:T(8,128)(2,1)S(1)}, u32[]{:S(2)}) copy-start(bf16[80,1024]{1,0:T(8,128)(2,1)S(1)} %collective-permute-done.21.refs_14_) | copy-start | bytes 491524
  97.7 15.1 %collective-permute-start.5 = (bf16[64,1536]{1,0:T(8,128)(2,1)}, bf16[64,1536]{1,0:T(8,128)(2,1)S(1)}, u32[]{:S(2)}, u32[]{:S(2)}) collective-permute-start(bf16[64,1536]{1,0:T(8,128)(2,1)} %get-tuple-element.55), channel_id=1, source_target_pairs={{0,1},{1,0},{2,3},{3,2},{4,5},{5,4},{6,7},{7,6},{8,9},{9,8},{10,11... | collective-permute-start | bytes 589832 | tf_op jit(solution)/shard_map/ppermute | solution.py:385
  101.1 25.4 %copy-start.31 = (bf16[80,1024]{1,0:T(8,128)(2,1)}, bf16[80,1024]{1,0:T(8,128)(2,1)S(1)}, u32[]{:S(2)}) copy-start(bf16[80,1024]{1,0:T(8,128)(2,1)S(1)} %collective-permute-done.22.refs_15_) | copy-start | bytes 491524
  101.1 25.3 %collective-permute-start.6 = (bf16[64,1536]{1,0:T(8,128)(2,1)}, bf16[64,1536]{1,0:T(8,128)(2,1)S(1)}, u32[]{:S(2)}, u32[]{:S(2)}) collective-permute-start(bf16[64,1536]{1,0:T(8,128)(2,1)} %get-tuple-element.56), channel_id=1, source_target_pairs={{0,2},{1,3},{2,0},{3,1},{4,6},{5,7},{6,4},{7,5},{8,10},{9,11},{10,... | collective-permute-start | bytes 589832 | tf_op jit(solution)/shard_map/ppermute | solution.py:385
  101.1 25.4 %copy-start.1 = (bf16[64,1536]{1,0:T(8,128)(2,1)}, bf16[64,1536]{1,0:T(8,128)(2,1)S(1)}, u32[]{:S(2)}) copy-start(bf16[64,1536]{1,0:T(8,128)(2,1)S(1)} %collective-permute-done.13.refs_5_) | copy-start | bytes 589828
  101.1 25.3 %collective-permute-start.7 = (bf16[64,1536]{1,0:T(8,128)(2,1)}, bf16[64,1536]{1,0:T(8,128)(2,1)S(1)}, u32[]{:S(2)}, u32[]{:S(2)}) collective-permute-start(bf16[64,1536]{1,0:T(8,128)(2,1)} %get-tuple-element.57), channel_id=1, source_target_pairs={{0,3},{1,2},{2,1},{3,0},{4,7},{5,6},{6,5},{7,4},{8,11},{9,10},{10,... | collective-permute-start | bytes 589832 | tf_op jit(solution)/shard_map/ppermute | solution.py:385
  422.3 13.7 %collective-permute-start.31 = (bf16[64,1536]{1,0:T(8,128)(2,1)}, bf16[64,1536]{1,0:T(8,128)(2,1)S(1)}, u32[]{:S(2)}, u32[]{:S(2)}) collective-permute-start(bf16[64,1536]{1,0:T(8,128)(2,1)} %get-tuple-element.83), channel_id=1, source_target_pairs={{0,1},{1,0},{2,3},{3,2},{4,5},{5,4},{6,7},{7,6},{8,9},{9,8},{10,11... | collective-permute-start | bytes 589832 | tf_op jit(solution)/shard_map/ppermute | solution.py:385
  427.1 17.3 %collective-permute-start.32 = (bf16[64,1536]{1,0:T(8,128)(2,1)}, bf16[64,1536]{1,0:T(8,128)(2,1)S(1)}, u32[]{:S(2)}, u32[]{:S(2)}) collective-permute-start(bf16[64,1536]{1,0:T(8,128)(2,1)} %get-tuple-element.84), channel_id=1, source_target_pairs={{0,2},{1,3},{2,0},{3,1},{4,6},{5,7},{6,4},{7,5},{8,10},{9,11},{10,... | collective-permute-start | bytes 589832 | tf_op jit(solution)/shard_map/ppermute | solution.py:385
  427.1 17.3 %collective-permute-start.33 = (bf16[64,1536]{1,0:T(8,128)(2,1)}, bf16[64,1536]{1,0:T(8,128)(2,1)S(1)}, u32[]{:S(2)}, u32[]{:S(2)}) collective-permute-start(bf16[64,1536]{1,0:T(8,128)(2,1)} %get-tuple-element.85), channel_id=1, source_target_pairs={{0,3},{1,2},{2,1},{3,0},{4,7},{5,6},{6,5},{7,4},{8,11},{9,10},{10,... | collective-permute-start | bytes 589832 | tf_op jit(solution)/shard_map/ppermute | solution.py:385
  429.5 23.1 %collective-permute-start.23 = (bf16[64,1536]{1,0:T(8,128)(2,1)}, bf16[64,1536]{1,0:T(8,128)(2,1)S(1)}, u32[]{:S(2)}, u32[]{:S(2)}) collective-permute-start(bf16[64,1536]{1,0:T(8,128)(2,1)} %get-tuple-element.75), channel_id=1, source_target_pairs={{0,1},{1,0},{2,3},{3,2},{4,5},{5,4},{6,7},{7,6},{8,9},{9,8},{10,11... | collective-permute-start | bytes 589832 | tf_op jit(solution)/shard_map/ppermute | solution.py:385
  430.6 30.7 %collective-permute-start.24 = (bf16[64,1536]{1,0:T(8,128)(2,1)}, bf16[64,1536]{1,0:T(8,128)(2,1)S(1)}, u32[]{:S(2)}, u32[]{:S(2)}) collective-permute-start(bf16[64,1536]{1,0:T(8,128)(2,1)} %get-tuple-element.76), channel_id=1, source_target_pairs={{0,2},{1,3},{2,0},{3,1},{4,6},{5,7},{6,4},{7,5},{8,10},{9,11},{10,... | collective-permute-start | bytes 589832 | tf_op jit(solution)/shard_map/ppermute | solution.py:385
  435.9 25.3 %collective-permute-start.25 = (bf16[64,1536]{1,0:T(8,128)(2,1)}, bf16[64,1536]{1,0:T(8,128)(2,1)S(1)}, u32[]{:S(2)}, u32[]{:S(2)}) collective-permute-start(bf16[64,1536]{1,0:T(8,128)(2,1)} %get-tuple-element.77), channel_id=1, source_target_pairs={{0,3},{1,2},{2,1},{3,0},{4,7},{5,6},{6,5},{7,4},{8,11},{9,10},{10,... | collective-permute-start | bytes 589832 | tf_op jit(solution)/shard_map/ppermute | solution.py:385
  447.3 21.4 %copy-start = (bf16[3,3,256,256]{3,2,1,0:T(8,128)(2,1)S(1)}, bf16[3,3,256,256]{3,2,1,0:T(8,128)(2,1)}, u32[]{:S(2)}) copy-start(bf16[3,3,256,256]{3,2,1,0:T(8,128)(2,1)} %param.8) | copy-start | bytes 3538948
  447.3 24.2 %collective-permute-start.35 = (bf16[256,1536]{1,0:T(8,128)(2,1)}, bf16[256,1536]{1,0:T(8,128)(2,1)S(1)}, u32[]{:S(2)}, u32[]{:S(2)}) collective-permute-start(bf16[256,1536]{1,0:T(8,128)(2,1)} %assemble.7.here_ref), channel_id=1, source_target_pairs={{4,0},{8,4},{12,8},{16,12},{20,16},{24,20},{28,24},{5,1},{9,5},{13... | collective-permute-start | bytes 2359304 | tf_op jit(solution)/shard_map/ppermute | solution.py:397
  448.7 24.3 %collective-permute-start.34 = (bf16[256,1536]{1,0:T(8,128)(2,1)}, bf16[256,1536]{1,0:T(8,128)(2,1)}, u32[]{:S(2)}, u32[]{:S(2)}) collective-permute-start(bf16[256,1536]{1,0:T(8,128)(2,1)} %assemble.7.here_ref), channel_id=1, source_target_pairs={{0,4},{4,8},{8,12},{12,16},{16,20},{20,24},{24,28},{1,5},{5,9},{9,... | collective-permute-start | bytes 2359304 | tf_op jit(solution)/shard_map/ppermute | solution.py:396
  464.2 29.8 %collective-permute-start.27 = (bf16[256,1536]{1,0:T(8,128)(2,1)}, bf16[256,1536]{1,0:T(8,128)(2,1)S(1)}, u32[]{:S(2)}, u32[]{:S(2)}) collective-permute-start(bf16[256,1536]{1,0:T(8,128)(2,1)} %assemble.6.here_ref), channel_id=1, source_target_pairs={{4,0},{8,4},{12,8},{16,12},{20,16},{24,20},{28,24},{5,1},{9,5},{13... | collective-permute-start | bytes 2359304 | tf_op jit(solution)/shard_map/ppermute | solution.py:397
  465.4 31.2 %collective-permute-start.26 = (bf16[256,1536]{1,0:T(8,128)(2,1)}, bf16[256,1536]{1,0:T(8,128)(2,1)S(1)}, u32[]{:S(2)}, u32[]{:S(2)}) collective-permute-start(bf16[256,1536]{1,0:T(8,128)(2,1)} %assemble.6.here_ref), channel_id=1, source_target_pairs={{0,4},{4,8},{8,12},{12,16},{16,20},{20,24},{24,28},{1,5},{5,9},{9,... | collective-permute-start | bytes 2359304 | tf_op jit(solution)/shard_map/ppermute | solution.py:396
  470.4 9.3 %collective-permute-start.39 = (bf16[64,1024]{1,0:T(8,128)(2,1)}, bf16[64,1024]{1,0:T(8,128)(2,1)S(1)}, u32[]{:S(2)}, u32[]{:S(2)}) collective-permute-start(bf16[64,1024]{1,0:T(8,128)(2,1)} %get-tuple-element.91), channel_id=1, source_target_pairs={{0,4},{4,0},{8,12},{12,8},{16,20},{20,16},{24,28},{28,24},{1,5},{5... | collective-permute-start | bytes 393224 | tf_op jit(solution)/shard_map/ppermute | solution.py:385
  471.5 20.1 %collective-permute-start.40 = (bf16[64,1024]{1,0:T(8,128)(2,1)}, bf16[64,1024]{1,0:T(8,128)(2,1)S(1)}, u32[]{:S(2)}, u32[]{:S(2)}) collective-permute-start(bf16[64,1024]{1,0:T(8,128)(2,1)} %get-tuple-element.92), channel_id=1, source_target_pairs={{0,8},{4,12},{8,0},{12,4},{16,24},{20,28},{24,16},{28,20},{1,9},{5... | collective-permute-start | bytes 393224 | tf_op jit(solution)/shard_map/ppermute | solution.py:385
  473.1 20.8 %collective-permute-start.41 = (bf16[64,1024]{1,0:T(8,128)(2,1)}, bf16[64,1024]{1,0:T(8,128)(2,1)S(1)}, u32[]{:S(2)}, u32[]{:S(2)}) collective-permute-start(bf16[64,1024]{1,0:T(8,128)(2,1)} %get-tuple-element.93), channel_id=1, source_target_pairs={{0,12},{4,8},{8,4},{12,0},{16,28},{20,24},{24,20},{28,16},{1,13},{... | collective-permute-start | bytes 393224 | tf_op jit(solution)/shard_map/ppermute | solution.py:385
  473.1 18.5 %copy-start.59 = (bf16[64,1024]{1,0:T(8,128)(2,1)S(1)}, bf16[64,1024]{1,0:T(8,128)(2,1)}, u32[]{:S(2)}) copy-start(bf16[64,1024]{1,0:T(8,128)(2,1)} %get-tuple-element.94) | copy-start | bytes 393220
  473.1 20.8 %copy-start.58 = (bf16[64,1024]{1,0:T(8,128)(2,1)S(1)}, bf16[64,1024]{1,0:T(8,128)(2,1)}, u32[]{:S(2)}) copy-start(bf16[64,1024]{1,0:T(8,128)(2,1)} %get-tuple-element.95) | copy-start | bytes 393220
  473.1 20.9 %copy-start.57 = (bf16[64,1024]{1,0:T(8,128)(2,1)S(1)}, bf16[64,1024]{1,0:T(8,128)(2,1)}, u32[]{:S(2)}) copy-start(bf16[64,1024]{1,0:T(8,128)(2,1)} %get-tuple-element.96) | copy-start | bytes 393220
  473.1 23.5 %copy-start.56 = (bf16[64,1024]{1,0:T(8,128)(2,1)S(1)}, bf16[64,1024]{1,0:T(8,128)(2,1)}, u32[]{:S(2)}) copy-start(bf16[64,1024]{1,0:T(8,128)(2,1)} %get-tuple-element.97) | copy-start | bytes 393220
  479.6 24.4 %copy-start.32 = (bf16[64,1024]{1,0:T(8,128)(2,1)}, bf16[64,1024]{1,0:T(8,128)(2,1)S(1)}, u32[]{:S(2)}) copy-start(bf16[64,1024]{1,0:T(8,128)(2,1)S(1)} %collective-permute-done.39.refs_1_) | copy-start | bytes 393220
  479.7 39.5 %collective-permute-start.36 = (bf16[64,1536]{1,0:T(8,128)(2,1)}, bf16[64,1536]{1,0:T(8,128)(2,1)S(1)}, u32[]{:S(2)}, u32[]{:S(2)}) collective-permute-start(bf16[64,1536]{1,0:T(8,128)(2,1)} %get-tuple-element.87), channel_id=1, source_target_pairs={{0,1},{1,0},{2,3},{3,2},{4,5},{5,4},{6,7},{7,6},{8,9},{9,8},{10,11... | collective-permute-start | bytes 589832 | tf_op jit(solution)/shard_map/ppermute | solution.py:385
  491.6 12.5 %collective-permute-start.42 = (bf16[64,1024]{1,0:T(8,128)(2,1)S(1)}, bf16[64,1024]{1,0:T(8,128)(2,1)S(1)}, u32[]{:S(2)}, u32[]{:S(2)}) collective-permute-start(bf16[64,1024]{1,0:T(8,128)(2,1)S(1)} %copy-done.59), channel_id=1, source_target_pairs={{0,16},{4,20},{8,24},{12,28},{16,0},{20,4},{24,8},{28,12},{1,17},{... | collective-permute-start | bytes 393224 | tf_op jit(solution)/shard_map/ppermute | solution.py:385
  493.9 20.8 %collective-permute-start.43 = (bf16[64,1024]{1,0:T(8,128)(2,1)S(1)}, bf16[64,1024]{1,0:T(8,128)(2,1)S(1)}, u32[]{:S(2)}, u32[]{:S(2)}) collective-permute-start(bf16[64,1024]{1,0:T(8,128)(2,1)S(1)} %copy-done.58), channel_id=1, source_target_pairs={{0,20},{4,16},{8,28},{12,24},{16,4},{20,0},{24,12},{28,8},{1,21},{... | collective-permute-start | bytes 393224 | tf_op jit(solution)/shard_map/ppermute | solution.py:385
  494.0 22.7 %collective-permute-start.44 = (bf16[64,1024]{1,0:T(8,128)(2,1)S(1)}, bf16[64,1024]{1,0:T(8,128)(2,1)S(1)}, u32[]{:S(2)}, u32[]{:S(2)}) collective-permute-start(bf16[64,1024]{1,0:T(8,128)(2,1)S(1)} %copy-done.57), channel_id=1, source_target_pairs={{0,24},{4,28},{8,16},{12,20},{16,8},{20,12},{24,0},{28,4},{1,25},{... | collective-permute-start | bytes 393224 | tf_op jit(solution)/shard_map/ppermute | solution.py:385
  496.6 18.1 %copy-start.48 = (bf16[64,1536]{1,0:T(8,128)(2,1)S(1)}, bf16[64,1536]{1,0:T(8,128)(2,1)}, u32[]{:S(2)}) copy-start(bf16[64,1536]{1,0:T(8,128)(2,1)} %get-tuple-element.89) | copy-start | bytes 589828
  496.6 20.6 %collective-permute-start.45 = (bf16[64,1024]{1,0:T(8,128)(2,1)S(1)}, bf16[64,1024]{1,0:T(8,128)(2,1)S(1)}, u32[]{:S(2)}, u32[]{:S(2)}) collective-permute-start(bf16[64,1024]{1,0:T(8,128)(2,1)S(1)} %copy-done.56), channel_id=1, source_target_pairs={{0,28},{4,24},{8,20},{12,16},{16,12},{20,8},{24,4},{28,0},{1,29},{... | collective-permute-start | bytes 393224 | tf_op jit(solution)/shard_map/ppermute | solution.py:385
  504.1 24.8 %collective-permute-start.37 = (bf16[64,1536]{1,0:T(8,128)(2,1)S(1)}, bf16[64,1536]{1,0:T(8,128)(2,1)S(1)}, u32[]{:S(2)}, u32[]{:S(2)}) collective-permute-start(bf16[64,1536]{1,0:T(8,128)(2,1)S(1)} %copy-done.49), channel_id=1, source_target_pairs={{0,2},{1,3},{2,0},{3,1},{4,6},{5,7},{6,4},{7,5},{8,10},{9,11},{10,... | collective-permute-start | bytes 589832 | tf_op jit(solution)/shard_map/ppermute | solution.py:385
  514.7 14.2 %collective-permute-start.38 = (bf16[64,1536]{1,0:T(8,128)(2,1)S(1)}, bf16[64,1536]{1,0:T(8,128)(2,1)S(1)}, u32[]{:S(2)}, u32[]{:S(2)}) collective-permute-start(bf16[64,1536]{1,0:T(8,128)(2,1)S(1)} %copy-done.48), channel_id=1, source_target_pairs={{0,3},{1,2},{2,1},{3,0},{4,7},{5,6},{6,5},{7,4},{8,11},{9,10},{10,... | collective-permute-start | bytes 589832 | tf_op jit(solution)/shard_map/ppermute | solution.py:385
  516.7 13.8 %collective-permute-start.28 = (bf16[64,1536]{1,0:T(8,128)(2,1)}, bf16[64,1536]{1,0:T(8,128)(2,1)S(1)}, u32[]{:S(2)}, u32[]{:S(2)}) collective-permute-start(bf16[64,1536]{1,0:T(8,128)(2,1)} %get-tuple-element.79), channel_id=1, source_target_pairs={{0,1},{1,0},{2,3},{3,2},{4,5},{5,4},{6,7},{7,6},{8,9},{9,8},{10,11... | collective-permute-start | bytes 589832 | tf_op jit(solution)/shard_map/ppermute | solution.py:385
  517.3 28.4 %collective-permute-start.29 = (bf16[64,1536]{1,0:T(8,128)(2,1)}, bf16[64,1536]{1,0:T(8,128)(2,1)S(1)}, u32[]{:S(2)}, u32[]{:S(2)}) collective-permute-start(bf16[64,1536]{1,0:T(8,128)(2,1)} %get-tuple-element.80), channel_id=1, source_target_pairs={{0,2},{1,3},{2,0},{3,1},{4,6},{5,7},{6,4},{7,5},{8,10},{9,11},{10,... | collective-permute-start | bytes 589832 | tf_op jit(solution)/shard_map/ppermute | solution.py:385
  519.1 26.5 %collective-permute-start.30 = (bf16[64,1536]{1,0:T(8,128)(2,1)}, bf16[64,1536]{1,0:T(8,128)(2,1)S(1)}, u32[]{:S(2)}, u32[]{:S(2)}) collective-permute-start(bf16[64,1536]{1,0:T(8,128)(2,1)} %get-tuple-element.81), channel_id=1, source_target_pairs={{0,3},{1,2},{2,1},{3,0},{4,7},{5,6},{6,5},{7,4},{8,11},{9,10},{10,... | collective-permute-start | bytes 589832 | tf_op jit(solution)/shard_map/ppermute | solution.py:385
  (42 other events, 295.7 us)

commit v2 on v1

--- a/solution.py
+++ b/solution.py
@@ -10,11 +10,14 @@
 SPACING = 8
 LANES = 128
 STEP = 120
-TOGETHER = 4
+WINDOW = 12
 OBS = 256
+SIDE = 16
+JOIN = 2
 
 VMEM = pl.BlockSpec(memory_space=pltpu.VMEM)
 SMEM = pl.BlockSpec(memory_space=pltpu.SMEM)
+SMALL = pl.CostEstimate(flops=1000, bytes_accessed=1000, transcendentals=0)
 PARAMS = pltpu.CompilerParams(vmem_limit_bytes=56 * 1024 * 1024)
 
 
@@ -66,6 +69,7 @@
         out_specs=[VMEM] * rows,
         scratch_shapes=[pltpu.VMEM((wide // LANES, group * rows, LANES), jnp.float32)],
         compiler_params=PARAMS,
+        cost_estimate=SMALL,
         name="split_rows",
     )(place, state)
 
@@ -97,6 +101,7 @@
         out_specs=VMEM,
         scratch_shapes=[pltpu.VMEM((wide // LANES, group * rows, LANES), jnp.float32)],
         compiler_params=PARAMS,
+        cost_estimate=SMALL,
         name="join_rows",
     )(place, *pieces)
 
@@ -117,6 +122,7 @@
         in_specs=[SMEM] + [VMEM] * len(pieces),
         out_specs=VMEM,
         compiler_params=PARAMS,
+        cost_estimate=SMALL,
         name="assemble",
     )(place, *pieces)
 
@@ -154,77 +160,154 @@
         out_specs=[VMEM] * parts,
         scratch_shapes=[pltpu.VMEM((3 * total, wide), jnp.float32)],
         compiler_params=PARAMS,
-        cost_estimate=pl.CostEstimate(
-            flops=18 * total * total * wide, bytes_accessed=8 * total * wide + 18 * total * total, transcendentals=0
-        ),
+        cost_estimate=SMALL,
         name="conv",
     )(place, weights, below, here, above)
 
 
-def pack_obs_kernel(width, place_ref, counts_ref, values_ref, weights_ref, cells_ref, *refs):
-    outs, tiles_ref = refs[:-1], refs[-1]
-    slabs = len(outs)
-    group = values_ref.shape[0] // slabs
-    slots = values_ref.shape[1]
+def pack_obs_kernel(width, counts_ref, values_ref, weights_ref, cells_ref, out_ref, tiles_ref):
+    slabs, depth, slots = out_ref.shape
+    group = depth - SIDE
     blocks = -(-width // STEP)
     for tile in range(slots // LANES):
         tiles_ref[tile] = values_ref[:, tile * LANES:(tile + 1) * LANES]
-    for k, out in enumerate(outs):
-        slab = place_ref[0] ^ k
+    for slab in range(slabs):
         used = lane_iota((1, slots)) < counts_ref[0, slab]
         values = jnp.concatenate(
             [tiles_ref[tile, pl.ds(slab, group, stride=slabs), :] for tile in range(slots // LANES)], axis=1
         )
-        out[:group, :] = jnp.where(used, values, 0.0).astype(jnp.bfloat16)
+        out_ref[slab, :group, :] = jnp.where(used, values, 0.0).astype(jnp.bfloat16)
         weights = jnp.where(used, weights_ref[slab], 0.0)
         local = (cells_ref[slab] - slab * (SPACING * width)).astype(jnp.float32)
         row = jnp.clip(jnp.floor((local + 0.5) * (1.0 / width)), 0.0, SPACING - 2.0)
         column = local - row * width
         block = jnp.clip(jnp.floor((column + 0.5) * (1.0 / STEP)), 0.0, blocks - 1.0)
-        tail = jnp.concatenate(
-            [weights, row * blocks + block, column - block * STEP, jnp.zeros((10, slots), jnp.float32)], axis=0
+        side = jnp.concatenate(
+            [weights, row * blocks + block, column - block * STEP, jnp.zeros((SIDE - 6, slots), jnp.float32)],
+            axis=0,
         )
-        out[group:, :] = tail.astype(jnp.bfloat16)
-
-
-def pack_obs(place, counts, values, weights, cells, width):
+        out_ref[slab, group:, :] = side.astype(jnp.bfloat16)
+
+
+def pack_obs(counts, values, weights, cells, width):
     group, slabs, slots = values.shape
     return pl.pallas_call(
         functools.partial(pack_obs_kernel, width),
-        out_shape=[jax.ShapeDtypeStruct((group + 16, slots), jnp.bfloat16)] * slabs,
-        in_specs=[SMEM, SMEM, VMEM, VMEM, VMEM],
-        out_specs=[VMEM] * slabs,
+        out_shape=jax.ShapeDtypeStruct((slabs, group + SIDE, slots), jnp.bfloat16),
+        in_specs=[SMEM, VMEM, VMEM, VMEM],
+        out_specs=VMEM,
         scratch_shapes=[pltpu.VMEM((slots // LANES, group * slabs, LANES), jnp.float32)],
         compiler_params=PARAMS,
+        cost_estimate=SMALL,
         name="pack_obs",
-    )(place, counts, values.reshape(group * slabs, slots), weights, cells)
-
-
-def unpack_obs_kernel(place_ref, *refs):
-    pieces, out_ref, tiles_ref = refs[:-2], refs[-2], refs[-1]
-    slabs = len(pieces)
-    group = out_ref.shape[0] // slabs
-    for k, piece in enumerate(pieces):
-        slab = place_ref[0] ^ k
-        for tile in range(tiles_ref.shape[0]):
-            part = piece[:, tile * LANES:(tile + 1) * LANES].astype(jnp.float32)
+    )(counts, values.reshape(group * slabs, slots), weights, cells)
+
+
+def sort_obs_kernel(begin, obs_ref, sorted_ref, rank_ref, first_ref, last_ref, joined_ref, column_ref):
+    sets, depth, size = sorted_ref.shape
+    group = depth - SIDE
+    each = obs_ref.shape[2]
+    for s in range(sets):
+        for i in range(size // each):
+            joined_ref[:, i * each:(i + 1) * each] = obs_ref[begin + s * (size // each) + i]
+        which = joined_ref[group:, :].astype(jnp.float32)[4:5]
+        key = which * size + lane_iota((1, size)).astype(jnp.float32)
+        column_ref[...] = jnp.transpose(jnp.broadcast_to(key, (LANES, size)))
+        ranks = []
+        for tile in range(size // LANES):
+            below = jnp.where(column_ref[...] < key[:, tile * LANES:(tile + 1) * LANES], 1.0, 0.0)
+            ranks.append(jnp.sum(below, axis=0, keepdims=True))
+        rank = jnp.concatenate(ranks, axis=1)
+        rank_ref[s] = rank.astype(jnp.int32)
+        column_ref[...] = jnp.transpose(jnp.broadcast_to(rank, (LANES, size)))
+
+        @pl.loop(0, size // OBS)
+        def _(tile):
+            start = pl.multiple_of(tile * OBS, OBS)
+            chosen = []
+            for i in range(OBS // LANES):
+                order = (lane_iota((1, LANES)) + (start + i * LANES)).astype(jnp.float32)
+                chosen.append(jnp.where(column_ref[...] == order, 1.0, 0.0).astype(jnp.bfloat16))
+            taken = jnp.dot(
+                joined_ref[...], jnp.concatenate(chosen, axis=1), preferred_element_type=jnp.float32
+            )
+            sorted_ref[s, :, pl.ds(start, OBS)] = taken.astype(jnp.bfloat16)
+            which = taken[group + 4:group + 5]
+            first_ref[s * (size // OBS) + tile] = jnp.min(which).astype(jnp.int32)
+            last_ref[s * (size // OBS) + tile] = jnp.max(which).astype(jnp.int32)
+
+
+def sort_obs(obs, begin, slabs):
+    depth, slots = obs.shape[1:]
+    size = slots * JOIN
+    sets = slabs // JOIN
+    return pl.pallas_call(
+        functools.partial(sort_obs_kernel, begin),
+        out_shape=[
+            jax.ShapeDtypeStruct((sets, depth, size), jnp.bfloat16),
+            jax.ShapeDtypeStruct((sets, 1, size), jnp.int32),
+            jax.ShapeDtypeStruct((sets * size // OBS,), jnp.int32),
+            jax.ShapeDtypeStruct((sets * size // OBS,), jnp.int32),
+        ],
+        in_specs=[VMEM],
+        out_specs=[VMEM, VMEM, SMEM, SMEM],
+        scratch_shapes=[pltpu.VMEM((depth, size), jnp.bfloat16), pltpu.VMEM((size, LANES), jnp.float32)],
+        compiler_params=PARAMS,
+        cost_estimate=SMALL,
+        name="sort_obs",
+    )(obs)
+
+
+def unsort_obs_kernel(sorted_ref, one_ref, two_ref, out_ref):
+    sets, group, size = sorted_ref.shape
+    each = out_ref.shape[2]
+    for s in range(sets):
+        @pl.loop(0, size // OBS)
+        def _(tile):
+            start = pl.multiple_of(tile * OBS, OBS)
+            rank = (one_ref if s < sets // 2 else two_ref)[s % (sets // 2), :, pl.ds(start, OBS)]
+            chosen = jnp.where(lax.broadcasted_iota(jnp.int32, (size, OBS), 0) == rank, 1.0, 0.0)
+            taken = jnp.dot(sorted_ref[s], chosen.astype(jnp.bfloat16), preferred_element_type=jnp.float32)
+            slab = s * (size // each) + tile // (each // OBS)
+            at = pl.ds(pl.multiple_of(tile % (each // OBS) * OBS, OBS), OBS)
+            out_ref[slab, :, at] = taken.astype(jnp.bfloat16)
+
+
+def unsort_obs(values, one, two, slabs):
+    sets, group, size = values.shape
+    return pl.pallas_call(
+        unsort_obs_kernel,
+        out_shape=jax.ShapeDtypeStruct((slabs, group, sets * size // slabs), jnp.bfloat16),
+        in_specs=[VMEM] * 3,
+        out_specs=VMEM,
+        compiler_params=PARAMS,
+        cost_estimate=SMALL,
+        name="unsort_obs",
+    )(values, one, two)
+
+
+def unpack_obs_kernel(values_ref, out_ref, tiles_ref):
+    slabs, group, slots = values_ref.shape
+    for slab in range(slabs):
+        for tile in range(slots // LANES):
+            part = values_ref[slab, :, tile * LANES:(tile + 1) * LANES].astype(jnp.float32)
             tiles_ref[tile, pl.ds(slab, group, stride=slabs), :] = part
-    for tile in range(tiles_ref.shape[0]):
+    for tile in range(slots // LANES):
         out_ref[:, tile * LANES:(tile + 1) * LANES] = tiles_ref[tile]
 
 
-def unpack_obs(place, pieces):
-    group, slots = pieces[0].shape
-    slabs = len(pieces)
+def unpack_obs(values):
+    slabs, group, slots = values.shape
     return pl.pallas_call(
         unpack_obs_kernel,
         out_shape=jax.ShapeDtypeStruct((group * slabs, slots), jnp.float32),
-        in_specs=[SMEM] + [VMEM] * slabs,
+        in_specs=[VMEM],
         out_specs=VMEM,
         scratch_shapes=[pltpu.VMEM((slots // LANES, group * slabs, LANES), jnp.float32)],
         compiler_params=PARAMS,
+        cost_estimate=SMALL,
         name="unpack_obs",
-    )(place, *pieces)
+    )(values)
 
 
 def gelu_value(value):
@@ -238,14 +321,20 @@
     )
 
 
-def observe_kernel(parts, rounds, slabs, width, place_ref, bias_ref, *refs):
+def observe_kernel(parts, rounds, width, place_ref, *refs):
     rows = parts * rounds
-    mixed, obs = refs[:rows], refs[rows:rows + slabs]
-    grads = refs[rows + slabs:2 * rows + slabs]
-    departures = refs[2 * rows + slabs:2 * rows + 2 * slabs]
-    pre_ref, table_ref, found_ref, row_ref = refs[2 * rows + 2 * slabs:]
+    firsts, lasts, halves, bias_ref = refs[0:2], refs[2:4], refs[4:6], refs[6]
+    mixed, grads, departure_ref = refs[7:7 + rows], refs[7 + rows:7 + 2 * rows], refs[7 + 2 * rows]
+    pre_ref, table_ref, found_ref, row_ref, obs_ref, arrival = refs[8 + 2 * rows:]
+    sets = obs_ref.shape[0] // 2
+    copies = [
+        pltpu.make_async_copy(half, obs_ref.at[pl.ds(i * sets, sets)], arrival.at[i])
+        for i, half in enumerate(halves)
+    ]
+    for copy in copies:
+        copy.start()
     group, wide = mixed[0].shape
-    slots = obs[0].shape[1]
+    size = obs_ref.shape[2]
     blocks = -(-width // STEP)
     tiles = wide // LANES
     place = place_ref[0]
@@ -285,46 +374,59 @@
                 table_ref[pl.ds(at, group), LANES:] = block
 
     found_ref[...] = jnp.zeros_like(found_ref)
-    steps = (rows - 1) * blocks // TOGETHER
-    high = TOGETHER * group
+    table_ref[(rows - 1) * blocks * group:, :] = jnp.zeros((WINDOW * group, 2 * LANES), jnp.bfloat16)
+    high = WINDOW * group
     lo_iota = lax.broadcasted_iota(jnp.int32, (LANES, OBS), 0)
-    for s in range(slabs):
-        @pl.loop(0, slots // OBS)
-        def _(sub):
-            at = pl.ds(pl.multiple_of(sub * OBS, OBS), OBS)
-            side = obs[s][group:, at].astype(jnp.float32)
-            which = side[4:5].astype(jnp.int32)
-            low = side[5:6].astype(jnp.int32)
-            first, second = lo_iota == low, lo_iota == low + 1
-            spread = jnp.concatenate(
-                [
-                    jnp.where(first, side[0:1], jnp.where(second, side[1:2], 0.0)),
-                    jnp.where(first, side[2:3], jnp.where(second, side[3:4], 0.0)),
-                ],
-                axis=0,
+
+    for copy in copies:
+        copy.wait()
+    count = firsts[0].shape[0]
+
+    @pl.loop(0, 2 * count)
+    def _(number):
+        s = number // (size // OBS)
+        at = pl.ds(pl.multiple_of(number % (size // OBS) * OBS, OBS), OBS)
+        side = obs_ref[s, group:, at].astype(jnp.float32)
+        which = side[4:5].astype(jnp.int32)
+        low = side[5:6].astype(jnp.int32)
+        first, second = lo_iota == low, lo_iota == low + 1
+        spread = jnp.concatenate(
+            [
+                jnp.where(first, side[0:1], jnp.where(second, side[1:2], 0.0)),
+                jnp.where(first, side[2:3], jnp.where(second, side[3:4], 0.0)),
+            ],
+            axis=0,
+        ).astype(jnp.bfloat16)
+        whole = jnp.broadcast_to(which, (group, OBS))
+        here, there = jnp.minimum(number, count - 1), jnp.maximum(number - count, 0)
+        lowest = jnp.where(number < count, firsts[0][here], firsts[1][there])
+        highest = jnp.where(number < count, lasts[0][here], lasts[1][there])
+        lowest = jnp.clip(lowest, 0, (rows - 1) * blocks - 1)
+        highest = jnp.clip(highest, 0, (rows - 1) * blocks - 1)
+        windows = (highest - lowest) // WINDOW + 1
+
+        def gather(window, model):
+            base = lowest + window * WINDOW
+            start = pl.multiple_of(base * group, group)
+            part = jnp.dot(table_ref[pl.ds(start, high), :], spread, preferred_element_type=jnp.float32)
+            for i in range(WINDOW):
+                model = jnp.where(whole == base + i, part[i * group:(i + 1) * group], model)
+            return model
+
+        model = lax.fori_loop(0, windows, gather, jnp.zeros((group, OBS), jnp.float32))
+        departure = model - obs_ref[s, :group, at].astype(jnp.float32)
+        departure_ref[s, :, at] = departure.astype(jnp.bfloat16)
+
+        @pl.loop(0, windows)
+        def _(window):
+            base = lowest + window * WINDOW
+            start = pl.multiple_of(base * group, group)
+            chosen = jnp.concatenate(
+                [jnp.where(whole == base + i, departure, 0.0) for i in range(WINDOW)], axis=0
             ).astype(jnp.bfloat16)
-            whole = jnp.broadcast_to(which, (group, OBS))
-
-            def gather(step, model):
-                start = pl.multiple_of(step * high, high)
-                part = jnp.dot(table_ref[pl.ds(start, high), :], spread, preferred_element_type=jnp.float32)
-                for i in range(TOGETHER):
-                    model = jnp.where(whole == step * TOGETHER + i, part[i * group:(i + 1) * group], model)
-                return model
-
-            model = lax.fori_loop(0, steps, gather, jnp.zeros((group, OBS), jnp.float32))
-            departure = model - obs[s][:group, at].astype(jnp.float32)
-            departures[s][:, at] = departure.astype(jnp.bfloat16)
-
-            @pl.loop(0, steps)
-            def _(step):
-                start = pl.multiple_of(step * high, high)
-                chosen = jnp.concatenate(
-                    [jnp.where(whole == step * TOGETHER + i, departure, 0.0) for i in range(TOGETHER)], axis=0
-                ).astype(jnp.bfloat16)
-                found_ref[pl.ds(start, high), :] += lax.dot_general(
-                    chosen, spread, (((1,), (1,)), ((), ())), preferred_element_type=jnp.float32
-                )
+            found_ref[pl.ds(start, high), :] += lax.dot_general(
+                chosen, spread, (((1,), (1,)), ((), ())), preferred_element_type=jnp.float32
+            )
 
     for turn in range(rounds):
         for k in range(parts):
@@ -355,28 +457,31 @@
             out[:, last * LANES:] = wrapped_tail(sums[0], sums[last], rem).astype(jnp.bfloat16)
 
 
-def observe(place, bias, mixed, obs, parts, width):
+def observe(place, one, two, bias, mixed, parts, width):
     group, wide = mixed[0].shape
-    rows, slabs = len(mixed), len(obs)
-    slots = obs[0].shape[1]
+    rows = len(mixed)
     blocks = -(-width // STEP)
-    found = (rows - 1) * blocks * group
+    found = ((rows - 1) * blocks + WINDOW) * group
+    sets, depth, size = 2 * one[0].shape[0], one[0].shape[1], one[0].shape[2]
     results = pl.pallas_call(
-        functools.partial(observe_kernel, parts, rows // parts, slabs, width),
+        functools.partial(observe_kernel, parts, rows // parts, width),
         out_shape=[jax.ShapeDtypeStruct((group, wide), jnp.bfloat16)] * rows
-        + [jax.ShapeDtypeStruct((group, slots), jnp.bfloat16)] * slabs,
-        in_specs=[SMEM] + [VMEM] * (1 + rows + slabs),
-        out_specs=[VMEM] * (rows + slabs),
+        + [jax.ShapeDtypeStruct((sets, group, size), jnp.bfloat16)],
+        in_specs=[SMEM] * 5 + [pl.BlockSpec(memory_space=pl.ANY)] * 2 + [VMEM] * (1 + rows),
+        out_specs=[VMEM] * (rows + 1),
         scratch_shapes=[
             pltpu.VMEM((rows, group, wide), jnp.float32),
             pltpu.VMEM((found, 2 * LANES), jnp.bfloat16),
             pltpu.VMEM((found, 2 * LANES), jnp.float32),
             pltpu.VMEM((group, wide), jnp.float32),
+            pltpu.VMEM((sets, depth, size), jnp.bfloat16),
+            pltpu.SemaphoreType.DMA((2,)),
         ],
         compiler_params=PARAMS,
+        cost_estimate=SMALL,
         name="observe",
-    )(place, bias, *mixed, *obs)
-    return results[:rows], results[rows:]
+    )(place, one[2], two[2], one[3], two[3], one[0], two[0], bias, *mixed)
+    return results[:rows], results[rows]
 
 
 def swap(piece, axis, k):
@@ -385,19 +490,36 @@
     return lax.ppermute(piece, axis, [(i, i ^ k) for i in range(lax.axis_size(axis))])
 
 
-def mix(place, weights, pieces, parts):
+def after(value, *others):
+    return lax.optimization_barrier((value, *others))[0]
+
+
+def mix(place, weights, pieces, parts, ahead=(), between=None):
     count = lax.axis_size("lat")
     forward = [(i, i + 1) for i in range(count - 1)]
     backward = [(i + 1, i) for i in range(count - 1)]
-    results = []
-    for turn in range(len(pieces) // parts):
-        own = pieces[turn * parts:(turn + 1) * parts]
-        here = assemble(place, [swap(own[k], "chan", k) for k in range(parts)])
-        below = lax.ppermute(here, "lat", forward)
-        above = lax.ppermute(here, "lat", backward)
-        mixed = conv(place, weights, below, here, above, parts)
-        results += [swap(mixed[k], "chan", k) for k in range(parts)]
-    return results
+    results, done = [None] * len(pieces), ()
+    turns = len(pieces) // parts
+    here, arrived, halos, mixed = None, [None] * parts, ahead, None
+    for turn in range(turns):
+        own = list(pieces[turn * parts:(turn + 1) * parts])
+        if turn:
+            own[1:] = [after(own[k], arrived[k] if k > 1 else here) for k in range(1, parts)]
+        arrived = [swap(own[k], "chan", k) for k in range(parts)]
+        if between is not None and turn == min(1, turns - 1):
+            done = between(here if turn else arrived[1])
+            arrived[0] = after(arrived[0], *done)
+        here = assemble(place, arrived)
+        if halos:
+            here = after(here, *halos)
+        halos = [lax.ppermute(here, "lat", forward), lax.ppermute(here, "lat", backward)]
+        ready = after(here, results[0]) if turn else here
+        mixed = list(conv(place, weights, halos[0], ready, halos[1], parts))
+        for k in range(parts):
+            if turn and k:
+                mixed[k] = after(mixed[k], results[(turn - 1) * parts + k])
+            results[turn * parts + k] = swap(mixed[k], "chan", k)
+    return results, done
 
 
 def shards(state, kernel, bias, innovations, interp, cells, counts):
@@ -406,22 +528,33 @@
     wide = padded_width(width)
     total = kernel.shape[2]
     chan_place = lax.axis_index("chan").reshape(1)
-    lat_place = lax.axis_index("lat").reshape(1)
     forward_weights = kernel.reshape(3, 3 * total, total)
     backward_weights = jnp.transpose(kernel[::-1, ::-1], (0, 1, 3, 2)).reshape(3, 3 * total, total)
 
-    mixed = mix(chan_place, forward_weights, split_rows(chan_place, state, parts, wide), parts)
-
-    interp_rows = jnp.transpose(interp[:, 0], (1, 0, 2)).astype(jnp.float32)
-    packed = pack_obs(
-        lat_place, counts, innovations[:, 0], interp_rows, cells[0][:, None, :], width
+    pieces = split_rows(chan_place, state, parts, wide)
+
+    def send_obs(ahead):
+        used, rows_of, cells_of = lax.optimization_barrier((counts, interp, cells, ahead))[:3]
+        interp_rows = jnp.transpose(rows_of[:, 0], (1, 0, 2)).astype(jnp.float32)
+        packed = pack_obs(used, innovations[:, 0], interp_rows, cells_of[0][:, None, :], width)
+        return lax.all_to_all(packed, "lat", split_axis=0, concat_axis=0, tiled=True)
+
+    obs = send_obs(pieces[0])
+    mixed, one = mix(
+        chan_place, forward_weights, pieces, parts, (obs,),
+        lambda ahead: sort_obs(after(obs, ahead), 0, slabs // 2),
     )
-    obs = [swap(packed[k], "lat", k) for k in range(slabs)]
-
-    grads, departures = observe(chan_place, bias[:, None], mixed, obs, parts, width)
-    returned = [swap(departures[k], "lat", k) for k in range(slabs)]
-    departures_out = unpack_obs(lat_place, returned).reshape(innovations.shape)
-    grad_state = join_rows(chan_place, mix(chan_place, backward_weights, grads, parts), parts, width)
+    two = sort_obs(after(obs, mixed[-parts]), slabs // 2, slabs // 2)
+    grads, departures = observe(chan_place, one, two, bias[:, None], mixed, parts, width)
+    grad_pieces, (unsorted,) = mix(
+        chan_place, backward_weights, grads, parts, (),
+        lambda ahead: [unsort_obs(after(departures, ahead), one[1], two[1], slabs)],
+    )
+    returned = lax.all_to_all(
+        after(unsorted, *grad_pieces[:1 - parts]), "lat", split_axis=0, concat_axis=0, tiled=True
+    )
+    departures_out = unpack_obs(returned).reshape(innovations.shape)
+    grad_state = join_rows(chan_place, grad_pieces, parts, width)
     return grad_state, departures_out
 
 

time: 553 us -> 269 us (0.49)
  Pallas kernels: 343 us -> 122 us
  starting transfers between devices: 116 us -> 72.7 us
  waiting for transfers between devices: 78.9 us -> 59.3 us
    pallas_call x2 -> x5, Pallas kernels: 298 us -> 77 us  [the longest x1 35.3 us: observe(): pl.pallas_call(functools.partial(observe_kernel, parts, rows // parts, wi...]
    ppermute x38 -> x24, starting transfers between devices: 96.3 us -> 40.4 us  [swap(): lax.ppermute(piece, axis, [(i, i ^ k) for i in range(lax.axis_size(axis))])]
    ppermute x38 -> x24, waiting for transfers between devices: 78.9 us -> 59.2 us  [swap(): lax.ppermute(piece, axis, [(i, i ^ k) for i in range(lax.axis_size(axis))])]
    all_to_all x0 -> x2, starting transfers between devices: none -> 16.4 us  [the longest x1 11.1 us: shards(): lax.all_to_all(after(unsorted, *grad_pieces[:1 - parts]), 'lat', split_ax...]
  transfers between devices with their start and end apart: 46 -> 34, of which waited for: 13 -> 10; matrix products, arithmetic and copies ran while one was open for 1% -> 1% of each run, Pallas kernels for 8% -> 28%
where the time goes in v2:
time: 269 us; the launch traced here: 268 us
  Pallas kernels  122 us (45%)
  starting transfers between devices  72.7 us (27%)
  waiting for transfers between devices  59.3 us (22%)
  local copies, waits for them, and re-layouts  12.9 us (5%)
    ppermute x24, waiting for transfers between devices, swap(): lax.ppermute(piece, axis, [(i, i ^ k) for i in range(lax.axis_size(axis))])  59.2 us
    ppermute x24, starting transfers between devices, swap(): lax.ppermute(piece, axis, [(i, i ^ k) for i in range(lax.axis_size(axis))])  40.4 us
    pallas_call x1, Pallas kernels, observe(): pl.pallas_call(functools.partial(observe_kernel, parts, rows // parts, wi...  35.3 us
    pallas_call x2, Pallas kernels, sort_obs(): pl.pallas_call(functools.partial(sort_obs_kernel, begin), out_shape=[jax....  26.1 us
    pallas_call x4, Pallas kernels, conv(): pl.pallas_call(conv_kernel, out_shape=[jax.ShapeDtypeStruct((group, wide)...  25.9 us
    pallas_call x1, Pallas kernels, unsort_obs(): pl.pallas_call(unsort_obs_kernel, out_shape=jax.ShapeDtypeStruct((slabs,...  12 us
    all_to_all x1, starting transfers between devices, shards(): lax.all_to_all(after(unsorted, *grad_pieces[:1 - parts]), 'lat', split_ax...  11.1 us
    ppermute x4, starting transfers between devices, mix(): lax.ppermute(here, 'lat', forward)  10.3 us
  transfers between devices with their start and end apart: 34, of which 10 were waited for; matrix products, arithmetic and copies ran while one was open for 1% of the time, Pallas kernels for 28%

profile of v2, /device:TPU:0, one launch (start us, length us, event | category | flops | bytes accessed | tf_op | source)
XLA Modules:
  0.0 267.7 jit_solution(9301558237291213341)
XLA Ops:
  0.7 3.2 %split_rows.1 = (bf16[64,1536]{1,0:T(8,128)(2,1)}, bf16[64,1536]{1,0:T(8,128)(2,1)}, bf16[64,1536]{1,0:T(8,128)(2,1)}, bf16[64,1536]{1,0:T(8,128)(2,1)}, bf16[64...) custom-call(s32[1]{0:T(128)} %bitcast.place_ref, ...), custom_call_target="tpu_custom_call" | custom-call | flops 1000 | bytes 1000 | tf_op jit(solution)/shard_map/split_rows/pallas_call | solution.py:65
  3.8 0.7 copy.15
  5.2 3.5 %pack_obs.1 = bf16[8,80,1024]{2,1,0:T(8,128)(2,1)} custom-call(s32[1,8]{1,0:T(1,128)} %counts_ref, f32[512,1024]{1,0:T(8,128)} %bitcast.23, f32[8,4,1024]{2,1,0:T(4,128)} %bitcast.24, s32[8,1,1024]{2,1,0:T(1,128)} %broadcast_in_dim_squeeze.3.cells_ref), custom_call_target="tpu_custom_call" | custom-call | flops 1000 | bytes 1000 | tf_op jit(solution)/shard_map/pack_obs/pallas_call | solution.py:194
  8.7 5.3 %all-to-all-start = ((bf16[8,80,1024]{2,1,0:T(8,128)(2,1)}), bf16[8,80,1024]{2,1,0:T(8,128)(2,1)S(1)}, u32[]{:S(2)}, u32[]{:S(2)}) async-start(bf16[8,80,1024]{2,1,0:T(8,128)(2,1)} %pack_obs.1), calls=%async_computation | async-start | bytes 2621440 | tf_op jit(solution)/shard_map/all_to_all | solution.py:540
  14.1 2.7 collective-permute-start.1
  16.7 1.4 collective-permute-start.2
  18.4 12.8 %collective-permute-done.1.refs_2_ = bf16[64,1536]{1,0:T(8,128)(2,1)S(1)} collective-permute-done((bf16[64,1536]{1,0:T(8,128)(2,1)S(1)}, bf16[64,1536]{1,0:T(8,128)(2,1)S(1)}, u32[]{:S(2)}, u32[]{:S(2)}) %collective-permute-start.1) | collective-permute-done | bytes 196640 | tf_op jit(solution)/shard_map/ppermute | solution.py:490
  31.2 0.9 collective-permute-done.refs_1_
  32.2 0.7 copy-done.20
  32.8 2.1 assemble.4.here_ref
  35.0 1.3 collective-permute-start.6
  36.3 1.3 collective-permute-start.7
  37.6 6.9 %collective-permute-start.4 = (bf16[64,1536]{1,0:T(8,128)(2,1)S(1)}, bf16[64,1536]{1,0:T(8,128)(2,1)S(1)}, u32[]{:S(2)}, u32[]{:S(2)}) collective-permute-start(bf16[64,1536]{1,0:T(8,128)(2,1)S(1)} %copy-done.41), channel_id=1, source_target_pairs={{0,2},{1,3},{2,0},{3,1},{4,6},{5,7},{6,4},{7,5},{8,10},{9,11},{10,... | collective-permute-start | bytes 589832 | tf_op jit(solution)/shard_map/ppermute | solution.py:490
  45.2 13.1 %sort_obs.2 = (bf16[2,80,2048]{2,1,0:T(8,128)(2,1)}, s32[2,1,2048]{2,1,0:T(1,128)}, s32[16]{0:T(128)}, s32[16]{0:T(128)}) custom-call(bf16[8,80,1024]{2,1,0:T(8,128)(2,1)} %copy-done), custom_call_target="tpu_custom_call" | custom-call | flops 1000 | bytes 1000 | tf_op jit(solution)/shard_map/sort_obs/pallas_call | solution.py:244
  58.3 1.6 collective-permute-done.3.refs_1_
  59.9 0.7 copy-done.14
  60.6 2.2 assemble.5.here_ref
  62.7 2.8 %collective-permute-start.8 = (bf16[256,1536]{1,0:T(8,128)(2,1)}, bf16[256,1536]{1,0:T(8,128)(2,1)S(1)}, u32[]{:S(2)}, u32[]{:S(2)}) collective-permute-start(bf16[256,1536]{1,0:T(8,128)(2,1)} %assemble.5.here_ref), channel_id=1, source_target_pairs={{0,4},{4,8},{8,12},{12,16},{16,20},{20,24},{24,28},{1,5},{5,9},{9,... | collective-permute-start | bytes 2359304 | tf_op jit(solution)/shard_map/ppermute | solution.py:515
  65.6 1.5 collective-permute-start.9
  67.1 6.5 %conv.4 = (bf16[64,1536]{1,0:T(8,128)(2,1)}, bf16[64,1536]{1,0:T(8,128)(2,1)}, bf16[64,1536]{1,0:T(8,128)(2,1)}, bf16[64,1536]{1,0:T(8,128)(2,1)}) custom-call(s32[1]{0:T(128)} %bitcast.place_ref, bf16[3,768,256]{2,1,0:T(8,128)(2,1)} %bitcast.18, bf16[256,1536]{1,0:T(8,128)(2,1)} %copy-done.4, bf16[256,1536]{1,0:T(8,128)(2,1)} %assemble.4.here_ref, ...), custom_call_target="tpu_custom_call" | custom-call | flops 1000 | bytes 1000 | tf_op jit(solution)/shard_map/conv/pallas_call | solution.py:156
  73.5 3.2 %collective-permute-start.12 = (bf16[64,1536]{1,0:T(8,128)(2,1)}, bf16[64,1536]{1,0:T(8,128)(2,1)S(1)}, u32[]{:S(2)}, u32[]{:S(2)}) collective-permute-start(bf16[64,1536]{1,0:T(8,128)(2,1)} %get-tuple-element.100), channel_id=1, source_target_pairs={{0,3},{1,2},{2,1},{3,0},{4,7},{5,6},{6,5},{7,4},{8,11},{9,10},{10,... | collective-permute-start | bytes 589832 | tf_op jit(solution)/shard_map/ppermute | solution.py:490
  76.7 1.5 collective-permute-start.11
  78.3 0.9 copy-done.8
  79.1 0.9 copy-done.9
  80.0 6.5 %conv.5 = (bf16[64,1536]{1,0:T(8,128)(2,1)}, bf16[64,1536]{1,0:T(8,128)(2,1)}, bf16[64,1536]{1,0:T(8,128)(2,1)}, bf16[64,1536]{1,0:T(8,128)(2,1)}) custom-call(s32[1]{0:T(128)} %bitcast.place_ref, bf16[3,768,256]{2,1,0:T(8,128)(2,1)} %bitcast.19, bf16[256,1536]{1,0:T(8,128)(2,1)} %copy-done.8, bf16[256,1536]{1,0:T(8,128)(2,1)} %assemble.5.here_ref, ...), custom_call_target="tpu_custom_call" | custom-call | flops 1000 | bytes 1000 | tf_op jit(solution)/shard_map/conv/pallas_call | solution.py:156
  86.5 2.9 %collective-permute-start.15 = (bf16[64,1536]{1,0:T(8,128)(2,1)}, bf16[64,1536]{1,0:T(8,128)(2,1)S(1)}, u32[]{:S(2)}, u32[]{:S(2)}) collective-permute-start(bf16[64,1536]{1,0:T(8,128)(2,1)} %get-tuple-element.106), channel_id=1, source_target_pairs={{0,3},{1,2},{2,1},{3,0},{4,7},{5,6},{6,5},{7,4},{8,11},{9,10},{10,... | collective-permute-start | bytes 589832 | tf_op jit(solution)/shard_map/ppermute | solution.py:490
  89.4 8.6 %collective-permute-done.11.refs_9_ = bf16[64,1536]{1,0:T(8,128)(2,1)S(1)} collective-permute-done((bf16[64,1536]{1,0:T(8,128)(2,1)}, bf16[64,1536]{1,0:T(8,128)(2,1)S(1)}, u32[]{:S(2)}, u32[]{:S(2)}) %collective-permute-start.11) | collective-permute-done | bytes 196640 | tf_op jit(solution)/shard_map/ppermute | solution.py:490
  98.0 2.4 collective-permute-start.13
  100.4 0.7 copy.11.refs_6_
  101.1 13.1 %sort_obs.3 = (bf16[2,80,2048]{2,1,0:T(8,128)(2,1)}, s32[2,1,2048]{2,1,0:T(1,128)}, s32[16]{0:T(128)}, s32[16]{0:T(128)}) custom-call(bf16[8,80,1024]{2,1,0:T(8,128)(2,1)} %copy-done), custom_call_target="tpu_custom_call" | custom-call | flops 1000 | bytes 1000 | tf_op jit(solution)/shard_map/sort_obs/pallas_call | solution.py:244
  115.0 35.3 %observe.1 = (bf16[64,1536]{1,0:T(8,128)(2,1)}, bf16[64,1536]{1,0:T(8,128)(2,1)}, bf16[64,1536]{1,0:T(8,128)(2,1)}, bf16[64,1536]{1,0:T(8,128)(2,1)}, bf16[64,15...) custom-call(s32[1]{0:T(128)} %bitcast.place_ref, ...), custom_call_target="tpu_custom_call" | custom-call | flops 1000 | bytes 1000 | tf_op jit(solution)/shard_map/observe/pallas_call | solution.py:466
  150.4 2.0 collective-permute-start.18
  152.4 2.4 collective-permute-start.16
  154.9 5.5 %collective-permute-done.18.refs_3_ = bf16[64,1536]{1,0:T(8,128)(2,1)S(1)} collective-permute-done((bf16[64,1536]{1,0:T(8,128)(2,1)}, bf16[64,1536]{1,0:T(8,128)(2,1)S(1)}, u32[]{:S(2)}, u32[]{:S(2)}) %collective-permute-start.18) | collective-permute-done | bytes 196640 | tf_op jit(solution)/shard_map/ppermute | solution.py:490
  160.4 9.8 %collective-permute-done.17.refs_2_ = bf16[64,1536]{1,0:T(8,128)(2,1)S(1)} collective-permute-done((bf16[64,1536]{1,0:T(8,128)(2,1)}, bf16[64,1536]{1,0:T(8,128)(2,1)S(1)}, u32[]{:S(2)}, u32[]{:S(2)}) %collective-permute-start.17) | collective-permute-done | bytes 196640 | tf_op jit(solution)/shard_map/ppermute | solution.py:490
  170.3 0.7 copy-done.19
  171.0 2.2 assemble.6.here_ref
  173.2 2.1 collective-permute-start.19
  175.2 1.5 collective-permute-start.20
  176.8 2.2 collective-permute-start.26
  179.0 2.3 collective-permute-start.24
  181.2 12.0 %unsort_obs.1 = bf16[8,64,1024]{2,1,0:T(8,128)(2,1)} custom-call(bf16[4,64,2048]{2,1,0:T(8,128)(2,1)} %get-tuple-element.117.sorted_ref, s32[2,1,2048]{2,1,0:T(1,128)} %get-tuple-element.81.one_ref, s32[2,1,2048]{2,1,0:T(1,128)} %get-tuple-element.118.two_ref), custom_call_target="tpu_custom_call" | custom-call | flops 1000 | bytes 1000 | tf_op jit(solution)/shard_map/unsort_obs/pallas_call | solution.py:278
  193.2 1.7 collective-permute-done.25.refs_2_
  194.9 0.7 copy-done.13
  195.6 0.7 copy-done.17
  196.3 2.2 assemble.7.here_ref
  198.4 4.1 %collective-permute-start.27 = (bf16[256,1536]{1,0:T(8,128)(2,1)}, bf16[256,1536]{1,0:T(8,128)(2,1)S(1)}, u32[]{:S(2)}, u32[]{:S(2)}) collective-permute-start(bf16[256,1536]{1,0:T(8,128)(2,1)} %assemble.7.here_ref), channel_id=1, source_target_pairs={{0,4},{4,8},{8,12},{12,16},{16,20},{20,24},{24,28},{1,5},{5,9},{9,... | collective-permute-start | bytes 2359304 | tf_op jit(solution)/shard_map/ppermute | solution.py:515
  202.6 1.3 collective-permute-start.28
  204.0 1.5 copy.9
  205.5 6.5 %conv.6 = (bf16[64,1536]{1,0:T(8,128)(2,1)}, bf16[64,1536]{1,0:T(8,128)(2,1)}, bf16[64,1536]{1,0:T(8,128)(2,1)}, bf16[64,1536]{1,0:T(8,128)(2,1)}) custom-call(s32[1]{0:T(128)} %bitcast.place_ref, bf16[3,768,256]{2,1,0:T(8,128)(2,1)} %bitcast.20, bf16[256,1536]{1,0:T(8,128)(2,1)} %copy-done.3, bf16[256,1536]{1,0:T(8,128)(2,1)} %assemble.6.here_ref, ...), custom_call_target="tpu_custom_call" | custom-call | flops 1000 | bytes 1000 | tf_op jit(solution)/shard_map/conv/pallas_call | solution.py:156
  212.3 2.1 collective-permute-start.22
  214.4 2.0 collective-permute-start.23
  216.4 0.9 copy-done.7
  217.3 6.5 %conv.7 = (bf16[64,1536]{1,0:T(8,128)(2,1)}, bf16[64,1536]{1,0:T(8,128)(2,1)}, bf16[64,1536]{1,0:T(8,128)(2,1)}, bf16[64,1536]{1,0:T(8,128)(2,1)}) custom-call(s32[1]{0:T(128)} %bitcast.place_ref, bf16[3,768,256]{2,1,0:T(8,128)(2,1)} %bitcast.21, bf16[256,1536]{1,0:T(8,128)(2,1)} %copy-done.7, bf16[256,1536]{1,0:T(8,128)(2,1)} %assemble.7.here_ref, ...), custom_call_target="tpu_custom_call" | custom-call | flops 1000 | bytes 1000 | tf_op jit(solution)/shard_map/conv/pallas_call | solution.py:156
  223.8 1.7 collective-permute-done.23.refs_3_
  225.5 11.1 %all-to-all-start.1 = ((bf16[8,64,1024]{2,1,0:T(8,128)(2,1)}), bf16[8,64,1024]{2,1,0:T(8,128)(2,1)S(1)}, u32[]{:S(2)}, u32[]{:S(2)}) async-start(bf16[8,64,1024]{2,1,0:T(8,128)(2,1)} %unsort_obs.1), calls=%async_computation.1 | async-start | bytes 2097152 | tf_op jit(solution)/shard_map/all_to_all | solution.py:553
  236.6 2.3 collective-permute-start.31
  239.0 2.9 %collective-permute-start.30 = (bf16[64,1536]{1,0:T(8,128)(2,1)S(1)}, bf16[64,1536]{1,0:T(8,128)(2,1)S(1)}, u32[]{:S(2)}, u32[]{:S(2)}) collective-permute-start(bf16[64,1536]{1,0:T(8,128)(2,1)S(1)} %copy-done.44), channel_id=1, source_target_pairs={{0,2},{1,3},{2,0},{3,1},{4,6},{5,7},{6,4},{7,5},{8,10},{9,11},{10,... | collective-permute-start | bytes 589832 | tf_op jit(solution)/shard_map/ppermute | solution.py:490
  241.9 4.4 %collective-permute-done.31.refs_7_ = bf16[64,1536]{1,0:T(8,128)(2,1)S(1)} collective-permute-done((bf16[64,1536]{1,0:T(8,128)(2,1)S(1)}, bf16[64,1536]{1,0:T(8,128)(2,1)S(1)}, u32[]{:S(2)}, u32[]{:S(2)}) %collective-permute-start.31) | collective-permute-done | bytes 196640 | tf_op jit(solution)/shard_map/ppermute | solution.py:490
  246.3 12.1 %collective-permute-done.30.refs_6_ = bf16[64,1536]{1,0:T(8,128)(2,1)S(1)} collective-permute-done((bf16[64,1536]{1,0:T(8,128)(2,1)S(1)}, bf16[64,1536]{1,0:T(8,128)(2,1)S(1)}, u32[]{:S(2)}, u32[]{:S(2)}) %collective-permute-start.30) | collective-permute-done | bytes 196640 | tf_op jit(solution)/shard_map/ppermute | solution.py:490
  259.0 0.7 copy-done.33
  259.7 3.7 %join_rows.1 = bf16[64,8,1440]{2,1,0:T(8,128)(2,1)} custom-call(s32[1]{0:T(128)} %bitcast.place_ref, bf16[64,1536]{1,0:T(8,128)(2,1)} %get-tuple-element.111.refs_0_, bf16[64,1536]{1,0:T(8,128)(2,1)} %copy-done.25, bf16[64,1536]{1,0:T(8,128)(2,1)} %copy-done.26, bf16[64,1536]{1,0:T(8,128)(2,1)} %copy-done.27, bf16[64,1536]{1,0:T(8,128)(2,1)} %get-tuple-element.128.refs_4_, ...), custom_call_target="tpu_custom_call" | custom-call | flops 1000 | bytes 1000 | tf_op jit(solution)/shard_map/join_rows/pallas_call | solution.py:97
  263.4 1.0 copy-done.2
  264.4 3.4 %unpack_obs.1 = f32[512,1024]{1,0:T(8,128)} custom-call(bf16[8,64,1024]{2,1,0:T(8,128)(2,1)} %copy-done.2), custom_call_target="tpu_custom_call" | custom-call | flops 1000 | bytes 1000 | tf_op jit(solution)/shard_map/unpack_obs/pallas_call | solution.py:301
  (123 shorter events, 3.7 us)
Async XLA Ops:
  0.6 3.2 %copy-start.34 = (bf16[4,1,8,1024]{3,2,1,0:T(8,128)(2,1)S(1)}, bf16[4,1,8,1024]{3,2,1,0:T(8,128)(2,1)}, u32[]{:S(2)}) copy-start(bf16[4,1,8,1024]{3,2,1,0:T(8,128)(2,1)} %param.11) | copy-start | bytes 196612
  0.6 3.9 %copy-start.35 = (s32[1,8,1024]{2,1,0:T(8,128)S(1)}, s32[1,8,1024]{2,1,0:T(8,128)}, u32[]{:S(2)}) copy-start(s32[1,8,1024]{2,1,0:T(8,128)} %param.12) | copy-start | bytes 98308
  8.7 5.3 %copy-start.48 = (bf16[64,1536]{1,0:T(8,128)(2,1)S(1)}, bf16[64,1536]{1,0:T(8,128)(2,1)}, u32[]{:S(2)}) copy-start(bf16[64,1536]{1,0:T(8,128)(2,1)} %get-tuple-element.74) | copy-start | bytes 589828
  8.7 8.0 %copy-start.47 = (bf16[64,1536]{1,0:T(8,128)(2,1)S(1)}, bf16[64,1536]{1,0:T(8,128)(2,1)}, u32[]{:S(2)}) copy-start(bf16[64,1536]{1,0:T(8,128)(2,1)} %get-tuple-element.75) | copy-start | bytes 589828
  8.7 9.4 %copy-start.46 = (bf16[64,1536]{1,0:T(8,128)(2,1)S(1)}, bf16[64,1536]{1,0:T(8,128)(2,1)}, u32[]{:S(2)}) copy-start(bf16[64,1536]{1,0:T(8,128)(2,1)} %get-tuple-element.73) | copy-start | bytes 589828
  8.7 26.3 %all-to-all-start = ((bf16[8,80,1024]{2,1,0:T(8,128)(2,1)}), bf16[8,80,1024]{2,1,0:T(8,128)(2,1)S(1)}, u32[]{:S(2)}, u32[]{:S(2)}) async-start(bf16[8,80,1024]{2,1,0:T(8,128)(2,1)} %pack_obs.1), calls=%async_computation | async-start | bytes 2621440 | tf_op jit(solution)/shard_map/all_to_all | solution.py:540
  14.0 23.6 %copy-start.41 = (bf16[64,1536]{1,0:T(8,128)(2,1)S(1)}, bf16[64,1536]{1,0:T(8,128)(2,1)}, u32[]{:S(2)}) copy-start(bf16[64,1536]{1,0:T(8,128)(2,1)} %get-tuple-element.87) | copy-start | bytes 589828
  14.0 30.5 %copy-start.39 = (bf16[64,1536]{1,0:T(8,128)(2,1)S(1)}, bf16[64,1536]{1,0:T(8,128)(2,1)}, u32[]{:S(2)}) copy-start(bf16[64,1536]{1,0:T(8,128)(2,1)} %get-tuple-element.89) | copy-start | bytes 589828
  14.1 30.9 %copy-start.37 = (bf16[64,1536]{1,0:T(8,128)(2,1)S(1)}, bf16[64,1536]{1,0:T(8,128)(2,1)}, u32[]{:S(2)}) copy-start(bf16[64,1536]{1,0:T(8,128)(2,1)} %get-tuple-element.85) | copy-start | bytes 589828
  14.1 17.1 %collective-permute-start.1 = (bf16[64,1536]{1,0:T(8,128)(2,1)S(1)}, bf16[64,1536]{1,0:T(8,128)(2,1)S(1)}, u32[]{:S(2)}, u32[]{:S(2)}) collective-permute-start(bf16[64,1536]{1,0:T(8,128)(2,1)S(1)} %copy-done.48), channel_id=1, source_target_pairs={{0,2},{1,3},{2,0},{3,1},{4,6},{5,7},{6,4},{7,5},{8,10},{9,11},{10,... | collective-permute-start | bytes 589832 | tf_op jit(solution)/shard_map/ppermute | solution.py:490
  16.7 14.5 %collective-permute-start.2 = (bf16[64,1536]{1,0:T(8,128)(2,1)S(1)}, bf16[64,1536]{1,0:T(8,128)(2,1)S(1)}, u32[]{:S(2)}, u32[]{:S(2)}) collective-permute-start(bf16[64,1536]{1,0:T(8,128)(2,1)S(1)} %copy-done.47), channel_id=1, source_target_pairs={{0,3},{1,2},{2,1},{3,0},{4,7},{5,6},{6,5},{7,4},{8,11},{9,10},{10,... | collective-permute-start | bytes 589832 | tf_op jit(solution)/shard_map/ppermute | solution.py:490
  18.1 14.1 %collective-permute-start = (bf16[64,1536]{1,0:T(8,128)(2,1)S(1)}, bf16[64,1536]{1,0:T(8,128)(2,1)S(1)}, u32[]{:S(2)}, u32[]{:S(2)}) collective-permute-start(bf16[64,1536]{1,0:T(8,128)(2,1)S(1)} %copy-done.46), channel_id=1, source_target_pairs={{0,1},{1,0},{2,3},{3,2},{4,5},{5,4},{6,7},{7,6},{8,9},{9,8},{10,11... | collective-permute-start | bytes 589832 | tf_op jit(solution)/shard_map/ppermute | solution.py:490
  35.0 10.2 %copy-start = (bf16[8,80,1024]{2,1,0:T(8,128)(2,1)}, bf16[8,80,1024]{2,1,0:T(8,128)(2,1)S(1)}, u32[]{:S(2)}) copy-start(bf16[8,80,1024]{2,1,0:T(8,128)(2,1)S(1)} %all-to-all-done.obs_ref) | copy-start | bytes 3932164
  35.0 27.7 %collective-permute-start.6 = (bf16[256,1536]{1,0:T(8,128)(2,1)}, bf16[256,1536]{1,0:T(8,128)(2,1)S(1)}, u32[]{:S(2)}, u32[]{:S(2)}) collective-permute-start(bf16[256,1536]{1,0:T(8,128)(2,1)} %assemble.4.here_ref), channel_id=1, source_target_pairs={{0,4},{4,8},{8,12},{12,16},{16,20},{20,24},{24,28},{1,5},{5,9},{9,... | collective-permute-start | bytes 2359304 | tf_op jit(solution)/shard_map/ppermute | solution.py:515
  36.3 26.4 %collective-permute-start.7 = (bf16[256,1536]{1,0:T(8,128)(2,1)}, bf16[256,1536]{1,0:T(8,128)(2,1)S(1)}, u32[]{:S(2)}, u32[]{:S(2)}) collective-permute-start(bf16[256,1536]{1,0:T(8,128)(2,1)} %assemble.4.here_ref), channel_id=1, source_target_pairs={{4,0},{8,4},{12,8},{16,12},{20,16},{24,20},{28,24},{5,1},{9,5},{13... | collective-permute-start | bytes 2359304 | tf_op jit(solution)/shard_map/ppermute | solution.py:515
  37.6 20.6 %collective-permute-start.4 = (bf16[64,1536]{1,0:T(8,128)(2,1)S(1)}, bf16[64,1536]{1,0:T(8,128)(2,1)S(1)}, u32[]{:S(2)}, u32[]{:S(2)}) collective-permute-start(bf16[64,1536]{1,0:T(8,128)(2,1)S(1)} %copy-done.41), channel_id=1, source_target_pairs={{0,2},{1,3},{2,0},{3,1},{4,6},{5,7},{6,4},{7,5},{8,10},{9,11},{10,... | collective-permute-start | bytes 589832 | tf_op jit(solution)/shard_map/ppermute | solution.py:490
  44.5 13.7 %collective-permute-start.5 = (bf16[64,1536]{1,0:T(8,128)(2,1)S(1)}, bf16[64,1536]{1,0:T(8,128)(2,1)S(1)}, u32[]{:S(2)}, u32[]{:S(2)}) collective-permute-start(bf16[64,1536]{1,0:T(8,128)(2,1)S(1)} %copy-done.39), channel_id=1, source_target_pairs={{0,3},{1,2},{2,1},{3,0},{4,7},{5,6},{6,5},{7,4},{8,11},{9,10},{10,... | collective-permute-start | bytes 589832 | tf_op jit(solution)/shard_map/ppermute | solution.py:490
  45.0 14.9 %collective-permute-start.3 = (bf16[64,1536]{1,0:T(8,128)(2,1)S(1)}, bf16[64,1536]{1,0:T(8,128)(2,1)S(1)}, u32[]{:S(2)}, u32[]{:S(2)}) collective-permute-start(bf16[64,1536]{1,0:T(8,128)(2,1)S(1)} %copy-done.37), channel_id=1, source_target_pairs={{0,1},{1,0},{2,3},{3,2},{4,5},{5,4},{6,7},{7,6},{8,9},{9,8},{10,11... | collective-permute-start | bytes 589832 | tf_op jit(solution)/shard_map/ppermute | solution.py:490
  62.7 4.3 %copy-start.4 = (bf16[256,1536]{1,0:T(8,128)(2,1)}, bf16[256,1536]{1,0:T(8,128)(2,1)S(1)}, u32[]{:S(2)}) copy-start(bf16[256,1536]{1,0:T(8,128)(2,1)S(1)} %collective-permute-done.6.below_ref) | copy-start | bytes 2359300
  62.7 4.3 %copy-start.6 = (bf16[256,1536]{1,0:T(8,128)(2,1)}, bf16[256,1536]{1,0:T(8,128)(2,1)S(1)}, u32[]{:S(2)}) copy-start(bf16[256,1536]{1,0:T(8,128)(2,1)S(1)} %collective-permute-done.7.above_ref) | copy-start | bytes 2359300
  62.7 15.5 %collective-permute-start.8 = (bf16[256,1536]{1,0:T(8,128)(2,1)}, bf16[256,1536]{1,0:T(8,128)(2,1)S(1)}, u32[]{:S(2)}, u32[]{:S(2)}) collective-permute-start(bf16[256,1536]{1,0:T(8,128)(2,1)} %assemble.5.here_ref), channel_id=1, source_target_pairs={{0,4},{4,8},{8,12},{12,16},{16,20},{20,24},{24,28},{1,5},{5,9},{9,... | collective-permute-start | bytes 2359304 | tf_op jit(solution)/shard_map/ppermute | solution.py:515
  65.6 12.7 %collective-permute-start.9 = (bf16[256,1536]{1,0:T(8,128)(2,1)}, bf16[256,1536]{1,0:T(8,128)(2,1)S(1)}, u32[]{:S(2)}, u32[]{:S(2)}) collective-permute-start(bf16[256,1536]{1,0:T(8,128)(2,1)} %assemble.5.here_ref), channel_id=1, source_target_pairs={{4,0},{8,4},{12,8},{16,12},{20,16},{24,20},{28,24},{5,1},{9,5},{13... | collective-permute-start | bytes 2359304 | tf_op jit(solution)/shard_map/ppermute | solution.py:515
  73.5 13.0 %collective-permute-start.12 = (bf16[64,1536]{1,0:T(8,128)(2,1)}, bf16[64,1536]{1,0:T(8,128)(2,1)S(1)}, u32[]{:S(2)}, u32[]{:S(2)}) collective-permute-start(bf16[64,1536]{1,0:T(8,128)(2,1)} %get-tuple-element.100), channel_id=1, source_target_pairs={{0,3},{1,2},{2,1},{3,0},{4,7},{5,6},{6,5},{7,4},{8,11},{9,10},{10,... | collective-permute-start | bytes 589832 | tf_op jit(solution)/shard_map/ppermute | solution.py:490
  76.7 21.3 %collective-permute-start.11 = (bf16[64,1536]{1,0:T(8,128)(2,1)}, bf16[64,1536]{1,0:T(8,128)(2,1)S(1)}, u32[]{:S(2)}, u32[]{:S(2)}) collective-permute-start(bf16[64,1536]{1,0:T(8,128)(2,1)} %get-tuple-element.99), channel_id=1, source_target_pairs={{0,2},{1,3},{2,0},{3,1},{4,6},{5,7},{6,4},{7,5},{8,10},{9,11},{10,... | collective-permute-start | bytes 589832 | tf_op jit(solution)/shard_map/ppermute | solution.py:490
  78.2 19.7 %collective-permute-start.10 = (bf16[64,1536]{1,0:T(8,128)(2,1)}, bf16[64,1536]{1,0:T(8,128)(2,1)S(1)}, u32[]{:S(2)}, u32[]{:S(2)}) collective-permute-start(bf16[64,1536]{1,0:T(8,128)(2,1)} %get-tuple-element.98), channel_id=1, source_target_pairs={{0,1},{1,0},{2,3},{3,2},{4,5},{5,4},{6,7},{7,6},{8,9},{9,8},{10,11... | collective-permute-start | bytes 589832 | tf_op jit(solution)/shard_map/ppermute | solution.py:490
  78.3 22.2 %copy-start.36 = (f32[64]{0:T(128)S(1)}, f32[64]{0:T(128)}, u32[]{:S(2)}) copy-start(f32[64]{0:T(128)} %param.9) | copy-start | bytes 772
  86.5 27.7 %copy-start.22 = (bf16[64,1536]{1,0:T(8,128)(2,1)}, bf16[64,1536]{1,0:T(8,128)(2,1)S(1)}, u32[]{:S(2)}) copy-start(bf16[64,1536]{1,0:T(8,128)(2,1)S(1)} %collective-permute-done.12.refs_10_) | copy-start | bytes 589828
  86.5 27.7 %collective-permute-start.15 = (bf16[64,1536]{1,0:T(8,128)(2,1)}, bf16[64,1536]{1,0:T(8,128)(2,1)S(1)}, u32[]{:S(2)}, u32[]{:S(2)}) collective-permute-start(bf16[64,1536]{1,0:T(8,128)(2,1)} %get-tuple-element.106), channel_id=1, source_target_pairs={{0,3},{1,2},{2,1},{3,0},{4,7},{5,6},{6,5},{7,4},{8,11},{9,10},{10,... | collective-permute-start | bytes 589832 | tf_op jit(solution)/shard_map/ppermute | solution.py:490
  98.0 16.3 %copy-start.23 = (bf16[64,1536]{1,0:T(8,128)(2,1)}, bf16[64,1536]{1,0:T(8,128)(2,1)S(1)}, u32[]{:S(2)}) copy-start(bf16[64,1536]{1,0:T(8,128)(2,1)S(1)} %collective-permute-done.11.refs_9_) | copy-start | bytes 589828
  98.0 16.2 %collective-permute-start.14 = (bf16[64,1536]{1,0:T(8,128)(2,1)}, bf16[64,1536]{1,0:T(8,128)(2,1)S(1)}, u32[]{:S(2)}, u32[]{:S(2)}) collective-permute-start(bf16[64,1536]{1,0:T(8,128)(2,1)} %get-tuple-element.104), channel_id=1, source_target_pairs={{0,2},{1,3},{2,0},{3,1},{4,6},{5,7},{6,4},{7,5},{8,10},{9,11},{10,... | collective-permute-start | bytes 589832 | tf_op jit(solution)/shard_map/ppermute | solution.py:490
  98.0 16.3 %copy-start.24 = (bf16[64,1536]{1,0:T(8,128)(2,1)}, bf16[64,1536]{1,0:T(8,128)(2,1)S(1)}, u32[]{:S(2)}) copy-start(bf16[64,1536]{1,0:T(8,128)(2,1)S(1)} %collective-permute-done.10.refs_8_) | copy-start | bytes 589828
  98.0 16.2 %collective-permute-start.13 = (bf16[64,1536]{1,0:T(8,128)(2,1)}, bf16[64,1536]{1,0:T(8,128)(2,1)S(1)}, u32[]{:S(2)}, u32[]{:S(2)}) collective-permute-start(bf16[64,1536]{1,0:T(8,128)(2,1)} %get-tuple-element.102), channel_id=1, source_target_pairs={{0,1},{1,0},{2,3},{3,2},{4,5},{5,4},{6,7},{7,6},{8,9},{9,8},{10,11... | collective-permute-start | bytes 589832 | tf_op jit(solution)/shard_map/ppermute | solution.py:490
  150.4 26.4 %copy-start.42 = (bf16[64,1536]{1,0:T(8,128)(2,1)S(1)}, bf16[64,1536]{1,0:T(8,128)(2,1)}, u32[]{:S(2)}) copy-start(bf16[64,1536]{1,0:T(8,128)(2,1)} %get-tuple-element.125) | copy-start | bytes 589828
  150.4 28.6 %copy-start.40 = (bf16[64,1536]{1,0:T(8,128)(2,1)S(1)}, bf16[64,1536]{1,0:T(8,128)(2,1)}, u32[]{:S(2)}) copy-start(bf16[64,1536]{1,0:T(8,128)(2,1)} %get-tuple-element.123) | copy-start | bytes 589828
  150.4 28.5 %copy-start.38 = (bf16[64,1536]{1,0:T(8,128)(2,1)S(1)}, bf16[64,1536]{1,0:T(8,128)(2,1)}, u32[]{:S(2)}) copy-start(bf16[64,1536]{1,0:T(8,128)(2,1)} %get-tuple-element.121) | copy-start | bytes 589828
  150.4 10.0 %collective-permute-start.18 = (bf16[64,1536]{1,0:T(8,128)(2,1)}, bf16[64,1536]{1,0:T(8,128)(2,1)S(1)}, u32[]{:S(2)}, u32[]{:S(2)}) collective-permute-start(bf16[64,1536]{1,0:T(8,128)(2,1)} %get-tuple-element.110), channel_id=1, source_target_pairs={{0,3},{1,2},{2,1},{3,0},{4,7},{5,6},{6,5},{7,4},{8,11},{9,10},{10,... | collective-permute-start | bytes 589832 | tf_op jit(solution)/shard_map/ppermute | solution.py:490
  152.4 17.8 %collective-permute-start.17 = (bf16[64,1536]{1,0:T(8,128)(2,1)}, bf16[64,1536]{1,0:T(8,128)(2,1)S(1)}, u32[]{:S(2)}, u32[]{:S(2)}) collective-permute-start(bf16[64,1536]{1,0:T(8,128)(2,1)} %get-tuple-element.109), channel_id=1, source_target_pairs={{0,2},{1,3},{2,0},{3,1},{4,6},{5,7},{6,4},{7,5},{8,10},{9,11},{10,... | collective-permute-start | bytes 589832 | tf_op jit(solution)/shard_map/ppermute | solution.py:490
  152.4 17.8 %collective-permute-start.16 = (bf16[64,1536]{1,0:T(8,128)(2,1)}, bf16[64,1536]{1,0:T(8,128)(2,1)S(1)}, u32[]{:S(2)}, u32[]{:S(2)}) collective-permute-start(bf16[64,1536]{1,0:T(8,128)(2,1)} %get-tuple-element.108), channel_id=1, source_target_pairs={{0,1},{1,0},{2,3},{3,2},{4,5},{5,4},{6,7},{7,6},{8,9},{9,8},{10,11... | collective-permute-start | bytes 589832 | tf_op jit(solution)/shard_map/ppermute | solution.py:490
  160.4 9.9 %copy-start.16 = (bf16[64,1536]{1,0:T(8,128)(2,1)}, bf16[64,1536]{1,0:T(8,128)(2,1)S(1)}, u32[]{:S(2)}) copy-start(bf16[64,1536]{1,0:T(8,128)(2,1)S(1)} %collective-permute-done.18.refs_3_) | copy-start | bytes 589828
  173.2 25.3 %collective-permute-start.19 = (bf16[256,1536]{1,0:T(8,128)(2,1)}, bf16[256,1536]{1,0:T(8,128)(2,1)S(1)}, u32[]{:S(2)}, u32[]{:S(2)}) collective-permute-start(bf16[256,1536]{1,0:T(8,128)(2,1)} %assemble.6.here_ref), channel_id=1, source_target_pairs={{0,4},{4,8},{8,12},{12,16},{16,20},{20,24},{24,28},{1,5},{5,9},{9,... | collective-permute-start | bytes 2359304 | tf_op jit(solution)/shard_map/ppermute | solution.py:515
  175.2 23.2 %collective-permute-start.20 = (bf16[256,1536]{1,0:T(8,128)(2,1)}, bf16[256,1536]{1,0:T(8,128)(2,1)S(1)}, u32[]{:S(2)}, u32[]{:S(2)}) collective-permute-start(bf16[256,1536]{1,0:T(8,128)(2,1)} %assemble.6.here_ref), channel_id=1, source_target_pairs={{4,0},{8,4},{12,8},{16,12},{20,16},{24,20},{28,24},{5,1},{9,5},{13... | collective-permute-start | bytes 2359304 | tf_op jit(solution)/shard_map/ppermute | solution.py:515
  176.8 16.5 %collective-permute-start.26 = (bf16[64,1536]{1,0:T(8,128)(2,1)S(1)}, bf16[64,1536]{1,0:T(8,128)(2,1)S(1)}, u32[]{:S(2)}, u32[]{:S(2)}) collective-permute-start(bf16[64,1536]{1,0:T(8,128)(2,1)S(1)} %copy-done.42), channel_id=1, source_target_pairs={{0,3},{1,2},{2,1},{3,0},{4,7},{5,6},{6,5},{7,4},{8,11},{9,10},{10,... | collective-permute-start | bytes 589832 | tf_op jit(solution)/shard_map/ppermute | solution.py:490
  178.9 16.0 %collective-permute-start.25 = (bf16[64,1536]{1,0:T(8,128)(2,1)S(1)}, bf16[64,1536]{1,0:T(8,128)(2,1)S(1)}, u32[]{:S(2)}, u32[]{:S(2)}) collective-permute-start(bf16[64,1536]{1,0:T(8,128)(2,1)S(1)} %copy-done.40), channel_id=1, source_target_pairs={{0,2},{1,3},{2,0},{3,1},{4,6},{5,7},{6,4},{7,5},{8,10},{9,11},{10,... | collective-permute-start | bytes 589832 | tf_op jit(solution)/shard_map/ppermute | solution.py:490
  179.0 16.0 %collective-permute-start.24 = (bf16[64,1536]{1,0:T(8,128)(2,1)S(1)}, bf16[64,1536]{1,0:T(8,128)(2,1)S(1)}, u32[]{:S(2)}, u32[]{:S(2)}) collective-permute-start(bf16[64,1536]{1,0:T(8,128)(2,1)S(1)} %copy-done.38), channel_id=1, source_target_pairs={{0,1},{1,0},{2,3},{3,2},{4,5},{5,4},{6,7},{7,6},{8,9},{9,8},{10,11... | collective-permute-start | bytes 589832 | tf_op jit(solution)/shard_map/ppermute | solution.py:490
  193.2 10.6 %copy-start.1 = (bf16[3,3,256,256]{3,2,1,0:T(8,128)(2,1)S(1)}, bf16[3,3,256,256]{3,2,1,0:T(8,128)(2,1)}, u32[]{:S(2)}) copy-start(bf16[3,3,256,256]{3,2,1,0:T(8,128)(2,1)} %param.8) | copy-start | bytes 3538948
  193.2 1.7 copy-start.11
  198.4 7.1 %copy-start.3 = (bf16[256,1536]{1,0:T(8,128)(2,1)}, bf16[256,1536]{1,0:T(8,128)(2,1)S(1)}, u32[]{:S(2)}) copy-start(bf16[256,1536]{1,0:T(8,128)(2,1)S(1)} %collective-permute-done.19.below_ref) | copy-start | bytes 2359300
  198.4 7.1 %copy-start.5 = (bf16[256,1536]{1,0:T(8,128)(2,1)}, bf16[256,1536]{1,0:T(8,128)(2,1)S(1)}, u32[]{:S(2)}) copy-start(bf16[256,1536]{1,0:T(8,128)(2,1)S(1)} %collective-permute-done.20.above_ref) | copy-start | bytes 2359300
  198.4 18.0 %collective-permute-start.27 = (bf16[256,1536]{1,0:T(8,128)(2,1)}, bf16[256,1536]{1,0:T(8,128)(2,1)S(1)}, u32[]{:S(2)}, u32[]{:S(2)}) collective-permute-start(bf16[256,1536]{1,0:T(8,128)(2,1)} %assemble.7.here_ref), channel_id=1, source_target_pairs={{0,4},{4,8},{8,12},{12,16},{16,20},{20,24},{24,28},{1,5},{5,9},{9,... | collective-permute-start | bytes 2359304 | tf_op jit(solution)/shard_map/ppermute | solution.py:515
  202.6 13.8 %collective-permute-start.28 = (bf16[256,1536]{1,0:T(8,128)(2,1)}, bf16[256,1536]{1,0:T(8,128)(2,1)}, u32[]{:S(2)}, u32[]{:S(2)}) collective-permute-start(bf16[256,1536]{1,0:T(8,128)(2,1)} %assemble.7.here_ref), channel_id=1, source_target_pairs={{4,0},{8,4},{12,8},{16,12},{20,16},{24,20},{28,24},{5,1},{9,5},{13... | collective-permute-start | bytes 2359304 | tf_op jit(solution)/shard_map/ppermute | solution.py:515
  212.0 11.8 %collective-permute-start.21 = (bf16[64,1536]{1,0:T(8,128)(2,1)}, bf16[64,1536]{1,0:T(8,128)(2,1)S(1)}, u32[]{:S(2)}, u32[]{:S(2)}) collective-permute-start(bf16[64,1536]{1,0:T(8,128)(2,1)} %get-tuple-element.112), channel_id=1, source_target_pairs={{0,1},{1,0},{2,3},{3,2},{4,5},{5,4},{6,7},{7,6},{8,9},{9,8},{10,11... | collective-permute-start | bytes 589832 | tf_op jit(solution)/shard_map/ppermute | solution.py:490
  212.3 11.5 %collective-permute-start.22 = (bf16[64,1536]{1,0:T(8,128)(2,1)}, bf16[64,1536]{1,0:T(8,128)(2,1)S(1)}, u32[]{:S(2)}, u32[]{:S(2)}) collective-permute-start(bf16[64,1536]{1,0:T(8,128)(2,1)} %get-tuple-element.113), channel_id=1, source_target_pairs={{0,2},{1,3},{2,0},{3,1},{4,6},{5,7},{6,4},{7,5},{8,10},{9,11},{10,... | collective-permute-start | bytes 589832 | tf_op jit(solution)/shard_map/ppermute | solution.py:490
  214.4 11.1 %collective-permute-start.23 = (bf16[64,1536]{1,0:T(8,128)(2,1)}, bf16[64,1536]{1,0:T(8,128)(2,1)S(1)}, u32[]{:S(2)}, u32[]{:S(2)}) collective-permute-start(bf16[64,1536]{1,0:T(8,128)(2,1)} %get-tuple-element.114), channel_id=1, source_target_pairs={{0,3},{1,2},{2,1},{3,0},{4,7},{5,6},{6,5},{7,4},{8,11},{9,10},{10,... | collective-permute-start | bytes 589832 | tf_op jit(solution)/shard_map/ppermute | solution.py:490
  223.7 12.9 %copy-start.45 = (bf16[64,1536]{1,0:T(8,128)(2,1)S(1)}, bf16[64,1536]{1,0:T(8,128)(2,1)}, u32[]{:S(2)}) copy-start(bf16[64,1536]{1,0:T(8,128)(2,1)} %get-tuple-element.134) | copy-start | bytes 589828
  223.8 15.2 %copy-start.44 = (bf16[64,1536]{1,0:T(8,128)(2,1)S(1)}, bf16[64,1536]{1,0:T(8,128)(2,1)}, u32[]{:S(2)}) copy-start(bf16[64,1536]{1,0:T(8,128)(2,1)} %get-tuple-element.132) | copy-start | bytes 589828
  223.8 18.1 %copy-start.43 = (bf16[64,1536]{1,0:T(8,128)(2,1)S(1)}, bf16[64,1536]{1,0:T(8,128)(2,1)}, u32[]{:S(2)}) copy-start(bf16[64,1536]{1,0:T(8,128)(2,1)} %get-tuple-element.130) | copy-start | bytes 589828
  223.8 34.6 %copy-start.25 = (bf16[64,1536]{1,0:T(8,128)(2,1)}, bf16[64,1536]{1,0:T(8,128)(2,1)S(1)}, u32[]{:S(2)}) copy-start(bf16[64,1536]{1,0:T(8,128)(2,1)S(1)} %collective-permute-done.21.refs_1_) | copy-start | bytes 589828
  223.8 34.6 %copy-start.26 = (bf16[64,1536]{1,0:T(8,128)(2,1)}, bf16[64,1536]{1,0:T(8,128)(2,1)S(1)}, u32[]{:S(2)}) copy-start(bf16[64,1536]{1,0:T(8,128)(2,1)S(1)} %collective-permute-done.22.refs_2_) | copy-start | bytes 589828
  225.5 32.9 %copy-start.27 = (bf16[64,1536]{1,0:T(8,128)(2,1)}, bf16[64,1536]{1,0:T(8,128)(2,1)S(1)}, u32[]{:S(2)}) copy-start(bf16[64,1536]{1,0:T(8,128)(2,1)S(1)} %collective-permute-done.23.refs_3_) | copy-start | bytes 589828
  225.5 37.9 %all-to-all-start.1 = ((bf16[8,64,1024]{2,1,0:T(8,128)(2,1)}), bf16[8,64,1024]{2,1,0:T(8,128)(2,1)S(1)}, u32[]{:S(2)}, u32[]{:S(2)}) async-start(bf16[8,64,1024]{2,1,0:T(8,128)(2,1)} %unsort_obs.1), calls=%async_computation.1 | async-start | bytes 2097152 | tf_op jit(solution)/shard_map/all_to_all | solution.py:553
  236.6 9.7 %collective-permute-start.31 = (bf16[64,1536]{1,0:T(8,128)(2,1)S(1)}, bf16[64,1536]{1,0:T(8,128)(2,1)S(1)}, u32[]{:S(2)}, u32[]{:S(2)}) collective-permute-start(bf16[64,1536]{1,0:T(8,128)(2,1)S(1)} %copy-done.45), channel_id=1, source_target_pairs={{0,3},{1,2},{2,1},{3,0},{4,7},{5,6},{6,5},{7,4},{8,11},{9,10},{10,... | collective-permute-start | bytes 589832 | tf_op jit(solution)/shard_map/ppermute | solution.py:490
  239.0 19.4 %collective-permute-start.30 = (bf16[64,1536]{1,0:T(8,128)(2,1)S(1)}, bf16[64,1536]{1,0:T(8,128)(2,1)S(1)}, u32[]{:S(2)}, u32[]{:S(2)}) collective-permute-start(bf16[64,1536]{1,0:T(8,128)(2,1)S(1)} %copy-done.44), channel_id=1, source_target_pairs={{0,2},{1,3},{2,0},{3,1},{4,6},{5,7},{6,4},{7,5},{8,10},{9,11},{10,... | collective-permute-start | bytes 589832 | tf_op jit(solution)/shard_map/ppermute | solution.py:490
  241.8 16.5 %collective-permute-start.29 = (bf16[64,1536]{1,0:T(8,128)(2,1)S(1)}, bf16[64,1536]{1,0:T(8,128)(2,1)S(1)}, u32[]{:S(2)}, u32[]{:S(2)}) collective-permute-start(bf16[64,1536]{1,0:T(8,128)(2,1)S(1)} %copy-done.43), channel_id=1, source_target_pairs={{0,1},{1,0},{2,3},{3,2},{4,5},{5,4},{6,7},{7,6},{8,9},{9,8},{10,11... | collective-permute-start | bytes 589832 | tf_op jit(solution)/shard_map/ppermute | solution.py:490
  246.3 12.1 %copy-start.31 = (bf16[64,1536]{1,0:T(8,128)(2,1)}, bf16[64,1536]{1,0:T(8,128)(2,1)S(1)}, u32[]{:S(2)}) copy-start(bf16[64,1536]{1,0:T(8,128)(2,1)S(1)} %collective-permute-done.31.refs_7_) | copy-start | bytes 589828
  (19 other events, 16.4 us)

commit v3 on v2

v3 whole, which is shorter than its diff:
```python
import functools

import jax
import jax.numpy as jnp
from jax import lax
from jax.experimental import pallas as pl
from jax.experimental.pallas import tpu as pltpu
from jax.sharding import PartitionSpec as P

SPACING = 8
LANES = 128
STEP = 120
TOGETHER = 4
WINDOW = 12
OBS = 256
SIDE = 16
JOIN = 2

VMEM = pl.BlockSpec(memory_space=pltpu.VMEM)
SMEM = pl.BlockSpec(memory_space=pltpu.SMEM)
CONV = pl.CostEstimate(flops=7 * 10**9, bytes_accessed=1000, transcendentals=0)
SMALL = pl.CostEstimate(flops=1000, bytes_accessed=1000, transcendentals=0)
PARAMS = pltpu.CompilerParams(vmem_limit_bytes=56 * 1024 * 1024)


def padded_width(width):
    return -(-(width + 3 * SPACING) // LANES) * LANES


def lane_iota(shape):
    return lax.broadcasted_iota(jnp.int32, shape, len(shape) - 1)


def wrapped_tail(first, tail, rem):
    lane = lane_iota(tail.shape)
    head = pltpu.roll(first, rem, 1)
    end = pltpu.roll(tail, LANES - rem, 1)
    out = jnp.where(lane < rem, tail, jnp.where(lane < rem + 2 * SPACING, head, 0.0))
    return jnp.where(lane >= LANES - SPACING, end, out)


def split_rows_kernel(parts, place_ref, state_ref, *refs):
    outs, rows_ref = refs[:-1], refs[-1]
    group, rows, width = state_ref.shape
    wide = outs[0].shape[1]
    main = width // LANES * LANES
    rem = width - main
    tiles = wide // LANES
    for tile in range(tiles):
        size = min(LANES, width - tile * LANES)
        part = state_ref[:, :, tile * LANES:tile * LANES + size].astype(jnp.float32)
        rows_ref[tile, :, :size] = part.reshape(group * rows, size)
    for number in range(rows):
        if number < parts:
            out, row = outs[number], place_ref[0] ^ number
        else:
            out, row = outs[parts - 1 + number // parts].at[number % parts * group:(number % parts + 1) * group], number
        strips = [rows_ref[tile, pl.ds(row, group, stride=rows), :] for tile in range(tiles)]
        for tile in range(tiles - 1):
            out[:, tile * LANES:(tile + 1) * LANES] = strips[tile].astype(jnp.bfloat16)
        out[:, main:] = wrapped_tail(strips[0], strips[-1], rem).astype(jnp.bfloat16)


def split_rows(place, state, parts, wide):
    group, rows, width = state.shape
    later = rows // parts - 1
    results = pl.pallas_call(
        functools.partial(split_rows_kernel, parts),
        out_shape=[jax.ShapeDtypeStruct((group, wide), jnp.bfloat16)] * parts
        + [jax.ShapeDtypeStruct((parts * group, wide), jnp.bfloat16)] * later,
        in_specs=[SMEM, VMEM],
        out_specs=[VMEM] * (parts + later),
        scratch_shapes=[pltpu.VMEM((wide // LANES, group * rows, LANES), jnp.float32)],
        compiler_params=PARAMS,
        cost_estimate=SMALL,
        name="split_rows",
    )(place, state)
    return [results[:parts], *results[parts:]]


def join_rows_kernel(parts, place_ref, *refs):
    pieces, out_ref, rows_ref = refs[:-2], refs[-2], refs[-1]
    group, rows, width = out_ref.shape
    for number in range(rows):
        turn, k = divmod(number, parts)
        if turn and turn == rows // parts - 1:
            piece, row = pieces[turn + k], turn * parts + (place_ref[0] ^ k)
        else:
            piece, row = pieces[turn].at[k * group:(k + 1) * group], number
        for tile in range(rows_ref.shape[0]):
            part = piece[:, tile * LANES:(tile + 1) * LANES].astype(jnp.float32)
            rows_ref[tile, pl.ds(row, group, stride=rows), :] = part
    for tile in range(rows_ref.shape[0]):
        size = min(LANES, width - tile * LANES)
        part = rows_ref[tile, :, :size].reshape(group, rows, size)
        out_ref[:, :, tile * LANES:tile * LANES + size] = part.astype(jnp.bfloat16)


def join_rows(place, blocks, parts, width):
    pieces = [piece for block in blocks for piece in (block if isinstance(block, list) else [block])]
    group, wide = blocks[0].shape[0] // parts, blocks[0].shape[1]
    rows = parts * len(blocks)
    return pl.pallas_call(
        functools.partial(join_rows_kernel, parts),
        out_shape=jax.ShapeDtypeStruct((group, rows, width), jnp.bfloat16),
        in_specs=[SMEM] + [VMEM] * len(pieces),
        out_specs=VMEM,
        scratch_shapes=[pltpu.VMEM((wide // LANES, group * rows, LANES), jnp.float32)],
        compiler_params=PARAMS,
        cost_estimate=SMALL,
        name="join_rows",
    )(place, *pieces)


def assemble_kernel(place_ref, *refs):
    pieces, out_ref = refs[:-1], refs[-1]
    group = pieces[0].shape[0]
    for k, piece in enumerate(pieces):
        start = pl.multiple_of((place_ref[0] ^ k) * group, group)
        out_ref[pl.ds(start, group), :] = piece[...]


def assemble(place, pieces):
    group, wide = pieces[0].shape
    return pl.pallas_call(
        assemble_kernel,
        out_shape=jax.ShapeDtypeStruct((group * len(pieces), wide), jnp.bfloat16),
        in_specs=[SMEM] + [VMEM] * len(pieces),
        out_specs=VMEM,
        compiler_params=PARAMS,
        cost_estimate=SMALL,
        name="assemble",
    )(place, *pieces)


def conv_kernel(place_ref, weights_ref, below_ref, here_ref, above_ref, *refs):
    outs, sums_ref = refs[:-1], refs[-1]
    total, wide = here_ref.shape
    columns = 4 * LANES
    share = total // max(len(outs), 4)

    @pl.loop(0, wide // columns)
    def _(tile):
        at = pl.ds(pl.multiple_of(tile * columns, columns), columns)
        part = jnp.dot(weights_ref[1], here_ref[:, at], preferred_element_type=jnp.float32)
        part += jnp.dot(weights_ref[0], below_ref[:, at], preferred_element_type=jnp.float32)
        part += jnp.dot(weights_ref[2], above_ref[:, at], preferred_element_type=jnp.float32)
        sums_ref[:, at] = part

    for number in range(total // share):
        if len(outs) > 1:
            out, start = outs[number], pl.multiple_of((place_ref[0] ^ number) * share, share)
        else:
            out, start = outs[0].at[number * share:(number + 1) * share], number * share
        left = sums_ref[pl.ds(start, share), :]
        middle = sums_ref[pl.ds(start + total, share), :]
        right = sums_ref[pl.ds(start + 2 * total, share), :]
        mixed = middle + pltpu.roll(left, SPACING, 1) + pltpu.roll(right, wide - SPACING, 1)
        out[...] = mixed.astype(jnp.bfloat16)


def conv(place, weights, below, here, above, parts):
    total, wide = here.shape
    results = pl.pallas_call(
        conv_kernel,
        out_shape=[jax.ShapeDtypeStruct((total // parts, wide), jnp.bfloat16)] * parts,
        in_specs=[SMEM] + [VMEM] * 4,
        out_specs=[VMEM] * parts,
        scratch_shapes=[pltpu.VMEM((3 * total, wide), jnp.float32)],
        compiler_params=PARAMS,
        cost_estimate=CONV,
        name="conv",
    )(place, weights, below, here, above)
    return results if parts > 1 else results[0]


def pack_obs_kernel(width, counts_ref, values_ref, weights_ref, cells_ref, out_ref, tiles_ref):
    slabs, depth, slots = out_ref.shape
    group = depth - SIDE
    blocks = -(-width // STEP)
    for tile in range(slots // LANES):
        tiles_ref[tile] = values_ref[:, tile * LANES:(tile + 1) * LANES]
    for slab in range(slabs):
        used = lane_iota((1, slots)) < counts_ref[0, slab]
        values = jnp.concatenate(
            [tiles_ref[tile, pl.ds(slab, group, stride=slabs), :] for tile in range(slots // LANES)], axis=1
        )
        out_ref[slab, :group, :] = jnp.where(used, values, 0.0).astype(jnp.bfloat16)
        weights = jnp.where(used, weights_ref[slab], 0.0)
        local = (cells_ref[slab] - slab * (SPACING * width)).astype(jnp.float32)
        row = jnp.clip(jnp.floor((local + 0.5) * (1.0 / width)), 0.0, SPACING - 2.0)
        column = local - row * width
        block = jnp.clip(jnp.floor((column + 0.5) * (1.0 / STEP)), 0.0, blocks - 1.0)
        side = jnp.concatenate(
            [weights, row * blocks + block, column - block * STEP, jnp.zeros((SIDE - 6, slots), jnp.float32)],
            axis=0,
        )
        out_ref[slab, group:, :] = side.astype(jnp.bfloat16)


def pack_obs(counts, values, weights, cells, width):
    group, slabs, slots = values.shape
    return pl.pallas_call(
        functools.partial(pack_obs_kernel, width),
        out_shape=jax.ShapeDtypeStruct((slabs, group + SIDE, slots), jnp.bfloat16),
        in_specs=[SMEM, VMEM, VMEM, VMEM],
        out_specs=VMEM,
        scratch_shapes=[pltpu.VMEM((slots // LANES, group * slabs, LANES), jnp.float32)],
        compiler_params=PARAMS,
        cost_estimate=SMALL,
        name="pack_obs",
    )(counts, values.reshape(group * slabs, slots), weights, cells)


def sort_obs_kernel(begin, obs_ref, sorted_ref, rank_ref, first_ref, last_ref, joined_ref, column_ref):
    sets, depth, size = sorted_ref.shape
    group = depth - SIDE
    each = obs_ref.shape[2]
    for s in range(sets):
        for i in range(size // each):
            joined_ref[:, i * each:(i + 1) * each] = obs_ref[begin + s * (size // each) + i]
        which = joined_ref[group:, :].astype(jnp.float32)[4:5]
        key = which * size + lane_iota((1, size)).astype(jnp.float32)
        column_ref[...] = jnp.transpose(jnp.broadcast_to(key, (LANES, size)))
        ranks = []
        for tile in range(size // LANES):
            below = jnp.where(column_ref[...] < key[:, tile * LANES:(tile + 1) * LANES], 1.0, 0.0)
            ranks.append(jnp.sum(below, axis=0, keepdims=True))
        rank = jnp.concatenate(ranks, axis=1)
        rank_ref[s] = rank.astype(jnp.int32)
        column_ref[...] = jnp.transpose(jnp.broadcast_to(rank, (LANES, size)))

        @pl.loop(0, size // OBS)
        def _(tile):
            start = pl.multiple_of(tile * OBS, OBS)
            chosen = []
            for i in range(OBS // LANES):
                order = (lane_iota((1, LANES)) + (start + i * LANES)).astype(jnp.float32)
                chosen.append(jnp.where(column_ref[...] == order, 1.0, 0.0).astype(jnp.bfloat16))
            taken = jnp.dot(
                joined_ref[...], jnp.concatenate(chosen, axis=1), preferred_element_type=jnp.float32
            )
            sorted_ref[s, :, pl.ds(start, OBS)] = taken.astype(jnp.bfloat16)
            which = taken[group + 4:group + 5]
            first_ref[s * (size // OBS) + tile] = jnp.min(which).astype(jnp.int32)
            last_ref[s * (size // OBS) + tile] = jnp.max(which).astype(jnp.int32)


def sort_obs(obs, begin, slabs):
    depth, slots = obs.shape[1:]
    size = slots * JOIN
    sets = slabs // JOIN
    return pl.pallas_call(
        functools.partial(sort_obs_kernel, begin),
        out_shape=[
            jax.ShapeDtypeStruct((sets, depth, size), jnp.bfloat16),
            jax.ShapeDtypeStruct((sets, 1, size), jnp.int32),
            jax.ShapeDtypeStruct((sets * size // OBS,), jnp.int32),
            jax.ShapeDtypeStruct((sets * size // OBS,), jnp.int32),
        ],
        in_specs=[VMEM],
        out_specs=[VMEM, VMEM, SMEM, SMEM],
        scratch_shapes=[pltpu.VMEM((depth, size), jnp.bfloat16), pltpu.VMEM((size, LANES), jnp.float32)],
        compiler_params=PARAMS,
        cost_estimate=SMALL,
        name="sort_obs",
    )(obs)


def unsort_obs_kernel(sorted_ref, one_ref, two_ref, out_ref):
    sets, group, size = sorted_ref.shape
    each = out_ref.shape[2]
    for s in range(sets):
        @pl.loop(0, size // OBS)
        def _(tile):
            start = pl.multiple_of(tile * OBS, OBS)
            rank = (one_ref if s < sets // 2 else two_ref)[s % (sets // 2), :, pl.ds(start, OBS)]
            chosen = jnp.where(lax.broadcasted_iota(jnp.int32, (size, OBS), 0) == rank, 1.0, 0.0)
            taken = jnp.dot(sorted_ref[s], chosen.astype(jnp.bfloat16), preferred_element_type=jnp.float32)
            slab = s * (size // each) + tile // (each // OBS)
            at = pl.ds(pl.multiple_of(tile % (each // OBS) * OBS, OBS), OBS)
            out_ref[slab, :, at] = taken.astype(jnp.bfloat16)


def unsort_obs(values, one, two, slabs):
    sets, group, size = values.shape
    return pl.pallas_call(
        unsort_obs_kernel,
        out_shape=jax.ShapeDtypeStruct((slabs, group, sets * size // slabs), jnp.bfloat16),
        in_specs=[VMEM] * 3,
        out_specs=VMEM,
        compiler_params=PARAMS,
        cost_estimate=SMALL,
        name="unsort_obs",
    )(values, one, two)


def unpack_obs_kernel(values_ref, out_ref, tiles_ref):
    slabs, group, slots = values_ref.shape
    for slab in range(slabs):
        for tile in range(slots // LANES):
            part = values_ref[slab, :, tile * LANES:(tile + 1) * LANES].astype(jnp.float32)
            tiles_ref[tile, pl.ds(slab, group, stride=slabs), :] = part
    for tile in range(slots // LANES):
        out_ref[:, tile * LANES:(tile + 1) * LANES] = tiles_ref[tile]


def unpack_obs(values):
    slabs, group, slots = values.shape
    return pl.pallas_call(
        unpack_obs_kernel,
        out_shape=jax.ShapeDtypeStruct((group * slabs, slots), jnp.float32),
        in_specs=[VMEM],
        out_specs=VMEM,
        scratch_shapes=[pltpu.VMEM((slots // LANES, group * slabs, LANES), jnp.float32)],
        compiler_params=PARAMS,
        cost_estimate=SMALL,
        name="unpack_obs",
    )(values)


def activate_kernel(parts, width, place_ref, bias_ref, *refs):
    pieces, table_ref, slope_ref = refs[:-2], refs[-2], refs[-1]
    blocks = -(-width // STEP)
    group, wide = slope_ref.shape[0] // parts, slope_ref.shape[1]
    lane = lane_iota((group, LANES))
    for k in range(parts):
        row = place_ref[0] ^ k if len(pieces) > 1 else k
        piece = pieces[k] if len(pieces) > 1 else pieces[0].at[k * group:(k + 1) * group]
        rows_at = pl.ds(pl.multiple_of(row * group, group), group)
        hidden = []
        for tile in range(wide // LANES):
            at = slice(tile * LANES, (tile + 1) * LANES)
            value = piece[:, at].astype(jnp.float32) + bias_ref[...]
            half = 0.5 * (1.0 + lax.erf(value * 0.7071067811865476))
            hidden.append(value * half)
            slope_ref[rows_at, at] = half + value * jnp.exp(-0.5 * value * value) * 0.3989422804014327
        for j in range(blocks):
            tile, shift = divmod(j * STEP, LANES)
            block = hidden[tile]
            if shift:
                block = jnp.where(
                    lane < LANES - shift,
                    pltpu.roll(block, LANES - shift, 1),
                    pltpu.roll(hidden[tile + 1], LANES - shift, 1),
                )
            start = pl.multiple_of((row * blocks + j) * group, group)
            table_ref[pl.ds(start, group), :] = block.astype(jnp.bfloat16)


def activate(place, bias, block, parts, width):
    pieces = block if isinstance(block, list) else [block]
    group, wide = bias.shape[0], pieces[0].shape[1]
    blocks = -(-width // STEP)
    return pl.pallas_call(
        functools.partial(activate_kernel, parts, width),
        out_shape=[
            jax.ShapeDtypeStruct((parts * blocks * group, LANES), jnp.bfloat16),
            jax.ShapeDtypeStruct((parts * group, wide), jnp.float32),
        ],
        in_specs=[SMEM] + [VMEM] * (1 + len(pieces)),
        out_specs=[VMEM] * 2,
        compiler_params=PARAMS,
        cost_estimate=SMALL,
        name="activate",
    )(place, bias, *pieces)


def observe_kernel(parts, turns, width, place_ref, *refs):
    rows = parts * turns
    firsts, lasts, halves = refs[0:2], refs[2:4], refs[4:6]
    tables, slopes, refs = refs[6:6 + turns], refs[6 + turns:6 + 2 * turns], refs[6 + 2 * turns:]
    pieces, grads, refs = refs[:parts], refs[parts:parts + turns - 1], refs[parts + turns - 1:]
    departure_ref, table_ref, found_ref, obs_ref, spread_ref, first_ref, arrival = refs
    grads = [first_ref, *grads]
    group, wide = slopes[0].shape[0] // parts, slopes[0].shape[1]
    size = obs_ref.shape[2]
    sets = obs_ref.shape[0] // 2
    blocks = -(-width // STEP)
    tiles = wide // LANES
    rem = width % LANES
    last = width // LANES
    lane = lane_iota((group, LANES))
    slab = blocks * group
    high = WINDOW * group

    copies = [
        pltpu.make_async_copy(half, obs_ref.at[pl.ds(i * sets, sets)], arrival.at[i])
        for i, half in enumerate(halves)
    ]
    for i, table in enumerate(tables):
        for lanes in range(2):
            start = (i * parts + 1 - lanes) * slab
            target = table_ref.at[pl.ds(start, parts * slab), pl.ds(lanes * LANES, LANES)]
            copies.append(pltpu.make_async_copy(table, target, arrival.at[2 + 2 * i + lanes]))
    for copy in copies:
        copy.start()
    for copy in copies:
        copy.wait()

    count = firsts[0].shape[0]
    lo_iota = lax.broadcasted_iota(jnp.int32, (LANES, OBS), 0)
    share = found_ref.shape[0] // (2 * count // TOGETHER)

    def find(number):
        s = number // (size // OBS)
        at = pl.ds(pl.multiple_of(number % (size // OBS) * OBS, OBS), OBS)
        side = obs_ref[s, group:, at].astype(jnp.float32)
        whole = jnp.broadcast_to(side[4:5].astype(jnp.int32), (8, OBS))
        here, there = jnp.minimum(number, count - 1), jnp.maximum(number - count, 0)
        lowest = jnp.where(number < count, firsts[0][here], firsts[1][there])
        highest = jnp.where(number < count, lasts[0][here], lasts[1][there])
        lowest = jnp.clip(lowest, 0, (rows - 1) * blocks - 1)
        highest = jnp.clip(highest, lowest, (rows - 1) * blocks - 1)
        return s, at, side, whole, lowest, (highest - lowest) // WINDOW + 1

    @pl.loop(0, 2 * count // TOGETHER)
    def _(batch):
        start = pl.multiple_of(batch * share, share)
        found_ref[pl.ds(start, share), :] = jnp.zeros((share, 2 * LANES), jnp.float32)
        items, spreads = [find(batch * TOGETHER + i) for i in range(TOGETHER)], []
        for i, (_, _, side, _, _, _) in enumerate(items):
            low = side[5:6].astype(jnp.int32)
            first, second = lo_iota == low, lo_iota == low + 1
            spread = jnp.concatenate(
                [
                    jnp.where(first, side[0:1], jnp.where(second, side[1:2], 0.0)),
                    jnp.where(first, side[2:3], jnp.where(second, side[3:4], 0.0)),
                ],
                axis=0,
            ).astype(jnp.bfloat16)
            spread_ref[batch * TOGETHER + i] = spread
            spreads.append(spread)

        def gather(item, spread, window, model):
            _, _, _, whole, lowest, _ = item
            base = lowest + window * WINDOW
            at = pl.ds(pl.multiple_of((base + blocks) * group, group), high)
            part = jnp.dot(table_ref[at, :], spread, preferred_element_type=jnp.float32)
            for i in range(WINDOW):
                block = part[i * group:(i + 1) * group].reshape(group // 8, 8, OBS)
                model = jnp.where((whole == base + i)[None], block, model)
            return model

        zero = jnp.zeros((group // 8, 8, OBS), jnp.float32)
        models = [gather(item, spread, 0, zero) for item, spread in zip(items, spreads)]

        def more(window, models):
            return [
                gather(item, spread_ref[batch * TOGETHER + i], jnp.minimum(window, item[-1] - 1), model)
                for i, (item, model) in enumerate(zip(items, models))
            ]

        models = lax.fori_loop(1, functools.reduce(jnp.maximum, [item[-1] for item in items]), more, models)
        for (s, at, _, _, _, _), model in zip(items, models):
            departure = model.reshape(group, OBS) - obs_ref[s, :group, at].astype(jnp.float32)
            departure_ref[s, :, at] = departure.astype(jnp.bfloat16)

    @pl.loop(0, 2 * count // TOGETHER)
    def _(batch):
        items = [find(batch * TOGETHER + i) for i in range(TOGETHER)]

        def scatter(i, window):
            s, at, _, whole, lowest, _ = items[i]
            departure = departure_ref[s, :, at].astype(jnp.float32).reshape(group // 8, 8, OBS)
            base = lowest + window * WINDOW
            chosen = [
                jnp.where((whole == base + i)[None], departure, 0.0).reshape(group, OBS) for i in range(WINDOW)
            ]
            rows_at = pl.ds(pl.multiple_of(base * group, group), high)
            found_ref[rows_at, :] += lax.dot_general(
                jnp.concatenate(chosen, axis=0).astype(jnp.bfloat16),
                spread_ref[batch * TOGETHER + i],
                (((1,), (1,)), ((), ())),
                preferred_element_type=jnp.float32,
            )

        for i in range(TOGETHER):
            scatter(i, 0)
        for i in range(TOGETHER):
            pl.loop(1, items[i][-1])(functools.partial(scatter, i))

    for row in range(rows):
        out, slope = [ref.at[row % parts * group:(row % parts + 1) * group] for ref in (grads[row // parts], slopes[row // parts])]
        sums = [jnp.zeros((group, LANES), jnp.float32) for _ in range(tiles)]
        for j in range(blocks):
            tile, shift = divmod(j * STEP, LANES)
            block = jnp.zeros((group, LANES), jnp.float32)
            if row < rows - 1:
                start = (row * blocks + j) * group
                block += found_ref[start:start + group, :LANES]
            if row > 0:
                start = ((row - 1) * blocks + j) * group
                block += found_ref[start:start + group, LANES:]
            if shift:
                block = pltpu.roll(block, shift, 1)
                sums[tile] += jnp.where(lane >= shift, block, 0.0)
                sums[tile + 1] += jnp.where(lane < shift, block, 0.0)
            else:
                sums[tile] += block
        sums[0] += jnp.where(lane == 0, pltpu.roll(sums[last], LANES - rem, 1), 0.0)
        for tile in range(tiles):
            at = slice(tile * LANES, (tile + 1) * LANES)
            sums[tile] *= slope[:, at]
            if tile < last:
                out[:, at] = sums[tile].astype(jnp.bfloat16)
        out[:, last * LANES:] = wrapped_tail(sums[0], sums[last], rem).astype(jnp.bfloat16)
    for k, piece in enumerate(pieces):
        piece[...] = first_ref[pl.ds(pl.multiple_of((place_ref[0] ^ k) * group, group), group), :]


def observe(place, one, two, tables, slopes, parts, width):
    group, wide = slopes[0].shape[0] // parts, slopes[0].shape[1]
    turns = len(slopes)
    rows = parts * turns
    blocks = -(-width // STEP)
    sets, depth, size = 2 * one[0].shape[0], one[0].shape[1], one[0].shape[2]
    numbers = sets * size // OBS
    found = -(-((rows - 1) * blocks + WINDOW) * group * TOGETHER // numbers // 8) * 8 * numbers // TOGETHER
    results = pl.pallas_call(
        functools.partial(observe_kernel, parts, turns, width),
        out_shape=[jax.ShapeDtypeStruct((group, wide), jnp.bfloat16)] * parts
        + [jax.ShapeDtypeStruct((parts * group, wide), jnp.bfloat16)] * (turns - 1)
        + [jax.ShapeDtypeStruct((sets, group, size), jnp.bfloat16)],
        in_specs=[SMEM] * 5 + [pl.BlockSpec(memory_space=pl.ANY)] * (2 + turns) + [VMEM] * turns,
        out_specs=[VMEM] * (parts + turns),
        scratch_shapes=[
            pltpu.VMEM(((rows + 1) * blocks * group, 2 * LANES), jnp.bfloat16),
            pltpu.VMEM((found, 2 * LANES), jnp.float32),
            pltpu.VMEM((sets, depth, size), jnp.bfloat16),
            pltpu.VMEM((numbers, 2 * LANES, OBS), jnp.bfloat16),
            pltpu.VMEM((parts * group, wide), jnp.bfloat16),
            pltpu.SemaphoreType.DMA((2 + 2 * turns,)),
        ],
        compiler_params=PARAMS,
        cost_estimate=SMALL,
        name="observe",
    )(place, one[2], two[2], one[3], two[3], one[0], two[0], *tables, *slopes)
    return [results[:parts], *results[parts:-1]], results[-1]


def after(value, *others):
    return lax.optimization_barrier((value, *others))[0]


def turn_over(block, axis):
    return lax.all_to_all(block, axis, split_axis=0, concat_axis=0, tiled=True)


def swap(pieces):
    count = lax.axis_size("chan")
    return [pieces[0]] + [
        lax.ppermute(pieces[k], "chan", [(i, i ^ k) for i in range(count)]) for k in range(1, count)
    ]


def mix(place, weights, blocks, ahead=(), between=None):
    count, turns = lax.axis_size("lat"), len(blocks)
    forward = [(i, i + 1) for i in range(count - 1)]
    backward = [(i + 1, i) for i in range(count - 1)]
    pieces = swap(blocks[0])
    heres = [after(assemble(place, pieces), *ahead)]
    for block in blocks[1:]:
        heres.append(turn_over(after(block, *pieces[1:]), "chan"))
    done = () if between is None else between(heres[0])
    if turns > 1:
        heres[1] = after(heres[1], *done)
    results, mixed = [], ()
    for turn in range(turns):
        here = heres[turn]
        halos = [lax.ppermute(here, "lat", forward), lax.ppermute(here, "lat", backward)]
        ready = after(here, *mixed, *heres[turn + 1:turn + 2], *done)
        split = lax.axis_size("chan") if turn and turn == turns - 1 else 1
        mixed = conv(place, weights, halos[0], ready, halos[1], split)
        if split > 1:
            mixed = list(mixed)
            results.append(swap(mixed))
        else:
            results.append(turn_over(after(mixed, *results[-1:]), "chan"))
            mixed = [mixed]
    return results, done, mixed[0]


def shards(state, kernel, bias, innovations, interp, cells, counts):
    rows, width = state.shape[1:]
    parts, slabs = lax.axis_size("chan"), lax.axis_size("lat")
    total = kernel.shape[2]
    place = lax.axis_index("chan").reshape(1)
    forward_weights = kernel.reshape(3, 3 * total, total)
    backward_weights = jnp.transpose(kernel[::-1, ::-1], (0, 1, 3, 2)).reshape(3, 3 * total, total)

    blocks = split_rows(place, state, parts, padded_width(width))

    used, rows_of, cells_of = lax.optimization_barrier((counts, interp, cells, blocks[0][0]))[:3]
    interp_rows = jnp.transpose(rows_of[:, 0], (1, 0, 2)).astype(jnp.float32)
    packed = pack_obs(used, innovations[:, 0], interp_rows, cells_of[0][:, None, :], width)
    obs = turn_over(packed, "lat")
    mixed, one, last = mix(
        place, forward_weights, blocks, (obs,), lambda ahead: sort_obs(after(obs, ahead), 0, slabs // 2)
    )
    two = sort_obs(after(obs, last), slabs // 2, slabs // 2)

    tables, slopes = [], []
    for block in mixed:
        table, slope = activate(after(place, *tables), bias[:, None], block, parts, width)
        tables.append(table)
        slopes.append(slope)
    grads, departures = observe(place, one, two, tables, slopes, parts, width)
    grad_blocks, (unsorted,), last = mix(
        place, backward_weights, grads, (),
        lambda ahead: [unsort_obs(after(departures, ahead), one[1], two[1], slabs)],
    )
    departures_out = unpack_obs(turn_over(after(unsorted, last, *grad_blocks[:-1]), "lat"))
    grad_state = join_rows(after(place, departures_out), grad_blocks, parts, width)
    return grad_state, departures_out.reshape(innovations.shape)


def solution(mesh):
    return jax.shard_map(
        shards,
        mesh=mesh,
        in_specs=(
            P("chan", "lat", None),
            P(),
            P("chan"),
            P("chan", "lat", None, None),
            P(None, "lat", None, None),
            P("lat", None, None),
            P("lat", None),
        ),
        out_specs=(P("chan", "lat", None), P("chan", "lat", None, None)),
        check_vma=False,
    )
```

time: 269 us -> 251 us (0.933)
  Pallas kernels: 122 us -> 109 us
  starting transfers between devices: 72.7 us -> 69.3 us
    ppermute x24 -> x12, waiting for transfers between devices: 59.2 us -> 33.2 us  [swap(): lax.ppermute(pieces[k], 'chan', [(i, i ^ k) for i in range(count)])]
    all_to_all x2 -> x6, waiting for transfers between devices: 0.01 us -> 25.5 us  [turn_over(): return lax.all_to_all(block, axis, split_axis=0, concat_axis=0, tiled=True)]
    ppermute x24 -> x12, starting transfers between devices: 40.4 us -> 19.9 us  [swap(): lax.ppermute(pieces[k], 'chan', [(i, i ^ k) for i in range(count)])]
    all_to_all x2 -> x6, starting transfers between devices: 16.4 us -> 30 us  [turn_over(): return lax.all_to_all(block, axis, split_axis=0, concat_axis=0, tiled=True)]
    pallas_call x7 -> x9, Pallas kernels: 68.1 us -> 59.9 us  [the longest x4 24 us: conv(): pl.pallas_call(conv_kernel, out_shape=[jax.ShapeDtypeStruct((total // par...]
    pallas_call x4 -> x2, Pallas kernels: 8.62 us -> 4.3 us  [assemble(): pl.pallas_call(assemble_kernel, out_shape=jax.ShapeDtypeStruct((group * l...]
    ppermute x4, starting transfers between devices: 10.3 us -> 14.3 us  [mix(): lax.ppermute(here, 'lat', forward)]
    unnamed x99 -> x65, local copies, waits for them, and re-layouts: 9.92 us -> 8.27 us
  transfers between devices with their start and end apart: 34 -> 26, of which waited for: 10 -> 8; matrix products, arithmetic and copies ran while one was open for 1% -> 1% of each run, Pallas kernels for 28% -> 29%
where the time goes in v3:
time: 251 us; the launch traced here: 249 us
  Pallas kernels  109 us (43%)
  starting transfers between devices  69.3 us (28%)
  waiting for transfers between devices  58.7 us (23%)
  local copies, waits for them, and re-layouts  11.2 us (4%)
    ppermute x12, waiting for transfers between devices, swap(): lax.ppermute(pieces[k], 'chan', [(i, i ^ k) for i in range(count)])  33.2 us
    all_to_all x6, starting transfers between devices, turn_over(): return lax.all_to_all(block, axis, split_axis=0, concat_axis=0, tiled=True)  30 us
    pallas_call x2, Pallas kernels, sort_obs(): pl.pallas_call(functools.partial(sort_obs_kernel, begin), out_shape=[jax....  26.2 us
    all_to_all x6, waiting for transfers between devices, turn_over(): return lax.all_to_all(block, axis, split_axis=0, concat_axis=0, tiled=True)  25.5 us
    pallas_call x4, Pallas kernels, conv(): pl.pallas_call(conv_kernel, out_shape=[jax.ShapeDtypeStruct((total // par...  24 us
    pallas_call x1, Pallas kernels, observe(): pl.pallas_call(functools.partial(observe_kernel, parts, turns, width), ou...  21.5 us
    ppermute x12, starting transfers between devices, swap(): lax.ppermute(pieces[k], 'chan', [(i, i ^ k) for i in range(count)])  19.9 us
    ppermute x4, starting transfers between devices, mix(): lax.ppermute(here, 'lat', forward)  14.3 us
  transfers between devices with their start and end apart: 26, of which 8 were waited for; matrix products, arithmetic and copies ran while one was open for 1% of the time, Pallas kernels for 29%

profile of v3, /device:TPU:0, one launch (start us, length us, event | category | flops | bytes accessed | tf_op | source)
XLA Modules:
  0.0 249.5 jit_solution(1342096447007617369)
XLA Ops:
  0.7 3.3 %split_rows.1 = (bf16[64,1536]{1,0:T(8,128)(2,1)}, bf16[64,1536]{1,0:T(8,128)(2,1)}, bf16[64,1536]{1,0:T(8,128)(2,1)}, bf16[64,1536]{1,0:T(8,128)(2,1)}, bf16[256,1536]{1,0:T(8,128)(2,1)}) custom-call(s32[1]{0:T(128)} %bitcast.place_ref, bf16[64,8,1440]{2,1,0:T(8,128)(2,1)} %state_ref.1), custom_call_target="tpu_custom_call" | custom-call | flops 1000 | bytes 1000 | tf_op jit(solution)/shard_map/split_rows/pallas_call | solution.py:67
  4.0 0.7 copy.16
  4.7 0.6 broadcast_in_dim_squeeze.3.cells_ref
  5.3 3.5 %pack_obs.1 = bf16[8,80,1024]{2,1,0:T(8,128)(2,1)} custom-call(s32[1,8]{1,0:T(1,128)} %counts_ref, f32[512,1024]{1,0:T(8,128)} %bitcast.29, f32[8,4,1024]{2,1,0:T(4,128)} %bitcast.43, s32[8,1,1024]{2,1,0:T(1,128)} %broadcast_in_dim_squeeze.3.cells_ref), custom_call_target="tpu_custom_call" | custom-call | flops 1000 | bytes 1000 | tf_op jit(solution)/shard_map/pack_obs/pallas_call | solution.py:203
  8.9 5.3 %all-to-all-start = ((bf16[8,80,1024]{2,1,0:T(8,128)(2,1)}), bf16[8,80,1024]{2,1,0:T(8,128)(2,1)S(1)}, u32[]{:S(2)}, u32[]{:S(2)}) async-start(bf16[8,80,1024]{2,1,0:T(8,128)(2,1)} %pack_obs.1), calls=%async_computation | async-start | bytes 2621440 | tf_op jit(solution)/shard_map/all_to_all | solution.py:547
  14.2 1.6 collective-permute-start
  15.9 2.6 %collective-permute-start.1 = (bf16[64,1536]{1,0:T(8,128)(2,1)S(1)}, bf16[64,1536]{1,0:T(8,128)(2,1)S(1)}, u32[]{:S(2)}, u32[]{:S(2)}) collective-permute-start(bf16[64,1536]{1,0:T(8,128)(2,1)S(1)} %copy-done.30), channel_id=1, source_target_pairs={{0,2},{1,3},{2,0},{3,1},{4,6},{5,7},{6,4},{7,5},{8,10},{9,11},{10,... | collective-permute-start | bytes 589832 | tf_op jit(solution)/shard_map/ppermute | solution.py:553
  18.4 0.2 collective-permute-start.2
  18.7 6.6 %collective-permute-done.refs_1_ = bf16[64,1536]{1,0:T(8,128)(2,1)S(1)} collective-permute-done((bf16[64,1536]{1,0:T(8,128)(2,1)S(1)}, bf16[64,1536]{1,0:T(8,128)(2,1)S(1)}, u32[]{:S(2)}, u32[]{:S(2)}) %collective-permute-start) | collective-permute-done | bytes 196640 | tf_op jit(solution)/shard_map/ppermute | solution.py:553
  25.3 7.7 %collective-permute-done.1.refs_2_ = bf16[64,1536]{1,0:T(8,128)(2,1)S(1)} collective-permute-done((bf16[64,1536]{1,0:T(8,128)(2,1)S(1)}, bf16[64,1536]{1,0:T(8,128)(2,1)S(1)}, u32[]{:S(2)}, u32[]{:S(2)}) %collective-permute-start.1) | collective-permute-done | bytes 196640 | tf_op jit(solution)/shard_map/ppermute | solution.py:553
  33.0 6.3 %all-to-all-start.1 = ((bf16[4,64,1536]{2,1,0:T(8,128)(2,1)}), bf16[4,64,1536]{2,1,0:T(8,128)(2,1)S(1)}, u32[]{:S(2)}, u32[]{:S(2)}) async-start(bf16[4,64,1536]{2,1,0:T(8,128)(2,1)} %bitcast.5), calls=%async_computation.1 | async-start | bytes 1572864 | tf_op jit(solution)/shard_map/all_to_all | solution.py:547
  39.3 2.2 assemble.2.here_ref
  41.4 1.3 collective-permute-start.4
  42.8 1.3 collective-permute-start.5
  44.1 13.1 %sort_obs.2 = (bf16[2,80,2048]{2,1,0:T(8,128)(2,1)}, s32[2,1,2048]{2,1,0:T(1,128)}, s32[16]{0:T(128)}, s32[16]{0:T(128)}) custom-call(bf16[8,80,1024]{2,1,0:T(8,128)(2,1)} %copy-done), custom_call_target="tpu_custom_call" | custom-call | flops 1000 | bytes 1000 | tf_op jit(solution)/shard_map/sort_obs/pallas_call | solution.py:253
  57.1 1.7 all-to-all-done.1
  58.9 4.1 %collective-permute-start.3 = (bf16[256,1536]{1,0:T(8,128)(2,1)S(1)}, bf16[256,1536]{1,0:T(8,128)(2,1)}, u32[]{:S(2)}, u32[]{:S(2)}) collective-permute-start(bf16[256,1536]{1,0:T(8,128)(2,1)S(1)} %bitcast.37), channel_id=1, source_target_pairs={{0,4},{4,8},{8,12},{12,16},{16,20},{20,24},{24,28},{1,5},{5,9},{9,... | collective-permute-start | bytes 2359304 | tf_op jit(solution)/shard_map/ppermute | solution.py:571
  63.0 1.3 collective-permute-start.6
  64.3 0.8 copy-done.23
  65.1 0.3 copy-done.25
  65.4 6.1 %conv.4 = bf16[256,1536]{1,0:T(8,128)(2,1)} custom-call(s32[1]{0:T(128)} %bitcast.place_ref, bf16[3,768,256]{2,1,0:T(8,128)(2,1)} %bitcast.30, bf16[256,1536]{1,0:T(8,128)(2,1)} %copy-done.23, bf16[256,1536]{1,0:T(8,128)(2,1)} %assemble.2.here_ref, bf16[256,1536]{1,0:T(8,128)(2,1)} %copy-done.25), custom_call_target="tpu_custom_call" | custom-call | flops 7000000000 | bytes 1000 | tf_op jit(solution)/shard_map/conv/pallas_call | solution.py:164
  71.5 5.1 %all-to-all-start.2 = ((bf16[4,64,1536]{2,1,0:T(8,128)(2,1)}), bf16[4,64,1536]{2,1,0:T(8,128)(2,1)S(1)}, u32[]{:S(2)}, u32[]{:S(2)}) async-start(bf16[4,64,1536]{2,1,0:T(8,128)(2,1)} %bitcast.41), calls=%async_computation.2 | async-start | bytes 1572864 | tf_op jit(solution)/shard_map/all_to_all | solution.py:547
  76.6 5.9 %conv.5 = (bf16[64,1536]{1,0:T(8,128)(2,1)}, bf16[64,1536]{1,0:T(8,128)(2,1)}, bf16[64,1536]{1,0:T(8,128)(2,1)}, bf16[64,1536]{1,0:T(8,128)(2,1)}) custom-call(s32[1]{0:T(128)} %bitcast.place_ref, bf16[3,768,256]{2,1,0:T(8,128)(2,1)} %bitcast.31, bf16[256,1536]{1,0:T(8,128)(2,1)} %collective-permute-done.3.below_ref, bf16[256,1536]{1,0:T(8,128)(2,1)} %bitcast.39, ...), custom_call_target="tpu_custom_call" | custom-call | flops 7000000000 | bytes 1000 | tf_op jit(solution)/shard_map/conv/pallas_call | solution.py:164
  82.5 2.0 collective-permute-start.7
  84.5 2.4 collective-permute-start.8
  86.9 0.7 copy.10.bias_ref
  87.6 13.1 %sort_obs.3 = (bf16[2,80,2048]{2,1,0:T(8,128)(2,1)}, s32[2,1,2048]{2,1,0:T(1,128)}, s32[16]{0:T(128)}, s32[16]{0:T(128)}) custom-call(bf16[8,80,1024]{2,1,0:T(8,128)(2,1)} %copy-done), custom_call_target="tpu_custom_call" | custom-call | flops 1000 | bytes 1000 | tf_op jit(solution)/shard_map/sort_obs/pallas_call | solution.py:253
  100.7 0.9 copy-done.2
  101.6 3.7 %activate.2 = (bf16[3072,128]{1,0:T(8,128)(2,1)}, f32[256,1536]{1,0:T(8,128)}) custom-call(s32[1]{0:T(128)} %bitcast.place_ref, f32[64,1]{1,0:T(8,128)} %copy.10.bias_ref, bf16[256,1536]{1,0:T(8,128)(2,1)} %bitcast.26), custom_call_target="tpu_custom_call" | custom-call | flops 1000 | bytes 1000 | tf_op jit(solution)/shard_map/activate/pallas_call | solution.py:355
  105.3 5.3 %collective-permute-done.8.refs_2_ = bf16[64,1536]{1,0:T(8,128)(2,1)S(1)} collective-permute-done((bf16[64,1536]{1,0:T(8,128)(2,1)}, bf16[64,1536]{1,0:T(8,128)(2,1)S(1)}, u32[]{:S(2)}, u32[]{:S(2)}) %collective-permute-start.8) | collective-permute-done | bytes 196640 | tf_op jit(solution)/shard_map/ppermute | solution.py:553
  110.6 0.7 copy-done.8
  111.2 0.7 copy-done.9
  111.9 3.8 %activate.3 = (bf16[3072,128]{1,0:T(8,128)(2,1)}, f32[256,1536]{1,0:T(8,128)}) custom-call(s32[1]{0:T(128)} %bitcast.place_ref, f32[64,1]{1,0:T(8,128)} %copy.10.bias_ref, bf16[64,1536]{1,0:T(8,128)(2,1)} %get-tuple-element.69.refs_0_, bf16[64,1536]{1,0:T(8,128)(2,1)} %copy-done.7, bf16[64,1536]{1,0:T(8,128)(2,1)} %copy-done.8, bf16[64,1536]{1,0:T(8,128)(2,1)} %copy-done.9), custom_call_target="tpu_custom_call" | custom-call | flops 1000 | bytes 1000 | tf_op jit(solution)/shard_map/activate/pallas_call | solution.py:355
  115.7 21.5 %observe.1 = (bf16[64,1536]{1,0:T(8,128)(2,1)}, bf16[64,1536]{1,0:T(8,128)(2,1)}, bf16[64,1536]{1,0:T(8,128)(2,1)}, bf16[64,1536]{1,0:T(8,128)(2,1)}, bf16[256,1...) custom-call(s32[1]{0:T(128)} %bitcast.place_ref, s32[16]{0:T(128)} %get-tuple-element.60.refs_0_, ...), custom_call_target="tpu_custom_call" | custom-call | flops 1000 | bytes 1000 | tf_op jit(solution)/shard_map/observe/pallas_call | solution.py:520
  137.2 4.2 %collective-permute-start.10 = (bf16[64,1536]{1,0:T(8,128)(2,1)}, bf16[64,1536]{1,0:T(8,128)(2,1)S(1)}, u32[]{:S(2)}, u32[]{:S(2)}) collective-permute-start(bf16[64,1536]{1,0:T(8,128)(2,1)} %get-tuple-element.84), channel_id=1, source_target_pairs={{0,1},{1,0},{2,3},{3,2},{4,5},{5,4},{6,7},{7,6},{8,9},{9,8},{10,11... | collective-permute-start | bytes 589832 | tf_op jit(solution)/shard_map/ppermute | solution.py:553
  141.4 2.4 collective-permute-start.12
  143.8 3.8 %collective-permute-done.10.refs_1_ = bf16[64,1536]{1,0:T(8,128)(2,1)S(1)} collective-permute-done((bf16[64,1536]{1,0:T(8,128)(2,1)}, bf16[64,1536]{1,0:T(8,128)(2,1)S(1)}, u32[]{:S(2)}, u32[]{:S(2)}) %collective-permute-start.10) | collective-permute-done | bytes 196640 | tf_op jit(solution)/shard_map/ppermute | solution.py:553
  147.6 9.8 %collective-permute-done.11.refs_2_ = bf16[64,1536]{1,0:T(8,128)(2,1)S(1)} collective-permute-done((bf16[64,1536]{1,0:T(8,128)(2,1)}, bf16[64,1536]{1,0:T(8,128)(2,1)S(1)}, u32[]{:S(2)}, u32[]{:S(2)}) %collective-permute-start.11) | collective-permute-done | bytes 196640 | tf_op jit(solution)/shard_map/ppermute | solution.py:553
  157.4 4.5 %all-to-all-start.3 = ((bf16[4,64,1536]{2,1,0:T(8,128)(2,1)}), bf16[4,64,1536]{2,1,0:T(8,128)(2,1)S(1)}, u32[]{:S(2)}, u32[]{:S(2)}) async-start(bf16[4,64,1536]{2,1,0:T(8,128)(2,1)} %bitcast.40), calls=%async_computation.3 | async-start | bytes 1572864 | tf_op jit(solution)/shard_map/all_to_all | solution.py:547
  161.9 2.1 assemble.3.here_ref
  164.1 2.2 collective-permute-start.14
  166.2 1.3 collective-permute-start.15
  167.5 0.1 reverse_bitcast_fusion
  167.6 1.5 copy.12
  169.2 12.0 %unsort_obs.1 = bf16[8,64,1024]{2,1,0:T(8,128)(2,1)} custom-call(bf16[4,64,2048]{2,1,0:T(8,128)(2,1)} %get-tuple-element.87.sorted_ref, s32[2,1,2048]{2,1,0:T(1,128)} %get-tuple-element.64.one_ref, s32[2,1,2048]{2,1,0:T(1,128)} %get-tuple-element.88.two_ref), custom_call_target="tpu_custom_call" | custom-call | flops 1000 | bytes 1000 | tf_op jit(solution)/shard_map/unsort_obs/pallas_call | solution.py:287
  181.2 6.7 %collective-permute-start.13 = (bf16[256,1536]{1,0:T(8,128)(2,1)S(1)}, bf16[256,1536]{1,0:T(8,128)(2,1)S(1)}, u32[]{:S(2)}, u32[]{:S(2)}) collective-permute-start(bf16[256,1536]{1,0:T(8,128)(2,1)S(1)} %bitcast.34), channel_id=1, source_target_pairs={{0,4},{4,8},{8,12},{12,16},{16,20},{20,24},{24,28},{1,5},{5,9},{9,... | collective-permute-start | bytes 2359304 | tf_op jit(solution)/shard_map/ppermute | solution.py:571
  187.9 1.3 collective-permute-start.16
  189.2 6.1 %conv.6 = bf16[256,1536]{1,0:T(8,128)(2,1)} custom-call(s32[1]{0:T(128)} %bitcast.place_ref, bf16[3,768,256]{2,1,0:T(8,128)(2,1)} %bitcast.32, bf16[256,1536]{1,0:T(8,128)(2,1)} %collective-permute-done.14.below_ref, bf16[256,1536]{1,0:T(8,128)(2,1)} %assemble.3.here_ref, bf16[256,1536]{1,0:T(8,128)(2,1)} %collective-permute-done.15.above_ref), custom_call_target="tpu_custom_call" | custom-call | flops 7000000000 | bytes 1000 | tf_op jit(solution)/shard_map/conv/pallas_call | solution.py:164
  195.3 5.1 %all-to-all-start.4 = ((bf16[4,64,1536]{2,1,0:T(8,128)(2,1)}), bf16[4,64,1536]{2,1,0:T(8,128)(2,1)S(1)}, u32[]{:S(2)}, u32[]{:S(2)}) async-start(bf16[4,64,1536]{2,1,0:T(8,128)(2,1)} %bitcast.42), calls=%async_computation.4 | async-start | bytes 1572864 | tf_op jit(solution)/shard_map/all_to_all | solution.py:547
  200.4 0.9 copy-done.22
  201.3 0.9 copy-done.24
  202.2 5.9 %conv.7 = (bf16[64,1536]{1,0:T(8,128)(2,1)}, bf16[64,1536]{1,0:T(8,128)(2,1)}, bf16[64,1536]{1,0:T(8,128)(2,1)}, bf16[64,1536]{1,0:T(8,128)(2,1)}) custom-call(s32[1]{0:T(128)} %bitcast.place_ref, bf16[3,768,256]{2,1,0:T(8,128)(2,1)} %bitcast.33, bf16[256,1536]{1,0:T(8,128)(2,1)} %copy-done.22, bf16[256,1536]{1,0:T(8,128)(2,1)} %bitcast.36, ...), custom_call_target="tpu_custom_call" | custom-call | flops 7000000000 | bytes 1000 | tf_op jit(solution)/shard_map/conv/pallas_call | solution.py:164
  208.1 12.8 %all-to-all-done.4 = bf16[4,64,1536]{2,1,0:T(8,128)(2,1)S(1)} async-done(((bf16[4,64,1536]{2,1,0:T(8,128)(2,1)}), bf16[4,64,1536]{2,1,0:T(8,128)(2,1)S(1)}, u32[]{:S(2)}, u32[]{:S(2)}) %all-to-all-start.4) | async-done | bytes 786464 | tf_op jit(solution)/shard_map/all_to_all | solution.py:547
  220.9 3.7 %all-to-all-start.5 = ((bf16[8,64,1024]{2,1,0:T(8,128)(2,1)}), bf16[8,64,1024]{2,1,0:T(8,128)(2,1)S(1)}, u32[]{:S(2)}, u32[]{:S(2)}) async-start(bf16[8,64,1024]{2,1,0:T(8,128)(2,1)} %unsort_obs.1), calls=%async_computation.5 | async-start | bytes 2097152 | tf_op jit(solution)/shard_map/all_to_all | solution.py:547
  224.6 0.1 collective-permute-start.17
  224.7 2.0 collective-permute-start.18
  226.7 2.4 collective-permute-start.19
  229.1 10.9 %all-to-all-done.5.values_ref = bf16[8,64,1024]{2,1,0:T(8,128)(2,1)S(1)} async-done(((bf16[8,64,1024]{2,1,0:T(8,128)(2,1)}), bf16[8,64,1024]{2,1,0:T(8,128)(2,1)S(1)}, u32[]{:S(2)}, u32[]{:S(2)}) %all-to-all-start.5) | async-done | bytes 1048608 | tf_op jit(solution)/shard_map/all_to_all | solution.py:547
  240.1 1.0 copy-done.1
  241.0 3.4 %unpack_obs.1 = f32[512,1024]{1,0:T(8,128)} custom-call(bf16[8,64,1024]{2,1,0:T(8,128)(2,1)} %copy-done.1), custom_call_target="tpu_custom_call" | custom-call | flops 1000 | bytes 1000 | tf_op jit(solution)/shard_map/unpack_obs/pallas_call | solution.py:310
  244.4 0.6 copy-done.16
  245.1 0.1 copy-done.17
  245.2 0.7 copy-done.18
  245.8 3.6 %join_rows.1 = bf16[64,8,1440]{2,1,0:T(8,128)(2,1)} custom-call(s32[1]{0:T(128)} %bitcast.place_ref, bf16[256,1536]{1,0:T(8,128)(2,1)} %bitcast.27, bf16[64,1536]{1,0:T(8,128)(2,1)} %get-tuple-element.94.refs_1_, bf16[64,1536]{1,0:T(8,128)(2,1)} %copy-done.16, bf16[64,1536]{1,0:T(8,128)(2,1)} %copy-done.17, bf16[64,1536]{1,0:T(8,128)(2,1)} %copy-done.18), custom_call_target="tpu_custom_call" | custom-call | flops 1000 | bytes 1000 | tf_op jit(solution)/shard_map/join_rows/pallas_call | solution.py:103
  (73 shorter events, 0.2 us)
Async XLA Ops:
  0.6 3.4 %copy-start.19 = (bf16[4,1,8,1024]{3,2,1,0:T(8,128)(2,1)S(1)}, bf16[4,1,8,1024]{3,2,1,0:T(8,128)(2,1)}, u32[]{:S(2)}) copy-start(bf16[4,1,8,1024]{3,2,1,0:T(8,128)(2,1)} %param.11) | copy-start | bytes 196612
  0.6 4.1 %copy-start.20 = (s32[1,8,1024]{2,1,0:T(8,128)S(1)}, s32[1,8,1024]{2,1,0:T(8,128)}, u32[]{:S(2)}) copy-start(s32[1,8,1024]{2,1,0:T(8,128)} %param.12) | copy-start | bytes 98308
  8.9 5.3 %copy-start.31 = (bf16[64,1536]{1,0:T(8,128)(2,1)S(1)}, bf16[64,1536]{1,0:T(8,128)(2,1)}, u32[]{:S(2)}) copy-start(bf16[64,1536]{1,0:T(8,128)(2,1)} %get-tuple-element.55) | copy-start | bytes 589828
  8.9 7.0 %copy-start.30 = (bf16[64,1536]{1,0:T(8,128)(2,1)S(1)}, bf16[64,1536]{1,0:T(8,128)(2,1)}, u32[]{:S(2)}) copy-start(bf16[64,1536]{1,0:T(8,128)(2,1)} %get-tuple-element.56) | copy-start | bytes 589828
  8.9 9.6 %copy-start.29 = (bf16[64,1536]{1,0:T(8,128)(2,1)S(1)}, bf16[64,1536]{1,0:T(8,128)(2,1)}, u32[]{:S(2)}) copy-start(bf16[64,1536]{1,0:T(8,128)(2,1)} %get-tuple-element.57) | copy-start | bytes 589828
  8.9 24.1 %all-to-all-start = ((bf16[8,80,1024]{2,1,0:T(8,128)(2,1)}), bf16[8,80,1024]{2,1,0:T(8,128)(2,1)S(1)}, u32[]{:S(2)}, u32[]{:S(2)}) async-start(bf16[8,80,1024]{2,1,0:T(8,128)(2,1)} %pack_obs.1), calls=%async_computation | async-start | bytes 2621440 | tf_op jit(solution)/shard_map/all_to_all | solution.py:547
  14.2 11.1 %collective-permute-start = (bf16[64,1536]{1,0:T(8,128)(2,1)S(1)}, bf16[64,1536]{1,0:T(8,128)(2,1)S(1)}, u32[]{:S(2)}, u32[]{:S(2)}) collective-permute-start(bf16[64,1536]{1,0:T(8,128)(2,1)S(1)} %copy-done.31), channel_id=1, source_target_pairs={{0,1},{1,0},{2,3},{3,2},{4,5},{5,4},{6,7},{7,6},{8,9},{9,8},{10,11... | collective-permute-start | bytes 589832 | tf_op jit(solution)/shard_map/ppermute | solution.py:553
  15.9 17.1 %collective-permute-start.1 = (bf16[64,1536]{1,0:T(8,128)(2,1)S(1)}, bf16[64,1536]{1,0:T(8,128)(2,1)S(1)}, u32[]{:S(2)}, u32[]{:S(2)}) collective-permute-start(bf16[64,1536]{1,0:T(8,128)(2,1)S(1)} %copy-done.30), channel_id=1, source_target_pairs={{0,2},{1,3},{2,0},{3,1},{4,6},{5,7},{6,4},{7,5},{8,10},{9,11},{10,... | collective-permute-start | bytes 589832 | tf_op jit(solution)/shard_map/ppermute | solution.py:553
  18.4 14.5 %collective-permute-start.2 = (bf16[64,1536]{1,0:T(8,128)(2,1)S(1)}, bf16[64,1536]{1,0:T(8,128)(2,1)S(1)}, u32[]{:S(2)}, u32[]{:S(2)}) collective-permute-start(bf16[64,1536]{1,0:T(8,128)(2,1)S(1)} %copy-done.29), channel_id=1, source_target_pairs={{0,3},{1,2},{2,1},{3,0},{4,7},{5,6},{6,5},{7,4},{8,11},{9,10},{10,... | collective-permute-start | bytes 589832 | tf_op jit(solution)/shard_map/ppermute | solution.py:553
  25.3 14.0 %copy-start.10 = (bf16[64,1536]{1,0:T(8,128)(2,1)}, bf16[64,1536]{1,0:T(8,128)(2,1)S(1)}, u32[]{:S(2)}) copy-start(bf16[64,1536]{1,0:T(8,128)(2,1)S(1)} %collective-permute-done.refs_1_) | copy-start | bytes 589828
  33.0 6.3 %copy-start.11 = (bf16[64,1536]{1,0:T(8,128)(2,1)}, bf16[64,1536]{1,0:T(8,128)(2,1)S(1)}, u32[]{:S(2)}) copy-start(bf16[64,1536]{1,0:T(8,128)(2,1)S(1)} %collective-permute-done.1.refs_2_) | copy-start | bytes 589828
  33.0 6.3 %copy-start.12 = (bf16[64,1536]{1,0:T(8,128)(2,1)}, bf16[64,1536]{1,0:T(8,128)(2,1)S(1)}, u32[]{:S(2)}) copy-start(bf16[64,1536]{1,0:T(8,128)(2,1)S(1)} %collective-permute-done.2.refs_3_) | copy-start | bytes 589828
  33.0 8.4 %copy-start = (bf16[8,80,1024]{2,1,0:T(8,128)(2,1)}, bf16[8,80,1024]{2,1,0:T(8,128)(2,1)S(1)}, u32[]{:S(2)}) copy-start(bf16[8,80,1024]{2,1,0:T(8,128)(2,1)S(1)} %all-to-all-done.obs_ref) | copy-start | bytes 3932164
  33.0 25.9 %all-to-all-start.1 = ((bf16[4,64,1536]{2,1,0:T(8,128)(2,1)}), bf16[4,64,1536]{2,1,0:T(8,128)(2,1)S(1)}, u32[]{:S(2)}, u32[]{:S(2)}) async-start(bf16[4,64,1536]{2,1,0:T(8,128)(2,1)} %bitcast.5), calls=%async_computation.1 | async-start | bytes 1572864 | tf_op jit(solution)/shard_map/all_to_all | solution.py:547
  41.4 22.8 %collective-permute-start.4 = (bf16[256,1536]{1,0:T(8,128)(2,1)}, bf16[256,1536]{1,0:T(8,128)(2,1)S(1)}, u32[]{:S(2)}, u32[]{:S(2)}) collective-permute-start(bf16[256,1536]{1,0:T(8,128)(2,1)} %assemble.2.here_ref), channel_id=1, source_target_pairs={{0,4},{4,8},{8,12},{12,16},{16,20},{20,24},{24,28},{1,5},{5,9},{9,... | collective-permute-start | bytes 2359304 | tf_op jit(solution)/shard_map/ppermute | solution.py:571
  42.8 21.5 %collective-permute-start.5 = (bf16[256,1536]{1,0:T(8,128)(2,1)}, bf16[256,1536]{1,0:T(8,128)(2,1)S(1)}, u32[]{:S(2)}, u32[]{:S(2)}) collective-permute-start(bf16[256,1536]{1,0:T(8,128)(2,1)} %assemble.2.here_ref), channel_id=1, source_target_pairs={{4,0},{8,4},{12,8},{16,12},{20,16},{24,20},{28,24},{5,1},{9,5},{13... | collective-permute-start | bytes 2359304 | tf_op jit(solution)/shard_map/ppermute | solution.py:571
  58.9 12.6 %copy-start.6 = (bf16[4,64,1536]{2,1,0:T(8,128)(2,1)}, bf16[4,64,1536]{2,1,0:T(8,128)(2,1)S(1)}, u32[]{:S(2)}) copy-start(bf16[4,64,1536]{2,1,0:T(8,128)(2,1)S(1)} %all-to-all-done.1) | copy-start | bytes 2359300
  58.9 17.7 %collective-permute-start.3 = (bf16[256,1536]{1,0:T(8,128)(2,1)S(1)}, bf16[256,1536]{1,0:T(8,128)(2,1)}, u32[]{:S(2)}, u32[]{:S(2)}) collective-permute-start(bf16[256,1536]{1,0:T(8,128)(2,1)S(1)} %bitcast.37), channel_id=1, source_target_pairs={{0,4},{4,8},{8,12},{12,16},{16,20},{20,24},{24,28},{1,5},{5,9},{9,... | collective-permute-start | bytes 2359304 | tf_op jit(solution)/shard_map/ppermute | solution.py:571
  63.0 13.6 %collective-permute-start.6 = (bf16[256,1536]{1,0:T(8,128)(2,1)S(1)}, bf16[256,1536]{1,0:T(8,128)(2,1)}, u32[]{:S(2)}, u32[]{:S(2)}) collective-permute-start(bf16[256,1536]{1,0:T(8,128)(2,1)S(1)} %bitcast.38), channel_id=1, source_target_pairs={{4,0},{8,4},{12,8},{16,12},{20,16},{24,20},{28,24},{5,1},{9,5},{13... | collective-permute-start | bytes 2359304 | tf_op jit(solution)/shard_map/ppermute | solution.py:571
  64.3 0.9 copy-start.23
  64.3 1.1 copy-start.25
  71.5 29.2 %all-to-all-start.2 = ((bf16[4,64,1536]{2,1,0:T(8,128)(2,1)}), bf16[4,64,1536]{2,1,0:T(8,128)(2,1)S(1)}, u32[]{:S(2)}, u32[]{:S(2)}) async-start(bf16[4,64,1536]{2,1,0:T(8,128)(2,1)} %bitcast.41), calls=%async_computation.2 | async-start | bytes 1572864 | tf_op jit(solution)/shard_map/all_to_all | solution.py:547
  76.6 10.3 %copy-start.21 = (f32[64]{0:T(128)S(1)}, f32[64]{0:T(128)}, u32[]{:S(2)}) copy-start(f32[64]{0:T(128)} %param.9) | copy-start | bytes 772
  82.5 22.7 %collective-permute-start.7 = (bf16[64,1536]{1,0:T(8,128)(2,1)}, bf16[64,1536]{1,0:T(8,128)(2,1)S(1)}, u32[]{:S(2)}, u32[]{:S(2)}) collective-permute-start(bf16[64,1536]{1,0:T(8,128)(2,1)} %get-tuple-element.76), channel_id=1, source_target_pairs={{0,1},{1,0},{2,3},{3,2},{4,5},{5,4},{6,7},{7,6},{8,9},{9,8},{10,11... | collective-permute-start | bytes 589832 | tf_op jit(solution)/shard_map/ppermute | solution.py:553
  84.5 26.0 %collective-permute-start.8 = (bf16[64,1536]{1,0:T(8,128)(2,1)}, bf16[64,1536]{1,0:T(8,128)(2,1)S(1)}, u32[]{:S(2)}, u32[]{:S(2)}) collective-permute-start(bf16[64,1536]{1,0:T(8,128)(2,1)} %get-tuple-element.77), channel_id=1, source_target_pairs={{0,2},{1,3},{2,0},{3,1},{4,6},{5,7},{6,4},{7,5},{8,10},{9,11},{10,... | collective-permute-start | bytes 589832 | tf_op jit(solution)/shard_map/ppermute | solution.py:553
  86.9 23.7 %collective-permute-start.9 = (bf16[64,1536]{1,0:T(8,128)(2,1)}, bf16[64,1536]{1,0:T(8,128)(2,1)S(1)}, u32[]{:S(2)}, u32[]{:S(2)}) collective-permute-start(bf16[64,1536]{1,0:T(8,128)(2,1)} %get-tuple-element.78), channel_id=1, source_target_pairs={{0,3},{1,2},{2,1},{3,0},{4,7},{5,6},{6,5},{7,4},{8,11},{9,10},{10,... | collective-permute-start | bytes 589832 | tf_op jit(solution)/shard_map/ppermute | solution.py:553
  100.7 0.9 copy-start.2
  105.3 5.3 %copy-start.7 = (bf16[64,1536]{1,0:T(8,128)(2,1)}, bf16[64,1536]{1,0:T(8,128)(2,1)S(1)}, u32[]{:S(2)}) copy-start(bf16[64,1536]{1,0:T(8,128)(2,1)S(1)} %collective-permute-done.7.refs_1_) | copy-start | bytes 589828
  110.6 0.7 copy-start.8
  111.2 0.7 copy-start.9
  137.2 10.4 %collective-permute-start.10 = (bf16[64,1536]{1,0:T(8,128)(2,1)}, bf16[64,1536]{1,0:T(8,128)(2,1)S(1)}, u32[]{:S(2)}, u32[]{:S(2)}) collective-permute-start(bf16[64,1536]{1,0:T(8,128)(2,1)} %get-tuple-element.84), channel_id=1, source_target_pairs={{0,1},{1,0},{2,3},{3,2},{4,5},{5,4},{6,7},{7,6},{8,9},{9,8},{10,11... | collective-permute-start | bytes 589832 | tf_op jit(solution)/shard_map/ppermute | solution.py:553
  141.4 16.0 %collective-permute-start.11 = (bf16[64,1536]{1,0:T(8,128)(2,1)}, bf16[64,1536]{1,0:T(8,128)(2,1)S(1)}, u32[]{:S(2)}, u32[]{:S(2)}) collective-permute-start(bf16[64,1536]{1,0:T(8,128)(2,1)} %get-tuple-element.85), channel_id=1, source_target_pairs={{0,2},{1,3},{2,0},{3,1},{4,6},{5,7},{6,4},{7,5},{8,10},{9,11},{10,... | collective-permute-start | bytes 589832 | tf_op jit(solution)/shard_map/ppermute | solution.py:553
  141.4 16.0 %collective-permute-start.12 = (bf16[64,1536]{1,0:T(8,128)(2,1)}, bf16[64,1536]{1,0:T(8,128)(2,1)S(1)}, u32[]{:S(2)}, u32[]{:S(2)}) collective-permute-start(bf16[64,1536]{1,0:T(8,128)(2,1)} %get-tuple-element.86), channel_id=1, source_target_pairs={{0,3},{1,2},{2,1},{3,0},{4,7},{5,6},{6,5},{7,4},{8,11},{9,10},{10,... | collective-permute-start | bytes 589832 | tf_op jit(solution)/shard_map/ppermute | solution.py:553
  147.6 14.4 %copy-start.13 = (bf16[64,1536]{1,0:T(8,128)(2,1)}, bf16[64,1536]{1,0:T(8,128)(2,1)S(1)}, u32[]{:S(2)}) copy-start(bf16[64,1536]{1,0:T(8,128)(2,1)S(1)} %collective-permute-done.10.refs_1_) | copy-start | bytes 589828
  157.4 4.5 %copy-start.14 = (bf16[64,1536]{1,0:T(8,128)(2,1)}, bf16[64,1536]{1,0:T(8,128)(2,1)S(1)}, u32[]{:S(2)}) copy-start(bf16[64,1536]{1,0:T(8,128)(2,1)S(1)} %collective-permute-done.11.refs_2_) | copy-start | bytes 589828
  157.4 4.5 %copy-start.15 = (bf16[64,1536]{1,0:T(8,128)(2,1)}, bf16[64,1536]{1,0:T(8,128)(2,1)S(1)}, u32[]{:S(2)}) copy-start(bf16[64,1536]{1,0:T(8,128)(2,1)S(1)} %collective-permute-done.12.refs_3_) | copy-start | bytes 589828
  157.4 10.1 %copy-start.4 = (bf16[3,3,256,256]{3,2,1,0:T(8,128)(2,1)S(1)}, bf16[3,3,256,256]{3,2,1,0:T(8,128)(2,1)}, u32[]{:S(2)}) copy-start(bf16[3,3,256,256]{3,2,1,0:T(8,128)(2,1)} %param.8) | copy-start | bytes 3538948
  157.4 23.8 %all-to-all-start.3 = ((bf16[4,64,1536]{2,1,0:T(8,128)(2,1)}), bf16[4,64,1536]{2,1,0:T(8,128)(2,1)S(1)}, u32[]{:S(2)}, u32[]{:S(2)}) async-start(bf16[4,64,1536]{2,1,0:T(8,128)(2,1)} %bitcast.40), calls=%async_computation.3 | async-start | bytes 1572864 | tf_op jit(solution)/shard_map/all_to_all | solution.py:547
  164.1 25.1 %collective-permute-start.14 = (bf16[256,1536]{1,0:T(8,128)(2,1)}, bf16[256,1536]{1,0:T(8,128)(2,1)}, u32[]{:S(2)}, u32[]{:S(2)}) collective-permute-start(bf16[256,1536]{1,0:T(8,128)(2,1)} %assemble.3.here_ref), channel_id=1, source_target_pairs={{0,4},{4,8},{8,12},{12,16},{16,20},{20,24},{24,28},{1,5},{5,9},{9,... | collective-permute-start | bytes 2359304 | tf_op jit(solution)/shard_map/ppermute | solution.py:571
  166.2 22.9 %collective-permute-start.15 = (bf16[256,1536]{1,0:T(8,128)(2,1)}, bf16[256,1536]{1,0:T(8,128)(2,1)}, u32[]{:S(2)}, u32[]{:S(2)}) collective-permute-start(bf16[256,1536]{1,0:T(8,128)(2,1)} %assemble.3.here_ref), channel_id=1, source_target_pairs={{4,0},{8,4},{12,8},{16,12},{20,16},{24,20},{28,24},{5,1},{9,5},{13... | collective-permute-start | bytes 2359304 | tf_op jit(solution)/shard_map/ppermute | solution.py:571
  181.2 14.1 %copy-start.5 = (bf16[4,64,1536]{2,1,0:T(8,128)(2,1)}, bf16[4,64,1536]{2,1,0:T(8,128)(2,1)S(1)}, u32[]{:S(2)}) copy-start(bf16[4,64,1536]{2,1,0:T(8,128)(2,1)S(1)} %all-to-all-done.3) | copy-start | bytes 2359300
  181.2 19.2 %collective-permute-start.13 = (bf16[256,1536]{1,0:T(8,128)(2,1)S(1)}, bf16[256,1536]{1,0:T(8,128)(2,1)S(1)}, u32[]{:S(2)}, u32[]{:S(2)}) collective-permute-start(bf16[256,1536]{1,0:T(8,128)(2,1)S(1)} %bitcast.34), channel_id=1, source_target_pairs={{0,4},{4,8},{8,12},{12,16},{16,20},{20,24},{24,28},{1,5},{5,9},{9,... | collective-permute-start | bytes 2359304 | tf_op jit(solution)/shard_map/ppermute | solution.py:571
  187.9 12.5 %collective-permute-start.16 = (bf16[256,1536]{1,0:T(8,128)(2,1)S(1)}, bf16[256,1536]{1,0:T(8,128)(2,1)S(1)}, u32[]{:S(2)}, u32[]{:S(2)}) collective-permute-start(bf16[256,1536]{1,0:T(8,128)(2,1)S(1)} %bitcast.35), channel_id=1, source_target_pairs={{4,0},{8,4},{12,8},{16,12},{20,16},{24,20},{28,24},{5,1},{9,5},{13... | collective-permute-start | bytes 2359304 | tf_op jit(solution)/shard_map/ppermute | solution.py:571
  195.3 25.6 %all-to-all-start.4 = ((bf16[4,64,1536]{2,1,0:T(8,128)(2,1)}), bf16[4,64,1536]{2,1,0:T(8,128)(2,1)S(1)}, u32[]{:S(2)}, u32[]{:S(2)}) async-start(bf16[4,64,1536]{2,1,0:T(8,128)(2,1)} %bitcast.42), calls=%async_computation.4 | async-start | bytes 1572864 | tf_op jit(solution)/shard_map/all_to_all | solution.py:547
  200.4 0.9 copy-start.22
  201.3 0.9 copy-start.24
  208.1 16.6 %copy-start.28 = (bf16[64,1536]{1,0:T(8,128)(2,1)S(1)}, bf16[64,1536]{1,0:T(8,128)(2,1)}, u32[]{:S(2)}) copy-start(bf16[64,1536]{1,0:T(8,128)(2,1)} %get-tuple-element.97) | copy-start | bytes 589828
  208.1 16.7 %copy-start.27 = (bf16[64,1536]{1,0:T(8,128)(2,1)S(1)}, bf16[64,1536]{1,0:T(8,128)(2,1)}, u32[]{:S(2)}) copy-start(bf16[64,1536]{1,0:T(8,128)(2,1)} %get-tuple-element.98) | copy-start | bytes 589828
  208.1 18.7 %copy-start.26 = (bf16[64,1536]{1,0:T(8,128)(2,1)S(1)}, bf16[64,1536]{1,0:T(8,128)(2,1)}, u32[]{:S(2)}) copy-start(bf16[64,1536]{1,0:T(8,128)(2,1)} %get-tuple-element.99) | copy-start | bytes 589828
  220.9 23.5 %copy-start.3 = (bf16[4,64,1536]{2,1,0:T(8,128)(2,1)}, bf16[4,64,1536]{2,1,0:T(8,128)(2,1)S(1)}, u32[]{:S(2)}) copy-start(bf16[4,64,1536]{2,1,0:T(8,128)(2,1)S(1)} %all-to-all-done.4) | copy-start | bytes 2359300
  220.9 19.1 %all-to-all-start.5 = ((bf16[8,64,1024]{2,1,0:T(8,128)(2,1)}), bf16[8,64,1024]{2,1,0:T(8,128)(2,1)S(1)}, u32[]{:S(2)}, u32[]{:S(2)}) async-start(bf16[8,64,1024]{2,1,0:T(8,128)(2,1)} %unsort_obs.1), calls=%async_computation.5 | async-start | bytes 2097152 | tf_op jit(solution)/shard_map/all_to_all | solution.py:547
  224.6 19.8 %collective-permute-start.17 = (bf16[64,1536]{1,0:T(8,128)(2,1)S(1)}, bf16[64,1536]{1,0:T(8,128)(2,1)S(1)}, u32[]{:S(2)}, u32[]{:S(2)}) collective-permute-start(bf16[64,1536]{1,0:T(8,128)(2,1)S(1)} %copy-done.28), channel_id=1, source_target_pairs={{0,1},{1,0},{2,3},{3,2},{4,5},{5,4},{6,7},{7,6},{8,9},{9,8},{10,11... | collective-permute-start | bytes 589832 | tf_op jit(solution)/shard_map/ppermute | solution.py:553
  224.7 19.7 %collective-permute-start.18 = (bf16[64,1536]{1,0:T(8,128)(2,1)S(1)}, bf16[64,1536]{1,0:T(8,128)(2,1)S(1)}, u32[]{:S(2)}, u32[]{:S(2)}) collective-permute-start(bf16[64,1536]{1,0:T(8,128)(2,1)S(1)} %copy-done.27), channel_id=1, source_target_pairs={{0,2},{1,3},{2,0},{3,1},{4,6},{5,7},{6,4},{7,5},{8,10},{9,11},{10,... | collective-permute-start | bytes 589832 | tf_op jit(solution)/shard_map/ppermute | solution.py:553
  226.7 17.7 %collective-permute-start.19 = (bf16[64,1536]{1,0:T(8,128)(2,1)S(1)}, bf16[64,1536]{1,0:T(8,128)(2,1)S(1)}, u32[]{:S(2)}, u32[]{:S(2)}) collective-permute-start(bf16[64,1536]{1,0:T(8,128)(2,1)S(1)} %copy-done.26), channel_id=1, source_target_pairs={{0,3},{1,2},{2,1},{3,0},{4,7},{5,6},{6,5},{7,4},{8,11},{9,10},{10,... | collective-permute-start | bytes 589832 | tf_op jit(solution)/shard_map/ppermute | solution.py:553
  240.1 1.0 copy-start.1
  244.4 0.7 copy-start.16
  244.4 0.8 copy-start.17
  245.2 0.7 copy-start.18

commit v4 on v3

--- a/solution.py
+++ b/solution.py
@@ -180,14 +180,15 @@
     blocks = -(-width // STEP)
     for tile in range(slots // LANES):
         tiles_ref[tile] = values_ref[:, tile * LANES:(tile + 1) * LANES]
+    all_weights = weights_ref[...].astype(jnp.float32)
     for slab in range(slabs):
         used = lane_iota((1, slots)) < counts_ref[0, slab]
         values = jnp.concatenate(
             [tiles_ref[tile, pl.ds(slab, group, stride=slabs), :] for tile in range(slots // LANES)], axis=1
         )
         out_ref[slab, :group, :] = jnp.where(used, values, 0.0).astype(jnp.bfloat16)
-        weights = jnp.where(used, weights_ref[slab], 0.0)
-        local = (cells_ref[slab] - slab * (SPACING * width)).astype(jnp.float32)
+        weights = jnp.where(used, all_weights[:, 0, slab, :], 0.0)
+        local = (cells_ref[0, slab:slab + 1, :] - slab * (SPACING * width)).astype(jnp.float32)
         row = jnp.clip(jnp.floor((local + 0.5) * (1.0 / width)), 0.0, SPACING - 2.0)
         column = local - row * width
         block = jnp.clip(jnp.floor((column + 0.5) * (1.0 / STEP)), 0.0, blocks - 1.0)
@@ -212,13 +213,13 @@
     )(counts, values.reshape(group * slabs, slots), weights, cells)
 
 
-def sort_obs_kernel(begin, obs_ref, sorted_ref, rank_ref, first_ref, last_ref, joined_ref, column_ref):
+def sort_obs_kernel(begin, place_ref, obs_ref, sorted_ref, rank_ref, first_ref, last_ref, joined_ref, column_ref):
     sets, depth, size = sorted_ref.shape
     group = depth - SIDE
     each = obs_ref.shape[2]
     for s in range(sets):
         for i in range(size // each):
-            joined_ref[:, i * each:(i + 1) * each] = obs_ref[begin + s * (size // each) + i]
+            joined_ref[:, i * each:(i + 1) * each] = obs_ref[place_ref[0] ^ (begin + s * (size // each) + i)]
         which = joined_ref[group:, :].astype(jnp.float32)[4:5]
         key = which * size + lane_iota((1, size)).astype(jnp.float32)
         column_ref[...] = jnp.transpose(jnp.broadcast_to(key, (LANES, size)))
@@ -246,7 +247,7 @@
             last_ref[s * (size // OBS) + tile] = jnp.max(which).astype(jnp.int32)
 
 
-def sort_obs(obs, begin, slabs):
+def sort_obs(place, obs, begin, slabs):
     depth, slots = obs.shape[1:]
     size = slots * JOIN
     sets = slabs // JOIN
@@ -258,65 +259,74 @@
             jax.ShapeDtypeStruct((sets * size // OBS,), jnp.int32),
             jax.ShapeDtypeStruct((sets * size // OBS,), jnp.int32),
         ],
-        in_specs=[VMEM],
+        in_specs=[SMEM, VMEM],
         out_specs=[VMEM, VMEM, SMEM, SMEM],
         scratch_shapes=[pltpu.VMEM((depth, size), jnp.bfloat16), pltpu.VMEM((size, LANES), jnp.float32)],
         compiler_params=PARAMS,
         cost_estimate=SMALL,
         name="sort_obs",
-    )(obs)
-
-
-def unsort_obs_kernel(sorted_ref, one_ref, two_ref, out_ref):
-    sets, group, size = sorted_ref.shape
-    each = out_ref.shape[2]
-    for s in range(sets):
-        @pl.loop(0, size // OBS)
+    )(place, obs)
+
+
+def unsort_obs_kernel(begin, count, sorted_ref, *refs):
+    ranks, outs = refs[:-count], refs[-count:]
+    size = sorted_ref.shape[2]
+    each = outs[0].shape[1]
+    places = [(rank_ref, s) for rank_ref in ranks for s in range(rank_ref.shape[0])]
+    for number, out in enumerate(outs):
+        s, offset = divmod(number * each, size)
+
+        @pl.loop(0, each // OBS)
         def _(tile):
             start = pl.multiple_of(tile * OBS, OBS)
-            rank = (one_ref if s < sets // 2 else two_ref)[s % (sets // 2), :, pl.ds(start, OBS)]
+            rank = places[s][0][places[s][1], :, pl.ds(offset + start, OBS)]
             chosen = jnp.where(lax.broadcasted_iota(jnp.int32, (size, OBS), 0) == rank, 1.0, 0.0)
-            taken = jnp.dot(sorted_ref[s], chosen.astype(jnp.bfloat16), preferred_element_type=jnp.float32)
-            slab = s * (size // each) + tile // (each // OBS)
-            at = pl.ds(pl.multiple_of(tile % (each // OBS) * OBS, OBS), OBS)
-            out_ref[slab, :, at] = taken.astype(jnp.bfloat16)
-
-
-def unsort_obs(values, one, two, slabs):
-    sets, group, size = values.shape
+            taken = jnp.dot(
+                sorted_ref[begin + s], chosen.astype(jnp.bfloat16), preferred_element_type=jnp.float32
+            )
+            out[:, pl.ds(start, OBS)] = taken.astype(jnp.bfloat16)
+
+
+def unsort_obs(values, begin, ranks):
+    group, size = values.shape[1:]
+    count = sum(rank.shape[0] for rank in ranks) * JOIN
     return pl.pallas_call(
-        unsort_obs_kernel,
-        out_shape=jax.ShapeDtypeStruct((slabs, group, sets * size // slabs), jnp.bfloat16),
-        in_specs=[VMEM] * 3,
-        out_specs=VMEM,
+        functools.partial(unsort_obs_kernel, begin, count),
+        out_shape=[jax.ShapeDtypeStruct((group, size // JOIN), jnp.bfloat16)] * count,
+        in_specs=[VMEM] * (1 + len(ranks)),
+        out_specs=[VMEM] * count,
         compiler_params=PARAMS,
         cost_estimate=SMALL,
         name="unsort_obs",
-    )(values, one, two)
-
-
-def unpack_obs_kernel(values_ref, out_ref, tiles_ref):
-    slabs, group, slots = values_ref.shape
-    for slab in range(slabs):
+    )(values, *ranks)
+
+
+def unpack_obs_kernel(place_ref, *refs):
+    pieces, out_ref, tiles_ref = refs[:-2], refs[-2], refs[-1]
+    slabs = len(pieces)
+    group, slots = pieces[0].shape
+    for k, piece in enumerate(pieces):
+        slab = place_ref[0] ^ k
         for tile in range(slots // LANES):
-            part = values_ref[slab, :, tile * LANES:(tile + 1) * LANES].astype(jnp.float32)
+            part = piece[:, tile * LANES:(tile + 1) * LANES].astype(jnp.float32)
             tiles_ref[tile, pl.ds(slab, group, stride=slabs), :] = part
     for tile in range(slots // LANES):
         out_ref[:, tile * LANES:(tile + 1) * LANES] = tiles_ref[tile]
 
 
-def unpack_obs(values):
-    slabs, group, slots = values.shape
+def unpack_obs(place, pieces):
+    slabs = len(pieces)
+    group, slots = pieces[0].shape
     return pl.pallas_call(
         unpack_obs_kernel,
         out_shape=jax.ShapeDtypeStruct((group * slabs, slots), jnp.float32),
-        in_specs=[VMEM],
+        in_specs=[SMEM] + [VMEM] * slabs,
         out_specs=VMEM,
         scratch_shapes=[pltpu.VMEM((slots // LANES, group * slabs, LANES), jnp.float32)],
         compiler_params=PARAMS,
         cost_estimate=SMALL,
         name="unpack_obs",
-    )(values)
+    )(place, *pieces)
 
 
 def activate_kernel(parts, width, place_ref, bias_ref, *refs):
@@ -368,14 +378,13 @@
 
 def observe_kernel(parts, turns, width, place_ref, *refs):
     rows = parts * turns
-    firsts, lasts, halves = refs[0:2], refs[2:4], refs[4:6]
-    tables, slopes, refs = refs[6:6 + turns], refs[6 + turns:6 + 2 * turns], refs[6 + 2 * turns:]
+    firsts, lasts, groups = refs[0:3], refs[3:6], refs[6:9]
+    tables, slopes, refs = refs[9:9 + turns], refs[9 + turns:9 + 2 * turns], refs[9 + 2 * turns:]
     pieces, grads, refs = refs[:parts], refs[parts:parts + turns - 1], refs[parts + turns - 1:]
     departure_ref, table_ref, found_ref, obs_ref, spread_ref, first_ref, arrival = refs
     grads = [first_ref, *grads]
     group, wide = slopes[0].shape[0] // parts, slopes[0].shape[1]
     size = obs_ref.shape[2]
-    sets = obs_ref.shape[0] // 2
     blocks = -(-width // STEP)
     tiles = wide // LANES
     rem = width % LANES
@@ -384,37 +393,41 @@
     slab = blocks * group
     high = WINDOW * group
 
-    copies = [
-        pltpu.make_async_copy(half, obs_ref.at[pl.ds(i * sets, sets)], arrival.at[i])
-        for i, half in enumerate(halves)
-    ]
+    copies, begin = [], 0
+    for i, some in enumerate(groups):
+        copies.append(pltpu.make_async_copy(some, obs_ref.at[pl.ds(begin, some.shape[0])], arrival.at[i]))
+        begin += some.shape[0]
     for i, table in enumerate(tables):
         for lanes in range(2):
             start = (i * parts + 1 - lanes) * slab
             target = table_ref.at[pl.ds(start, parts * slab), pl.ds(lanes * LANES, LANES)]
-            copies.append(pltpu.make_async_copy(table, target, arrival.at[2 + 2 * i + lanes]))
+            copies.append(pltpu.make_async_copy(table, target, arrival.at[3 + 2 * i + lanes]))
     for copy in copies:
         copy.start()
     for copy in copies:
         copy.wait()
 
-    count = firsts[0].shape[0]
+    numbers = obs_ref.shape[0] * (size // OBS)
     lo_iota = lax.broadcasted_iota(jnp.int32, (LANES, OBS), 0)
-    share = found_ref.shape[0] // (2 * count // TOGETHER)
+    share = found_ref.shape[0] // (numbers // TOGETHER)
 
     def find(number):
         s = number // (size // OBS)
         at = pl.ds(pl.multiple_of(number % (size // OBS) * OBS, OBS), OBS)
         side = obs_ref[s, group:, at].astype(jnp.float32)
         whole = jnp.broadcast_to(side[4:5].astype(jnp.int32), (8, OBS))
-        here, there = jnp.minimum(number, count - 1), jnp.maximum(number - count, 0)
-        lowest = jnp.where(number < count, firsts[0][here], firsts[1][there])
-        highest = jnp.where(number < count, lasts[0][here], lasts[1][there])
+        lowest = highest = begin = 0
+        for low_ref, high_ref in zip(firsts, lasts):
+            count = low_ref.shape[0]
+            inside = jnp.clip(number - begin, 0, count - 1)
+            lowest = jnp.where(number >= begin, low_ref[inside], lowest)
+            highest = jnp.where(number >= begin, high_ref[inside], highest)
+            begin += count
         lowest = jnp.clip(lowest, 0, (rows - 1) * blocks - 1)
         highest = jnp.clip(highest, lowest, (rows - 1) * blocks - 1)
         return s, at, side, whole, lowest, (highest - lowest) // WINDOW + 1
 
-    @pl.loop(0, 2 * count // TOGETHER)
+    @pl.loop(0, numbers // TOGETHER)
     def _(batch):
         start = pl.multiple_of(batch * share, share)
         found_ref[pl.ds(start, share), :] = jnp.zeros((share, 2 * LANES), jnp.float32)
@@ -456,7 +469,7 @@
             departure = model.reshape(group, OBS) - obs_ref[s, :group, at].astype(jnp.float32)
             departure_ref[s, :, at] = departure.astype(jnp.bfloat16)
 
-    @pl.loop(0, 2 * count // TOGETHER)
+    @pl.loop(0, numbers // TOGETHER)
     def _(batch):
         items = [find(batch * TOGETHER + i) for i in range(TOGETHER)]
 
@@ -509,12 +522,13 @@
         piece[...] = first_ref[pl.ds(pl.multiple_of((place_ref[0] ^ k) * group, group), group), :]
 
 
-def observe(place, one, two, tables, slopes, parts, width):
+def observe(place, groups, tables, slopes, parts, width):
     group, wide = slopes[0].shape[0] // parts, slopes[0].shape[1]
     turns = len(slopes)
     rows = parts * turns
     blocks = -(-width // STEP)
-    sets, depth, size = 2 * one[0].shape[0], one[0].shape[1], one[0].shape[2]
+    sets = sum(group[0].shape[0] for group in groups)
+    depth, size = groups[0][0].shape[1:]
     numbers = sets * size // OBS
     found = -(-((rows - 1) * blocks + WINDOW) * group * TOGETHER // numbers // 8) * 8 * numbers // TOGETHER
     results = pl.pallas_call(
@@ -522,7 +536,7 @@
         out_shape=[jax.ShapeDtypeStruct((group, wide), jnp.bfloat16)] * parts
         + [jax.ShapeDtypeStruct((parts * group, wide), jnp.bfloat16)] * (turns - 1)
         + [jax.ShapeDtypeStruct((sets, group, size), jnp.bfloat16)],
-        in_specs=[SMEM] * 5 + [pl.BlockSpec(memory_space=pl.ANY)] * (2 + turns) + [VMEM] * turns,
+        in_specs=[SMEM] * 7 + [pl.BlockSpec(memory_space=pl.ANY)] * (3 + turns) + [VMEM] * turns,
         out_specs=[VMEM] * (parts + turns),
         scratch_shapes=[
             pltpu.VMEM(((rows + 1) * blocks * group, 2 * LANES), jnp.bfloat16),
@@ -530,12 +544,12 @@
             pltpu.VMEM((sets, depth, size), jnp.bfloat16),
             pltpu.VMEM((numbers, 2 * LANES, OBS), jnp.bfloat16),
             pltpu.VMEM((parts * group, wide), jnp.bfloat16),
-            pltpu.SemaphoreType.DMA((2 + 2 * turns,)),
+            pltpu.SemaphoreType.DMA((3 + 2 * turns,)),
         ],
         compiler_params=PARAMS,
         cost_estimate=SMALL,
         name="observe",
-    )(place, one[2], two[2], one[3], two[3], one[0], two[0], *tables, *slopes)
+    )(place, *[some[i] for i in (2, 3, 0) for some in groups], *tables, *slopes)
     return [results[:parts], *results[parts:-1]], results[-1]
 
 
@@ -547,70 +561,75 @@
     return lax.all_to_all(block, axis, split_axis=0, concat_axis=0, tiled=True)
 
 
-def swap(pieces):
-    count = lax.axis_size("chan")
+def swap(pieces, axis):
+    count = lax.axis_size(axis)
     return [pieces[0]] + [
-        lax.ppermute(pieces[k], "chan", [(i, i ^ k) for i in range(count)]) for k in range(1, count)
+        lax.ppermute(pieces[k], axis, [(i, i ^ k) for i in range(count)]) for k in range(1, count)
     ]
 
 
-def mix(place, weights, blocks, ahead=(), between=None):
+def mix(place, weights, blocks, ahead, between, beyond):
     count, turns = lax.axis_size("lat"), len(blocks)
     forward = [(i, i + 1) for i in range(count - 1)]
     backward = [(i + 1, i) for i in range(count - 1)]
-    pieces = swap(blocks[0])
+    pieces = swap(blocks[0], "chan")
     heres = [after(assemble(place, pieces), *ahead)]
     for block in blocks[1:]:
         heres.append(turn_over(after(block, *pieces[1:]), "chan"))
-    done = () if between is None else between(heres[0])
+    done = between(heres[0])
     if turns > 1:
         heres[1] = after(heres[1], *done)
-    results, mixed = [], ()
+    results, mixed, rest = [], (), ()
     for turn in range(turns):
         here = heres[turn]
         halos = [lax.ppermute(here, "lat", forward), lax.ppermute(here, "lat", backward)]
-        ready = after(here, *mixed, *heres[turn + 1:turn + 2], *done)
+        ready = after(here, *mixed, *heres[turn + 1:turn + 2], *done, *rest)
         split = lax.axis_size("chan") if turn and turn == turns - 1 else 1
         mixed = conv(place, weights, halos[0], ready, halos[1], split)
         if split > 1:
             mixed = list(mixed)
-            results.append(swap(mixed))
+            results.append(swap(mixed, "chan"))
         else:
             results.append(turn_over(after(mixed, *results[-1:]), "chan"))
             mixed = [mixed]
-    return results, done, mixed[0]
+        if turn == 0:
+            rest = beyond(mixed[0])
+    return results, done, rest, mixed[0]
 
 
 def shards(state, kernel, bias, innovations, interp, cells, counts):
     rows, width = state.shape[1:]
     parts, slabs = lax.axis_size("chan"), lax.axis_size("lat")
     total = kernel.shape[2]
-    place = lax.axis_index("chan").reshape(1)
+    place, lat_place = lax.axis_index("chan").reshape(1), lax.axis_index("lat").reshape(1)
     forward_weights = kernel.reshape(3, 3 * total, total)
     backward_weights = jnp.transpose(kernel[::-1, ::-1], (0, 1, 3, 2)).reshape(3, 3 * total, total)
 
     blocks = split_rows(place, state, parts, padded_width(width))
 
-    used, rows_of, cells_of = lax.optimization_barrier((counts, interp, cells, blocks[0][0]))[:3]
-    interp_rows = jnp.transpose(rows_of[:, 0], (1, 0, 2)).astype(jnp.float32)
-    packed = pack_obs(used, innovations[:, 0], interp_rows, cells_of[0][:, None, :], width)
+    packed = pack_obs(after(counts, blocks[0][0]), innovations[:, 0], interp, cells, width)
     obs = turn_over(packed, "lat")
-    mixed, one, last = mix(
-        place, forward_weights, blocks, (obs,), lambda ahead: sort_obs(after(obs, ahead), 0, slabs // 2)
+    quarter = slabs // 4
+    mixed, one, two, last = mix(
+        place, forward_weights, blocks, (obs,),
+        lambda ahead: sort_obs(lat_place, after(obs, ahead), 0, quarter),
+        lambda ahead: sort_obs(lat_place, after(obs, ahead), quarter, quarter),
     )
-    two = sort_obs(after(obs, last), slabs // 2, slabs // 2)
+    three = sort_obs(lat_place, after(obs, last), 2 * quarter, 2 * quarter)
 
     tables, slopes = [], []
     for block in mixed:
         table, slope = activate(after(place, *tables), bias[:, None], block, parts, width)
         tables.append(table)
         slopes.append(slope)
-    grads, departures = observe(place, one, two, tables, slopes, parts, width)
-    grad_blocks, (unsorted,), last = mix(
+    grads, departures = observe(place, [one, two, three], tables, slopes, parts, width)
+    grad_blocks, low, high, last = mix(
         place, backward_weights, grads, (),
-        lambda ahead: [unsort_obs(after(departures, ahead), one[1], two[1], slabs)],
+        lambda ahead: unsort_obs(after(departures, ahead), 0, [one[1], two[1]]),
+        lambda ahead: unsort_obs(after(departures, ahead), 2 * quarter // JOIN, [three[1]]),
     )
-    departures_out = unpack_obs(turn_over(after(unsorted, last, *grad_blocks[:-1]), "lat"))
+    unsorted = lax.optimization_barrier((*low, *high, last))[:slabs]
+    departures_out = unpack_obs(lat_place, swap(unsorted, "lat"))
     grad_state = join_rows(after(place, departures_out), grad_blocks, parts, width)
     return grad_state, departures_out.reshape(innovations.shape)
 

time: 251 us -> 245 us (0.976)
  waiting for transfers between devices: 58.7 us -> 43.1 us
  starting transfers between devices: 69.3 us -> 79.3 us
  Pallas kernels: 109 us -> 112 us
    all_to_all x6 -> x5, waiting for transfers between devices: 25.5 us -> 11.5 us  [turn_over(): return lax.all_to_all(block, axis, split_axis=0, concat_axis=0, tiled=True)]
    ppermute x12 -> x19, starting transfers between devices: 19.9 us -> 31.8 us  [swap(): lax.ppermute(pieces[k], axis, [(i, i ^ k) for i in range(count)])]
    pallas_call x2 -> x3, Pallas kernels: 26.2 us -> 28.1 us  [sort_obs(): pl.pallas_call(functools.partial(sort_obs_kernel, begin), out_shape=[jax....]
    ppermute x12 -> x19, waiting for transfers between devices: 33.2 us -> 31.6 us  [swap(): lax.ppermute(pieces[k], axis, [(i, i ^ k) for i in range(count)])]
    pallas_call x1 -> x2, Pallas kernels: 12 us -> 13.6 us  [unsort_obs(): pl.pallas_call(functools.partial(unsort_obs_kernel, begin, count), out_sh...]
    unnamed x65 -> x80, local copies, waits for them, and re-layouts: 8.27 us -> 6.97 us
    all_to_all x6 -> x5, starting transfers between devices: 30 us -> 29.2 us  [turn_over(): return lax.all_to_all(block, axis, split_axis=0, concat_axis=0, tiled=True)]
  transfers between devices with their start and end apart: 26 -> 32, of which waited for: 8 -> 10; matrix products, arithmetic and copies ran while one was open for 1% -> 1% of each run, Pallas kernels for 29% -> 31%
where the time goes in v4:
time: 245 us
  Pallas kernels  112 us (46%)
  starting transfers between devices  79.3 us (32%)
  waiting for transfers between devices  43.1 us (18%)
  local copies, waits for them, and re-layouts  9.28 us (4%)
    ppermute x19, starting transfers between devices, swap(): lax.ppermute(pieces[k], axis, [(i, i ^ k) for i in range(count)])  31.8 us
    ppermute x19, waiting for transfers between devices, swap(): lax.ppermute(pieces[k], axis, [(i, i ^ k) for i in range(count)])  31.6 us
    all_to_all x5, starting transfers between devices, turn_over(): return lax.all_to_all(block, axis, split_axis=0, concat_axis=0, tiled=True)  29.2 us
    pallas_call x3, Pallas kernels, sort_obs(): pl.pallas_call(functools.partial(sort_obs_kernel, begin), out_shape=[jax....  28.1 us
    pallas_call x4, Pallas kernels, conv(): pl.pallas_call(conv_kernel, out_shape=[jax.ShapeDtypeStruct((total // par...  24 us
    pallas_call x1, Pallas kernels, observe(): pl.pallas_call(functools.partial(observe_kernel, parts, turns, width), ou...  20.6 us
    pallas_call x2, Pallas kernels, unsort_obs(): pl.pallas_call(functools.partial(unsort_obs_kernel, begin, count), out_sh...  13.6 us
    ppermute x4, starting transfers between devices, mix(): lax.ppermute(here, 'lat', forward)  13.2 us
  transfers between devices with their start and end apart: 32, of which 10 were waited for; matrix products, arithmetic and copies ran while one was open for 1% of the time, Pallas kernels for 31%

profile of v4, /device:TPU:0, one launch (start us, length us, event | category | flops | bytes accessed | tf_op | source)
XLA Modules:
  0.0 244.7 jit_solution(7316201544644002386)
XLA Ops:
  0.6 3.3 %split_rows.1 = (bf16[64,1536]{1,0:T(8,128)(2,1)}, bf16[64,1536]{1,0:T(8,128)(2,1)}, bf16[64,1536]{1,0:T(8,128)(2,1)}, bf16[64,1536]{1,0:T(8,128)(2,1)}, bf16[256,1536]{1,0:T(8,128)(2,1)}) custom-call(s32[1]{0:T(128)} %bitcast.place_ref, bf16[64,8,1440]{2,1,0:T(8,128)(2,1)} %state_ref.1), custom_call_target="tpu_custom_call" | custom-call | flops 1000 | bytes 1000 | tf_op jit(solution)/shard_map/split_rows/pallas_call | solution.py:67
  3.9 3.6 %pack_obs.1 = bf16[8,80,1024]{2,1,0:T(8,128)(2,1)} custom-call(s32[1,8]{1,0:T(1,128)} %counts_ref, f32[512,1024]{1,0:T(8,128)} %bitcast.21, bf16[4,1,8,1024]{3,2,1,0:T(8,128)(2,1)} %weights_ref.1, s32[1,8,1024]{2,1,0:T(8,128)} %cells_ref.1), custom_call_target="tpu_custom_call" | custom-call | flops 1000 | bytes 1000 | tf_op jit(solution)/shard_map/pack_obs/pallas_call | solution.py:204
  7.5 5.3 %all-to-all-start = ((bf16[8,80,1024]{2,1,0:T(8,128)(2,1)}), bf16[8,80,1024]{2,1,0:T(8,128)(2,1)S(1)}, u32[]{:S(2)}, u32[]{:S(2)}) async-start(bf16[8,80,1024]{2,1,0:T(8,128)(2,1)} %pack_obs.1), calls=%async_computation | async-start | bytes 2621440 | tf_op jit(solution)/shard_map/all_to_all | solution.py:561
  12.8 1.6 collective-permute-start
  14.5 2.6 %collective-permute-start.1 = (bf16[64,1536]{1,0:T(8,128)(2,1)S(1)}, bf16[64,1536]{1,0:T(8,128)(2,1)S(1)}, u32[]{:S(2)}, u32[]{:S(2)}) collective-permute-start(bf16[64,1536]{1,0:T(8,128)(2,1)S(1)} %copy-done.31), channel_id=1, source_target_pairs={{0,2},{1,3},{2,0},{3,1},{4,6},{5,7},{6,4},{7,5},{8,10},{9,11},{10,... | collective-permute-start | bytes 589832 | tf_op jit(solution)/shard_map/ppermute | solution.py:567
  17.3 6.6 %collective-permute-done.refs_1_ = bf16[64,1536]{1,0:T(8,128)(2,1)S(1)} collective-permute-done((bf16[64,1536]{1,0:T(8,128)(2,1)S(1)}, bf16[64,1536]{1,0:T(8,128)(2,1)S(1)}, u32[]{:S(2)}, u32[]{:S(2)}) %collective-permute-start) | collective-permute-done | bytes 196640 | tf_op jit(solution)/shard_map/ppermute | solution.py:567
  23.9 7.7 %collective-permute-done.1.refs_2_ = bf16[64,1536]{1,0:T(8,128)(2,1)S(1)} collective-permute-done((bf16[64,1536]{1,0:T(8,128)(2,1)S(1)}, bf16[64,1536]{1,0:T(8,128)(2,1)S(1)}, u32[]{:S(2)}, u32[]{:S(2)}) %collective-permute-start.1) | collective-permute-done | bytes 196640 | tf_op jit(solution)/shard_map/ppermute | solution.py:567
  31.6 6.3 %all-to-all-start.1 = ((bf16[4,64,1536]{2,1,0:T(8,128)(2,1)}), bf16[4,64,1536]{2,1,0:T(8,128)(2,1)S(1)}, u32[]{:S(2)}, u32[]{:S(2)}) async-start(bf16[4,64,1536]{2,1,0:T(8,128)(2,1)} %bitcast.4), calls=%async_computation.1 | async-start | bytes 1572864 | tf_op jit(solution)/shard_map/all_to_all | solution.py:561
  37.9 2.1 assemble.2.here_ref
  40.0 1.3 collective-permute-start.3
  41.4 1.3 collective-permute-start.4
  42.7 7.5 %sort_obs.3 = (bf16[1,80,2048]{2,1,0:T(8,128)(2,1)}, s32[1,1,2048]{2,1,0:T(1,128)}, s32[8]{0:T(128)}, s32[8]{0:T(128)}) custom-call(s32[1]{0:T(128)} %bitcast.1.place_ref, bf16[8,80,1024]{2,1,0:T(8,128)(2,1)} %copy-done), custom_call_target="tpu_custom_call" | custom-call | flops 1000 | bytes 1000 | tf_op jit(solution)/shard_map/sort_obs/pallas_call | solution.py:254
  50.2 7.3 %all-to-all-done.1 = bf16[4,64,1536]{2,1,0:T(8,128)(2,1)S(1)} async-done(((bf16[4,64,1536]{2,1,0:T(8,128)(2,1)}), bf16[4,64,1536]{2,1,0:T(8,128)(2,1)S(1)}, u32[]{:S(2)}, u32[]{:S(2)}) %all-to-all-start.1) | async-done | bytes 786464 | tf_op jit(solution)/shard_map/all_to_all | solution.py:561
  57.5 2.2 collective-permute-start.5
  59.7 1.3 collective-permute-start.6
  61.0 0.8 copy-done.27
  62.1 6.1 %conv.4 = bf16[256,1536]{1,0:T(8,128)(2,1)} custom-call(s32[1]{0:T(128)} %bitcast.place_ref, bf16[3,768,256]{2,1,0:T(8,128)(2,1)} %bitcast.23, bf16[256,1536]{1,0:T(8,128)(2,1)} %copy-done.27, bf16[256,1536]{1,0:T(8,128)(2,1)} %assemble.2.here_ref, bf16[256,1536]{1,0:T(8,128)(2,1)} %copy-done.29), custom_call_target="tpu_custom_call" | custom-call | flops 7000000000 | bytes 1000 | tf_op jit(solution)/shard_map/conv/pallas_call | solution.py:164
  68.2 3.7 %all-to-all-start.2 = ((bf16[4,64,1536]{2,1,0:T(8,128)(2,1)}), bf16[4,64,1536]{2,1,0:T(8,128)(2,1)S(1)}, u32[]{:S(2)}, u32[]{:S(2)}) async-start(bf16[4,64,1536]{2,1,0:T(8,128)(2,1)} %bitcast.35), calls=%async_computation.2 | async-start | bytes 1572864 | tf_op jit(solution)/shard_map/all_to_all | solution.py:561
  71.9 7.5 %sort_obs.4 = (bf16[1,80,2048]{2,1,0:T(8,128)(2,1)}, s32[1,1,2048]{2,1,0:T(1,128)}, s32[8]{0:T(128)}, s32[8]{0:T(128)}) custom-call(s32[1]{0:T(128)} %bitcast.1.place_ref, bf16[8,80,1024]{2,1,0:T(8,128)(2,1)} %copy-done), custom_call_target="tpu_custom_call" | custom-call | flops 1000 | bytes 1000 | tf_op jit(solution)/shard_map/sort_obs/pallas_call | solution.py:254
  79.4 5.9 %conv.5 = (bf16[64,1536]{1,0:T(8,128)(2,1)}, bf16[64,1536]{1,0:T(8,128)(2,1)}, bf16[64,1536]{1,0:T(8,128)(2,1)}, bf16[64,1536]{1,0:T(8,128)(2,1)}) custom-call(s32[1]{0:T(128)} %bitcast.place_ref, bf16[3,768,256]{2,1,0:T(8,128)(2,1)} %bitcast.24, bf16[256,1536]{1,0:T(8,128)(2,1)} %collective-permute-done.5.below_ref, bf16[256,1536]{1,0:T(8,128)(2,1)} %bitcast.33, ...), custom_call_target="tpu_custom_call" | custom-call | flops 7000000000 | bytes 1000 | tf_op jit(solution)/shard_map/conv/pallas_call | solution.py:164
  85.4 1.8 collective-permute-start.7
  87.2 2.4 collective-permute-start.8
  89.8 0.7 copy.9.bias_ref
  90.5 13.1 %sort_obs.5 = (bf16[2,80,2048]{2,1,0:T(8,128)(2,1)}, s32[2,1,2048]{2,1,0:T(1,128)}, s32[16]{0:T(128)}, s32[16]{0:T(128)}) custom-call(s32[1]{0:T(128)} %bitcast.1.place_ref, bf16[8,80,1024]{2,1,0:T(8,128)(2,1)} %copy-done), custom_call_target="tpu_custom_call" | custom-call | flops 1000 | bytes 1000 | tf_op jit(solution)/shard_map/sort_obs/pallas_call | solution.py:254
  103.6 0.9 copy-done.1
  104.4 3.7 %activate.2 = (bf16[3072,128]{1,0:T(8,128)(2,1)}, f32[256,1536]{1,0:T(8,128)}) custom-call(s32[1]{0:T(128)} %bitcast.place_ref, f32[64,1]{1,0:T(8,128)} %copy.9.bias_ref, bf16[256,1536]{1,0:T(8,128)(2,1)} %bitcast.19), custom_call_target="tpu_custom_call" | custom-call | flops 1000 | bytes 1000 | tf_op jit(solution)/shard_map/activate/pallas_call | solution.py:365
  108.1 0.6 copy-done.6
  108.9 0.7 copy-done.8
  109.5 3.8 %activate.3 = (bf16[3072,128]{1,0:T(8,128)(2,1)}, f32[256,1536]{1,0:T(8,128)}) custom-call(s32[1]{0:T(128)} %bitcast.place_ref, f32[64,1]{1,0:T(8,128)} %copy.9.bias_ref, bf16[64,1536]{1,0:T(8,128)(2,1)} %get-tuple-element.91.refs_0_, bf16[64,1536]{1,0:T(8,128)(2,1)} %copy-done.6, bf16[64,1536]{1,0:T(8,128)(2,1)} %copy-done.7, bf16[64,1536]{1,0:T(8,128)(2,1)} %copy-done.8), custom_call_target="tpu_custom_call" | custom-call | flops 1000 | bytes 1000 | tf_op jit(solution)/shard_map/activate/pallas_call | solution.py:365
  113.3 20.6 %observe.1 = (bf16[64,1536]{1,0:T(8,128)(2,1)}, bf16[64,1536]{1,0:T(8,128)(2,1)}, bf16[64,1536]{1,0:T(8,128)(2,1)}, bf16[64,1536]{1,0:T(8,128)(2,1)}, bf16[256,1...) custom-call(s32[1]{0:T(128)} %bitcast.place_ref, s32[8]{0:T(128)} %get-tuple-element.77.refs_0_, ...), custom_call_target="tpu_custom_call" | custom-call | flops 1000 | bytes 1000 | tf_op jit(solution)/shard_map/observe/pallas_call | solution.py:534
  133.9 1.0 collective-permute-start.10
  134.9 3.3 %collective-permute-start.11 = (bf16[64,1536]{1,0:T(8,128)(2,1)}, bf16[64,1536]{1,0:T(8,128)(2,1)S(1)}, u32[]{:S(2)}, u32[]{:S(2)}) collective-permute-start(bf16[64,1536]{1,0:T(8,128)(2,1)} %get-tuple-element.107), channel_id=1, source_target_pairs={{0,2},{1,3},{2,0},{3,1},{4,6},{5,7},{6,4},{7,5},{8,10},{9,11},{10,... | collective-permute-start | bytes 589832 | tf_op jit(solution)/shard_map/ppermute | solution.py:567
  138.4 1.5 collective-permute-done.10.refs_1_
  139.9 4.7 %collective-permute-done.11.refs_2_ = bf16[64,1536]{1,0:T(8,128)(2,1)S(1)} collective-permute-done((bf16[64,1536]{1,0:T(8,128)(2,1)}, bf16[64,1536]{1,0:T(8,128)(2,1)S(1)}, u32[]{:S(2)}, u32[]{:S(2)}) %collective-permute-start.11) | collective-permute-done | bytes 196640 | tf_op jit(solution)/shard_map/ppermute | solution.py:567
  144.5 4.0 %collective-permute-done.12.refs_3_ = bf16[64,1536]{1,0:T(8,128)(2,1)S(1)} collective-permute-done((bf16[64,1536]{1,0:T(8,128)(2,1)}, bf16[64,1536]{1,0:T(8,128)(2,1)S(1)}, u32[]{:S(2)}, u32[]{:S(2)}) %collective-permute-start.12) | collective-permute-done | bytes 196640 | tf_op jit(solution)/shard_map/ppermute | solution.py:567
  148.6 8.9 %all-to-all-start.3 = ((bf16[4,64,1536]{2,1,0:T(8,128)(2,1)}), bf16[4,64,1536]{2,1,0:T(8,128)(2,1)S(1)}, u32[]{:S(2)}, u32[]{:S(2)}) async-start(bf16[4,64,1536]{2,1,0:T(8,128)(2,1)} %bitcast.34), calls=%async_computation.3 | async-start | bytes 1572864 | tf_op jit(solution)/shard_map/all_to_all | solution.py:561
  157.5 2.2 assemble.3.here_ref
  159.6 4.6 %collective-permute-start.13 = (bf16[256,1536]{1,0:T(8,128)(2,1)}, bf16[256,1536]{1,0:T(8,128)(2,1)}, u32[]{:S(2)}, u32[]{:S(2)}) collective-permute-start(bf16[256,1536]{1,0:T(8,128)(2,1)} %assemble.3.here_ref), channel_id=1, source_target_pairs={{0,4},{4,8},{8,12},{12,16},{16,20},{20,24},{24,28},{1,5},{5,9},{9,... | collective-permute-start | bytes 2359304 | tf_op jit(solution)/shard_map/ppermute | solution.py:585
  164.2 1.3 collective-permute-start.14
  165.6 1.5 copy.11
  167.2 6.8 %unsort_obs.2 = (bf16[64,1024]{1,0:T(8,128)(2,1)}, bf16[64,1024]{1,0:T(8,128)(2,1)}, bf16[64,1024]{1,0:T(8,128)(2,1)}, bf16[64,1024]{1,0:T(8,128)(2,1)}) custom-call(bf16[4,64,2048]{2,1,0:T(8,128)(2,1)} %get-tuple-element.118.sorted_ref, s32[1,1,2048]{2,1,0:T(1,128)} %get-tuple-element.81.refs_0_, s32[1,1,2048]{2,1,0:T(1,128)} %get-tuple-element.88.refs_1_), custom_call_target="tpu_custom_call" | custom-call | flops 1000 | bytes 1000 | tf_op jit(solution)/shard_map/unsort_obs/pallas_call | solution.py:293
  174.0 4.2 %all-to-all-done.3 = bf16[4,64,1536]{2,1,0:T(8,128)(2,1)S(1)} async-done(((bf16[4,64,1536]{2,1,0:T(8,128)(2,1)}), bf16[4,64,1536]{2,1,0:T(8,128)(2,1)S(1)}, u32[]{:S(2)}, u32[]{:S(2)}) %all-to-all-start.3) | async-done | bytes 786464 | tf_op jit(solution)/shard_map/all_to_all | solution.py:561
  178.1 5.1 %collective-permute-start.15 = (bf16[256,1536]{1,0:T(8,128)(2,1)S(1)}, bf16[256,1536]{1,0:T(8,128)(2,1)S(1)}, u32[]{:S(2)}, u32[]{:S(2)}) collective-permute-start(bf16[256,1536]{1,0:T(8,128)(2,1)S(1)} %bitcast.28), channel_id=1, source_target_pairs={{0,4},{4,8},{8,12},{12,16},{16,20},{20,24},{24,28},{1,5},{5,9},{9,... | collective-permute-start | bytes 2359304 | tf_op jit(solution)/shard_map/ppermute | solution.py:585
  183.2 1.3 collective-permute-start.16
  184.6 6.1 %conv.6 = bf16[256,1536]{1,0:T(8,128)(2,1)} custom-call(s32[1]{0:T(128)} %bitcast.place_ref, bf16[3,768,256]{2,1,0:T(8,128)(2,1)} %bitcast.25, bf16[256,1536]{1,0:T(8,128)(2,1)} %collective-permute-done.13.below_ref, bf16[256,1536]{1,0:T(8,128)(2,1)} %assemble.3.here_ref, bf16[256,1536]{1,0:T(8,128)(2,1)} %collective-permute-done.14.above_ref), custom_call_target="tpu_custom_call" | custom-call | flops 7000000000 | bytes 1000 | tf_op jit(solution)/shard_map/conv/pallas_call | solution.py:164
  190.6 5.1 %all-to-all-start.4 = ((bf16[4,64,1536]{2,1,0:T(8,128)(2,1)}), bf16[4,64,1536]{2,1,0:T(8,128)(2,1)S(1)}, u32[]{:S(2)}, u32[]{:S(2)}) async-start(bf16[4,64,1536]{2,1,0:T(8,128)(2,1)} %bitcast.27), calls=%async_computation.4 | async-start | bytes 1572864 | tf_op jit(solution)/shard_map/all_to_all | solution.py:561
  195.7 6.8 %unsort_obs.3 = (bf16[64,1024]{1,0:T(8,128)(2,1)}, bf16[64,1024]{1,0:T(8,128)(2,1)}, bf16[64,1024]{1,0:T(8,128)(2,1)}, bf16[64,1024]{1,0:T(8,128)(2,1)}) custom-call(bf16[4,64,2048]{2,1,0:T(8,128)(2,1)} %get-tuple-element.118.sorted_ref, s32[2,1,2048]{2,1,0:T(1,128)} %get-tuple-element.119.refs_0_), custom_call_target="tpu_custom_call" | custom-call | flops 1000 | bytes 1000 | tf_op jit(solution)/shard_map/unsort_obs/pallas_call | solution.py:293
  202.6 0.9 copy-done.26
  203.4 0.9 copy-done.28
  204.3 5.9 %conv.7 = (bf16[64,1536]{1,0:T(8,128)(2,1)}, bf16[64,1536]{1,0:T(8,128)(2,1)}, bf16[64,1536]{1,0:T(8,128)(2,1)}, bf16[64,1536]{1,0:T(8,128)(2,1)}) custom-call(s32[1]{0:T(128)} %bitcast.place_ref, bf16[3,768,256]{2,1,0:T(8,128)(2,1)} %bitcast.26, bf16[256,1536]{1,0:T(8,128)(2,1)} %copy-done.26, bf16[256,1536]{1,0:T(8,128)(2,1)} %bitcast.30, ...), custom_call_target="tpu_custom_call" | custom-call | flops 7000000000 | bytes 1000 | tf_op jit(solution)/shard_map/conv/pallas_call | solution.py:164
  210.2 4.9 %collective-permute-start.17 = (bf16[64,1024]{1,0:T(8,128)(2,1)S(1)}, bf16[64,1024]{1,0:T(8,128)(2,1)S(1)}, u32[]{:S(2)}, u32[]{:S(2)}) collective-permute-start(bf16[64,1024]{1,0:T(8,128)(2,1)S(1)} %copy-done.37), channel_id=1, source_target_pairs={{0,4},{4,0},{8,12},{12,8},{16,20},{20,16},{24,28},{28,24},{1,5},{5... | collective-permute-start | bytes 393224 | tf_op jit(solution)/shard_map/ppermute | solution.py:567
  215.2 1.7 collective-permute-start.18
  217.1 1.6 collective-permute-start.21
  218.7 1.8 collective-permute-start.24
  220.5 1.0 collective-permute-done.18.refs_2_
  221.5 2.7 %collective-permute-start.25 = (bf16[64,1536]{1,0:T(8,128)(2,1)}, bf16[64,1536]{1,0:T(8,128)(2,1)S(1)}, u32[]{:S(2)}, u32[]{:S(2)}) collective-permute-start(bf16[64,1536]{1,0:T(8,128)(2,1)} %get-tuple-element.136), channel_id=1, source_target_pairs={{0,2},{1,3},{2,0},{3,1},{4,6},{5,7},{6,4},{7,5},{8,10},{9,11},{10,... | collective-permute-start | bytes 589832 | tf_op jit(solution)/shard_map/ppermute | solution.py:567
  224.2 3.1 %collective-permute-start.26 = (bf16[64,1536]{1,0:T(8,128)(2,1)}, bf16[64,1536]{1,0:T(8,128)(2,1)S(1)}, u32[]{:S(2)}, u32[]{:S(2)}) collective-permute-start(bf16[64,1536]{1,0:T(8,128)(2,1)} %get-tuple-element.137), channel_id=1, source_target_pairs={{0,3},{1,2},{2,1},{3,0},{4,7},{5,6},{6,5},{7,4},{8,11},{9,10},{10,... | collective-permute-start | bytes 589832 | tf_op jit(solution)/shard_map/ppermute | solution.py:567
  227.4 2.4 collective-permute-start.23
  229.8 4.8 %collective-permute-done.22.refs_6_ = bf16[64,1024]{1,0:T(8,128)(2,1)S(1)} collective-permute-done((bf16[64,1024]{1,0:T(8,128)(2,1)S(1)}, bf16[64,1024]{1,0:T(8,128)(2,1)S(1)}, u32[]{:S(2)}, u32[]{:S(2)}) %collective-permute-start.22) | collective-permute-done | bytes 131104 | tf_op jit(solution)/shard_map/ppermute | solution.py:567
  234.6 1.2 collective-permute-done.23.refs_7_
  235.9 0.6 copy-done.24
  236.5 3.4 %unpack_obs.1 = f32[512,1024]{1,0:T(8,128)} custom-call(s32[1]{0:T(128)} %bitcast.1.place_ref, bf16[64,1024]{1,0:T(8,128)(2,1)} %get-tuple-element.126.refs_0_, bf16[64,1024]{1,0:T(8,128)(2,1)} %copy-done.18, bf16[64,1024]{1,0:T(8,128)(2,1)} %copy-done.19, bf16[64,1024]{1,0:T(8,128)(2,1)} %copy-done.20, bf16[64,1024]{1,0:T(8,128)(2,1)} %copy-done.21, ...), custom_call_target="tpu_custom_call" | custom-call | flops 1000 | bytes 1000 | tf_op jit(solution)/shard_map/unpack_obs/pallas_call | solution.py:320
  240.0 0.6 copy-done.15
  241.0 3.6 %join_rows.1 = bf16[64,8,1440]{2,1,0:T(8,128)(2,1)} custom-call(s32[1]{0:T(128)} %bitcast.place_ref, bf16[256,1536]{1,0:T(8,128)(2,1)} %bitcast.20, bf16[64,1536]{1,0:T(8,128)(2,1)} %get-tuple-element.125.refs_1_, bf16[64,1536]{1,0:T(8,128)(2,1)} %copy-done.15, bf16[64,1536]{1,0:T(8,128)(2,1)} %copy-done.16, bf16[64,1536]{1,0:T(8,128)(2,1)} %copy-done.17), custom_call_target="tpu_custom_call" | custom-call | flops 1000 | bytes 1000 | tf_op jit(solution)/shard_map/join_rows/pallas_call | solution.py:103
  (101 shorter events, 2.0 us)
Async XLA Ops:
  7.5 5.3 %copy-start.32 = (bf16[64,1536]{1,0:T(8,128)(2,1)S(1)}, bf16[64,1536]{1,0:T(8,128)(2,1)}, u32[]{:S(2)}) copy-start(bf16[64,1536]{1,0:T(8,128)(2,1)} %get-tuple-element.72) | copy-start | bytes 589828
  7.5 7.0 %copy-start.31 = (bf16[64,1536]{1,0:T(8,128)(2,1)S(1)}, bf16[64,1536]{1,0:T(8,128)(2,1)}, u32[]{:S(2)}) copy-start(bf16[64,1536]{1,0:T(8,128)(2,1)} %get-tuple-element.73) | copy-start | bytes 589828
  7.5 9.6 %copy-start.30 = (bf16[64,1536]{1,0:T(8,128)(2,1)S(1)}, bf16[64,1536]{1,0:T(8,128)(2,1)}, u32[]{:S(2)}) copy-start(bf16[64,1536]{1,0:T(8,128)(2,1)} %get-tuple-element.74) | copy-start | bytes 589828
  7.5 24.1 %all-to-all-start = ((bf16[8,80,1024]{2,1,0:T(8,128)(2,1)}), bf16[8,80,1024]{2,1,0:T(8,128)(2,1)S(1)}, u32[]{:S(2)}, u32[]{:S(2)}) async-start(bf16[8,80,1024]{2,1,0:T(8,128)(2,1)} %pack_obs.1), calls=%async_computation | async-start | bytes 2621440 | tf_op jit(solution)/shard_map/all_to_all | solution.py:561
  12.8 11.1 %collective-permute-start = (bf16[64,1536]{1,0:T(8,128)(2,1)S(1)}, bf16[64,1536]{1,0:T(8,128)(2,1)S(1)}, u32[]{:S(2)}, u32[]{:S(2)}) collective-permute-start(bf16[64,1536]{1,0:T(8,128)(2,1)S(1)} %copy-done.32), channel_id=1, source_target_pairs={{0,1},{1,0},{2,3},{3,2},{4,5},{5,4},{6,7},{7,6},{8,9},{9,8},{10,11... | collective-permute-start | bytes 589832 | tf_op jit(solution)/shard_map/ppermute | solution.py:567
  14.5 17.1 %collective-permute-start.1 = (bf16[64,1536]{1,0:T(8,128)(2,1)S(1)}, bf16[64,1536]{1,0:T(8,128)(2,1)S(1)}, u32[]{:S(2)}, u32[]{:S(2)}) collective-permute-start(bf16[64,1536]{1,0:T(8,128)(2,1)S(1)} %copy-done.31), channel_id=1, source_target_pairs={{0,2},{1,3},{2,0},{3,1},{4,6},{5,7},{6,4},{7,5},{8,10},{9,11},{10,... | collective-permute-start | bytes 589832 | tf_op jit(solution)/shard_map/ppermute | solution.py:567
  17.1 14.5 %collective-permute-start.2 = (bf16[64,1536]{1,0:T(8,128)(2,1)S(1)}, bf16[64,1536]{1,0:T(8,128)(2,1)S(1)}, u32[]{:S(2)}, u32[]{:S(2)}) collective-permute-start(bf16[64,1536]{1,0:T(8,128)(2,1)S(1)} %copy-done.30), channel_id=1, source_target_pairs={{0,3},{1,2},{2,1},{3,0},{4,7},{5,6},{6,5},{7,4},{8,11},{9,10},{10,... | collective-permute-start | bytes 589832 | tf_op jit(solution)/shard_map/ppermute | solution.py:567
  23.9 14.0 %copy-start.9 = (bf16[64,1536]{1,0:T(8,128)(2,1)}, bf16[64,1536]{1,0:T(8,128)(2,1)S(1)}, u32[]{:S(2)}) copy-start(bf16[64,1536]{1,0:T(8,128)(2,1)S(1)} %collective-permute-done.refs_1_) | copy-start | bytes 589828
  31.6 6.3 %copy-start.10 = (bf16[64,1536]{1,0:T(8,128)(2,1)}, bf16[64,1536]{1,0:T(8,128)(2,1)S(1)}, u32[]{:S(2)}) copy-start(bf16[64,1536]{1,0:T(8,128)(2,1)S(1)} %collective-permute-done.1.refs_2_) | copy-start | bytes 589828
  31.6 6.3 %copy-start.11 = (bf16[64,1536]{1,0:T(8,128)(2,1)}, bf16[64,1536]{1,0:T(8,128)(2,1)S(1)}, u32[]{:S(2)}) copy-start(bf16[64,1536]{1,0:T(8,128)(2,1)S(1)} %collective-permute-done.2.refs_3_) | copy-start | bytes 589828
  31.6 8.4 %copy-start = (bf16[8,80,1024]{2,1,0:T(8,128)(2,1)}, bf16[8,80,1024]{2,1,0:T(8,128)(2,1)S(1)}, u32[]{:S(2)}) copy-start(bf16[8,80,1024]{2,1,0:T(8,128)(2,1)S(1)} %all-to-all-done.obs_ref) | copy-start | bytes 3932164
  31.6 25.9 %all-to-all-start.1 = ((bf16[4,64,1536]{2,1,0:T(8,128)(2,1)}), bf16[4,64,1536]{2,1,0:T(8,128)(2,1)S(1)}, u32[]{:S(2)}, u32[]{:S(2)}) async-start(bf16[4,64,1536]{2,1,0:T(8,128)(2,1)} %bitcast.4), calls=%async_computation.1 | async-start | bytes 1572864 | tf_op jit(solution)/shard_map/all_to_all | solution.py:561
  40.0 20.9 %collective-permute-start.3 = (bf16[256,1536]{1,0:T(8,128)(2,1)}, bf16[256,1536]{1,0:T(8,128)(2,1)S(1)}, u32[]{:S(2)}, u32[]{:S(2)}) collective-permute-start(bf16[256,1536]{1,0:T(8,128)(2,1)} %assemble.2.here_ref), channel_id=1, source_target_pairs={{0,4},{4,8},{8,12},{12,16},{16,20},{20,24},{24,28},{1,5},{5,9},{9,... | collective-permute-start | bytes 2359304 | tf_op jit(solution)/shard_map/ppermute | solution.py:585
  41.4 19.6 %collective-permute-start.4 = (bf16[256,1536]{1,0:T(8,128)(2,1)}, bf16[256,1536]{1,0:T(8,128)(2,1)S(1)}, u32[]{:S(2)}, u32[]{:S(2)}) collective-permute-start(bf16[256,1536]{1,0:T(8,128)(2,1)} %assemble.2.here_ref), channel_id=1, source_target_pairs={{4,0},{8,4},{12,8},{16,12},{20,16},{24,20},{28,24},{5,1},{9,5},{13... | collective-permute-start | bytes 2359304 | tf_op jit(solution)/shard_map/ppermute | solution.py:585
  57.5 10.7 %copy-start.5 = (bf16[4,64,1536]{2,1,0:T(8,128)(2,1)}, bf16[4,64,1536]{2,1,0:T(8,128)(2,1)S(1)}, u32[]{:S(2)}) copy-start(bf16[4,64,1536]{2,1,0:T(8,128)(2,1)S(1)} %all-to-all-done.1) | copy-start | bytes 2359300
  57.5 21.9 %collective-permute-start.5 = (bf16[256,1536]{1,0:T(8,128)(2,1)S(1)}, bf16[256,1536]{1,0:T(8,128)(2,1)}, u32[]{:S(2)}, u32[]{:S(2)}) collective-permute-start(bf16[256,1536]{1,0:T(8,128)(2,1)S(1)} %bitcast.31), channel_id=1, source_target_pairs={{0,4},{4,8},{8,12},{12,16},{16,20},{20,24},{24,28},{1,5},{5,9},{9,... | collective-permute-start | bytes 2359304 | tf_op jit(solution)/shard_map/ppermute | solution.py:585
  59.7 19.8 %collective-permute-start.6 = (bf16[256,1536]{1,0:T(8,128)(2,1)S(1)}, bf16[256,1536]{1,0:T(8,128)(2,1)}, u32[]{:S(2)}, u32[]{:S(2)}) collective-permute-start(bf16[256,1536]{1,0:T(8,128)(2,1)S(1)} %bitcast.32), channel_id=1, source_target_pairs={{4,0},{8,4},{12,8},{16,12},{20,16},{24,20},{28,24},{5,1},{9,5},{13... | collective-permute-start | bytes 2359304 | tf_op jit(solution)/shard_map/ppermute | solution.py:585
  61.0 0.9 copy-start.27
  61.0 1.1 copy-start.29
  68.2 35.3 %all-to-all-start.2 = ((bf16[4,64,1536]{2,1,0:T(8,128)(2,1)}), bf16[4,64,1536]{2,1,0:T(8,128)(2,1)S(1)}, u32[]{:S(2)}, u32[]{:S(2)}) async-start(bf16[4,64,1536]{2,1,0:T(8,128)(2,1)} %bitcast.35), calls=%async_computation.2 | async-start | bytes 1572864 | tf_op jit(solution)/shard_map/all_to_all | solution.py:561
  79.4 10.4 %copy-start.25 = (f32[64]{0:T(128)S(1)}, f32[64]{0:T(128)}, u32[]{:S(2)}) copy-start(f32[64]{0:T(128)} %param.9) | copy-start | bytes 772
  85.4 22.7 %collective-permute-start.7 = (bf16[64,1536]{1,0:T(8,128)(2,1)}, bf16[64,1536]{1,0:T(8,128)(2,1)S(1)}, u32[]{:S(2)}, u32[]{:S(2)}) collective-permute-start(bf16[64,1536]{1,0:T(8,128)(2,1)} %get-tuple-element.98), channel_id=1, source_target_pairs={{0,1},{1,0},{2,3},{3,2},{4,5},{5,4},{6,7},{7,6},{8,9},{9,8},{10,11... | collective-permute-start | bytes 589832 | tf_op jit(solution)/shard_map/ppermute | solution.py:567
  87.2 20.9 %collective-permute-start.8 = (bf16[64,1536]{1,0:T(8,128)(2,1)}, bf16[64,1536]{1,0:T(8,128)(2,1)S(1)}, u32[]{:S(2)}, u32[]{:S(2)}) collective-permute-start(bf16[64,1536]{1,0:T(8,128)(2,1)} %get-tuple-element.99), channel_id=1, source_target_pairs={{0,2},{1,3},{2,0},{3,1},{4,6},{5,7},{6,4},{7,5},{8,10},{9,11},{10,... | collective-permute-start | bytes 589832 | tf_op jit(solution)/shard_map/ppermute | solution.py:567
  89.5 18.6 %collective-permute-start.9 = (bf16[64,1536]{1,0:T(8,128)(2,1)}, bf16[64,1536]{1,0:T(8,128)(2,1)S(1)}, u32[]{:S(2)}, u32[]{:S(2)}) collective-permute-start(bf16[64,1536]{1,0:T(8,128)(2,1)} %get-tuple-element.100), channel_id=1, source_target_pairs={{0,3},{1,2},{2,1},{3,0},{4,7},{5,6},{6,5},{7,4},{8,11},{9,10},{10,... | collective-permute-start | bytes 589832 | tf_op jit(solution)/shard_map/ppermute | solution.py:567
  103.6 0.9 copy-start.1
  133.9 5.9 %collective-permute-start.10 = (bf16[64,1536]{1,0:T(8,128)(2,1)}, bf16[64,1536]{1,0:T(8,128)(2,1)S(1)}, u32[]{:S(2)}, u32[]{:S(2)}) collective-permute-start(bf16[64,1536]{1,0:T(8,128)(2,1)} %get-tuple-element.106), channel_id=1, source_target_pairs={{0,1},{1,0},{2,3},{3,2},{4,5},{5,4},{6,7},{7,6},{8,9},{9,8},{10,11... | collective-permute-start | bytes 589832 | tf_op jit(solution)/shard_map/ppermute | solution.py:567
  134.9 9.6 %collective-permute-start.11 = (bf16[64,1536]{1,0:T(8,128)(2,1)}, bf16[64,1536]{1,0:T(8,128)(2,1)S(1)}, u32[]{:S(2)}, u32[]{:S(2)}) collective-permute-start(bf16[64,1536]{1,0:T(8,128)(2,1)} %get-tuple-element.107), channel_id=1, source_target_pairs={{0,2},{1,3},{2,0},{3,1},{4,6},{5,7},{6,4},{7,5},{8,10},{9,11},{10,... | collective-permute-start | bytes 589832 | tf_op jit(solution)/shard_map/ppermute | solution.py:567
  138.2 10.4 %collective-permute-start.12 = (bf16[64,1536]{1,0:T(8,128)(2,1)}, bf16[64,1536]{1,0:T(8,128)(2,1)S(1)}, u32[]{:S(2)}, u32[]{:S(2)}) collective-permute-start(bf16[64,1536]{1,0:T(8,128)(2,1)} %get-tuple-element.108), channel_id=1, source_target_pairs={{0,3},{1,2},{2,1},{3,0},{4,7},{5,6},{6,5},{7,4},{8,11},{9,10},{10,... | collective-permute-start | bytes 589832 | tf_op jit(solution)/shard_map/ppermute | solution.py:567
  139.9 17.6 %copy-start.12 = (bf16[64,1536]{1,0:T(8,128)(2,1)}, bf16[64,1536]{1,0:T(8,128)(2,1)S(1)}, u32[]{:S(2)}) copy-start(bf16[64,1536]{1,0:T(8,128)(2,1)S(1)} %collective-permute-done.10.refs_1_) | copy-start | bytes 589828
  144.5 12.9 %copy-start.13 = (bf16[64,1536]{1,0:T(8,128)(2,1)}, bf16[64,1536]{1,0:T(8,128)(2,1)S(1)}, u32[]{:S(2)}) copy-start(bf16[64,1536]{1,0:T(8,128)(2,1)S(1)} %collective-permute-done.11.refs_2_) | copy-start | bytes 589828
  148.6 8.9 %copy-start.14 = (bf16[64,1536]{1,0:T(8,128)(2,1)}, bf16[64,1536]{1,0:T(8,128)(2,1)S(1)}, u32[]{:S(2)}) copy-start(bf16[64,1536]{1,0:T(8,128)(2,1)S(1)} %collective-permute-done.12.refs_3_) | copy-start | bytes 589828
  148.6 17.0 %copy-start.3 = (bf16[3,3,256,256]{3,2,1,0:T(8,128)(2,1)S(1)}, bf16[3,3,256,256]{3,2,1,0:T(8,128)(2,1)}, u32[]{:S(2)}) copy-start(bf16[3,3,256,256]{3,2,1,0:T(8,128)(2,1)} %param.8) | copy-start | bytes 3538948
  148.6 29.6 %all-to-all-start.3 = ((bf16[4,64,1536]{2,1,0:T(8,128)(2,1)}), bf16[4,64,1536]{2,1,0:T(8,128)(2,1)S(1)}, u32[]{:S(2)}, u32[]{:S(2)}) async-start(bf16[4,64,1536]{2,1,0:T(8,128)(2,1)} %bitcast.34), calls=%async_computation.3 | async-start | bytes 1572864 | tf_op jit(solution)/shard_map/all_to_all | solution.py:561
  159.6 24.9 %collective-permute-start.13 = (bf16[256,1536]{1,0:T(8,128)(2,1)}, bf16[256,1536]{1,0:T(8,128)(2,1)}, u32[]{:S(2)}, u32[]{:S(2)}) collective-permute-start(bf16[256,1536]{1,0:T(8,128)(2,1)} %assemble.3.here_ref), channel_id=1, source_target_pairs={{0,4},{4,8},{8,12},{12,16},{16,20},{20,24},{24,28},{1,5},{5,9},{9,... | collective-permute-start | bytes 2359304 | tf_op jit(solution)/shard_map/ppermute | solution.py:585
  164.2 20.3 %collective-permute-start.14 = (bf16[256,1536]{1,0:T(8,128)(2,1)}, bf16[256,1536]{1,0:T(8,128)(2,1)}, u32[]{:S(2)}, u32[]{:S(2)}) collective-permute-start(bf16[256,1536]{1,0:T(8,128)(2,1)} %assemble.3.here_ref), channel_id=1, source_target_pairs={{4,0},{8,4},{12,8},{16,12},{20,16},{24,20},{28,24},{5,1},{9,5},{13... | collective-permute-start | bytes 2359304 | tf_op jit(solution)/shard_map/ppermute | solution.py:585
  178.1 12.5 %copy-start.4 = (bf16[4,64,1536]{2,1,0:T(8,128)(2,1)}, bf16[4,64,1536]{2,1,0:T(8,128)(2,1)S(1)}, u32[]{:S(2)}) copy-start(bf16[4,64,1536]{2,1,0:T(8,128)(2,1)S(1)} %all-to-all-done.3) | copy-start | bytes 2359300
  178.1 24.4 %collective-permute-start.15 = (bf16[256,1536]{1,0:T(8,128)(2,1)S(1)}, bf16[256,1536]{1,0:T(8,128)(2,1)S(1)}, u32[]{:S(2)}, u32[]{:S(2)}) collective-permute-start(bf16[256,1536]{1,0:T(8,128)(2,1)S(1)} %bitcast.28), channel_id=1, source_target_pairs={{0,4},{4,8},{8,12},{12,16},{16,20},{20,24},{24,28},{1,5},{5,9},{9,... | collective-permute-start | bytes 2359304 | tf_op jit(solution)/shard_map/ppermute | solution.py:585
  183.2 19.3 %collective-permute-start.16 = (bf16[256,1536]{1,0:T(8,128)(2,1)S(1)}, bf16[256,1536]{1,0:T(8,128)(2,1)S(1)}, u32[]{:S(2)}, u32[]{:S(2)}) collective-permute-start(bf16[256,1536]{1,0:T(8,128)(2,1)S(1)} %bitcast.29), channel_id=1, source_target_pairs={{4,0},{8,4},{12,8},{16,12},{20,16},{24,20},{28,24},{5,1},{9,5},{13... | collective-permute-start | bytes 2359304 | tf_op jit(solution)/shard_map/ppermute | solution.py:585
  190.6 49.4 %all-to-all-start.4 = ((bf16[4,64,1536]{2,1,0:T(8,128)(2,1)}), bf16[4,64,1536]{2,1,0:T(8,128)(2,1)S(1)}, u32[]{:S(2)}, u32[]{:S(2)}) async-start(bf16[4,64,1536]{2,1,0:T(8,128)(2,1)} %bitcast.27), calls=%async_computation.4 | async-start | bytes 1572864 | tf_op jit(solution)/shard_map/all_to_all | solution.py:561
  202.5 7.8 %copy-start.37 = (bf16[64,1024]{1,0:T(8,128)(2,1)S(1)}, bf16[64,1024]{1,0:T(8,128)(2,1)}, u32[]{:S(2)}) copy-start(bf16[64,1024]{1,0:T(8,128)(2,1)} %get-tuple-element.127) | copy-start | bytes 393220
  202.5 12.7 %copy-start.34 = (bf16[64,1024]{1,0:T(8,128)(2,1)S(1)}, bf16[64,1024]{1,0:T(8,128)(2,1)}, u32[]{:S(2)}) copy-start(bf16[64,1024]{1,0:T(8,128)(2,1)} %get-tuple-element.128) | copy-start | bytes 393220
  202.5 14.4 %copy-start.33 = (bf16[64,1024]{1,0:T(8,128)(2,1)S(1)}, bf16[64,1024]{1,0:T(8,128)(2,1)}, u32[]{:S(2)}) copy-start(bf16[64,1024]{1,0:T(8,128)(2,1)} %get-tuple-element.129) | copy-start | bytes 393220
  202.5 14.5 %copy-start.39 = (bf16[64,1024]{1,0:T(8,128)(2,1)S(1)}, bf16[64,1024]{1,0:T(8,128)(2,1)}, u32[]{:S(2)}) copy-start(bf16[64,1024]{1,0:T(8,128)(2,1)} %get-tuple-element.130) | copy-start | bytes 393220
  202.5 14.6 %copy-start.38 = (bf16[64,1024]{1,0:T(8,128)(2,1)S(1)}, bf16[64,1024]{1,0:T(8,128)(2,1)}, u32[]{:S(2)}) copy-start(bf16[64,1024]{1,0:T(8,128)(2,1)} %get-tuple-element.131) | copy-start | bytes 393220
  202.5 24.8 %copy-start.36 = (bf16[64,1024]{1,0:T(8,128)(2,1)S(1)}, bf16[64,1024]{1,0:T(8,128)(2,1)}, u32[]{:S(2)}) copy-start(bf16[64,1024]{1,0:T(8,128)(2,1)} %get-tuple-element.132) | copy-start | bytes 393220
  202.5 24.9 %copy-start.35 = (bf16[64,1024]{1,0:T(8,128)(2,1)S(1)}, bf16[64,1024]{1,0:T(8,128)(2,1)}, u32[]{:S(2)}) copy-start(bf16[64,1024]{1,0:T(8,128)(2,1)} %get-tuple-element.133) | copy-start | bytes 393220
  203.4 0.9 copy-start.28
  210.2 8.5 %collective-permute-start.17 = (bf16[64,1024]{1,0:T(8,128)(2,1)S(1)}, bf16[64,1024]{1,0:T(8,128)(2,1)S(1)}, u32[]{:S(2)}, u32[]{:S(2)}) collective-permute-start(bf16[64,1024]{1,0:T(8,128)(2,1)S(1)} %copy-done.37), channel_id=1, source_target_pairs={{0,4},{4,0},{8,12},{12,8},{16,20},{20,16},{24,28},{28,24},{1,5},{5... | collective-permute-start | bytes 393224 | tf_op jit(solution)/shard_map/ppermute | solution.py:567
  215.2 6.3 %collective-permute-start.18 = (bf16[64,1024]{1,0:T(8,128)(2,1)S(1)}, bf16[64,1024]{1,0:T(8,128)(2,1)S(1)}, u32[]{:S(2)}, u32[]{:S(2)}) collective-permute-start(bf16[64,1024]{1,0:T(8,128)(2,1)S(1)} %copy-done.34), channel_id=1, source_target_pairs={{0,8},{4,12},{8,0},{12,4},{16,24},{20,28},{24,16},{28,20},{1,9},{5... | collective-permute-start | bytes 393224 | tf_op jit(solution)/shard_map/ppermute | solution.py:567
  216.9 7.3 %collective-permute-start.19 = (bf16[64,1024]{1,0:T(8,128)(2,1)S(1)}, bf16[64,1024]{1,0:T(8,128)(2,1)S(1)}, u32[]{:S(2)}, u32[]{:S(2)}) collective-permute-start(bf16[64,1024]{1,0:T(8,128)(2,1)S(1)} %copy-done.33), channel_id=1, source_target_pairs={{0,12},{4,8},{8,4},{12,0},{16,28},{20,24},{24,20},{28,16},{1,13},{... | collective-permute-start | bytes 393224 | tf_op jit(solution)/shard_map/ppermute | solution.py:567
  217.0 10.3 %collective-permute-start.20 = (bf16[64,1024]{1,0:T(8,128)(2,1)S(1)}, bf16[64,1024]{1,0:T(8,128)(2,1)S(1)}, u32[]{:S(2)}, u32[]{:S(2)}) collective-permute-start(bf16[64,1024]{1,0:T(8,128)(2,1)S(1)} %copy-done.39), channel_id=1, source_target_pairs={{0,16},{4,20},{8,24},{12,28},{16,0},{20,4},{24,8},{28,12},{1,17},{... | collective-permute-start | bytes 393224 | tf_op jit(solution)/shard_map/ppermute | solution.py:567
  217.1 10.2 %collective-permute-start.21 = (bf16[64,1024]{1,0:T(8,128)(2,1)S(1)}, bf16[64,1024]{1,0:T(8,128)(2,1)S(1)}, u32[]{:S(2)}, u32[]{:S(2)}) collective-permute-start(bf16[64,1024]{1,0:T(8,128)(2,1)S(1)} %copy-done.38), channel_id=1, source_target_pairs={{0,20},{4,16},{8,28},{12,24},{16,4},{20,0},{24,12},{28,8},{1,21},{... | collective-permute-start | bytes 393224 | tf_op jit(solution)/shard_map/ppermute | solution.py:567
  218.7 17.1 %copy-start.18 = (bf16[64,1024]{1,0:T(8,128)(2,1)}, bf16[64,1024]{1,0:T(8,128)(2,1)S(1)}, u32[]{:S(2)}) copy-start(bf16[64,1024]{1,0:T(8,128)(2,1)S(1)} %collective-permute-done.17.refs_1_) | copy-start | bytes 393220
  218.7 21.2 %collective-permute-start.24 = (bf16[64,1536]{1,0:T(8,128)(2,1)}, bf16[64,1536]{1,0:T(8,128)(2,1)S(1)}, u32[]{:S(2)}, u32[]{:S(2)}) collective-permute-start(bf16[64,1536]{1,0:T(8,128)(2,1)} %get-tuple-element.135), channel_id=1, source_target_pairs={{0,1},{1,0},{2,3},{3,2},{4,5},{5,4},{6,7},{7,6},{8,9},{9,8},{10,11... | collective-permute-start | bytes 589832 | tf_op jit(solution)/shard_map/ppermute | solution.py:567
  221.5 14.3 %copy-start.19 = (bf16[64,1024]{1,0:T(8,128)(2,1)}, bf16[64,1024]{1,0:T(8,128)(2,1)S(1)}, u32[]{:S(2)}) copy-start(bf16[64,1024]{1,0:T(8,128)(2,1)S(1)} %collective-permute-done.18.refs_2_) | copy-start | bytes 393220
  221.5 18.4 %collective-permute-start.25 = (bf16[64,1536]{1,0:T(8,128)(2,1)}, bf16[64,1536]{1,0:T(8,128)(2,1)S(1)}, u32[]{:S(2)}, u32[]{:S(2)}) collective-permute-start(bf16[64,1536]{1,0:T(8,128)(2,1)} %get-tuple-element.136), channel_id=1, source_target_pairs={{0,2},{1,3},{2,0},{3,1},{4,6},{5,7},{6,4},{7,5},{8,10},{9,11},{10,... | collective-permute-start | bytes 589832 | tf_op jit(solution)/shard_map/ppermute | solution.py:567
  224.2 11.7 %copy-start.20 = (bf16[64,1024]{1,0:T(8,128)(2,1)}, bf16[64,1024]{1,0:T(8,128)(2,1)S(1)}, u32[]{:S(2)}) copy-start(bf16[64,1024]{1,0:T(8,128)(2,1)S(1)} %collective-permute-done.19.refs_3_) | copy-start | bytes 393220
  224.2 15.8 %collective-permute-start.26 = (bf16[64,1536]{1,0:T(8,128)(2,1)}, bf16[64,1536]{1,0:T(8,128)(2,1)S(1)}, u32[]{:S(2)}, u32[]{:S(2)}) collective-permute-start(bf16[64,1536]{1,0:T(8,128)(2,1)} %get-tuple-element.137), channel_id=1, source_target_pairs={{0,3},{1,2},{2,1},{3,0},{4,7},{5,6},{6,5},{7,4},{8,11},{9,10},{10,... | collective-permute-start | bytes 589832 | tf_op jit(solution)/shard_map/ppermute | solution.py:567
  227.3 8.6 %copy-start.21 = (bf16[64,1024]{1,0:T(8,128)(2,1)}, bf16[64,1024]{1,0:T(8,128)(2,1)S(1)}, u32[]{:S(2)}) copy-start(bf16[64,1024]{1,0:T(8,128)(2,1)S(1)} %collective-permute-done.20.refs_4_) | copy-start | bytes 393220
  227.3 7.3 %collective-permute-start.22 = (bf16[64,1024]{1,0:T(8,128)(2,1)S(1)}, bf16[64,1024]{1,0:T(8,128)(2,1)S(1)}, u32[]{:S(2)}, u32[]{:S(2)}) collective-permute-start(bf16[64,1024]{1,0:T(8,128)(2,1)S(1)} %copy-done.36), channel_id=1, source_target_pairs={{0,24},{4,28},{8,16},{12,20},{16,8},{20,12},{24,0},{28,4},{1,25},{... | collective-permute-start | bytes 393224 | tf_op jit(solution)/shard_map/ppermute | solution.py:567
  227.4 8.5 %copy-start.22 = (bf16[64,1024]{1,0:T(8,128)(2,1)}, bf16[64,1024]{1,0:T(8,128)(2,1)S(1)}, u32[]{:S(2)}) copy-start(bf16[64,1024]{1,0:T(8,128)(2,1)S(1)} %collective-permute-done.21.refs_5_) | copy-start | bytes 393220
  227.4 8.4 %collective-permute-start.23 = (bf16[64,1024]{1,0:T(8,128)(2,1)S(1)}, bf16[64,1024]{1,0:T(8,128)(2,1)S(1)}, u32[]{:S(2)}, u32[]{:S(2)}) collective-permute-start(bf16[64,1024]{1,0:T(8,128)(2,1)S(1)} %copy-done.35), channel_id=1, source_target_pairs={{0,28},{4,24},{8,20},{12,16},{16,12},{20,8},{24,4},{28,0},{1,29},{... | collective-permute-start | bytes 393224 | tf_op jit(solution)/shard_map/ppermute | solution.py:567
  234.6 1.3 copy-start.23
  240.0 1.0 copy-start.2
  (8 other events, 5.8 us)

commit v5 on v4

--- a/solution.py
+++ b/solution.py
@@ -136,7 +136,7 @@
 def conv_kernel(place_ref, weights_ref, below_ref, here_ref, above_ref, *refs):
     outs, sums_ref = refs[:-1], refs[-1]
     total, wide = here_ref.shape
-    columns = 4 * LANES
+    columns = wide // 2 if wide % (4 * LANES) == 0 else LANES
     share = total // max(len(outs), 4)
 
     @pl.loop(0, wide // columns)

time: 245 us -> 243 us (level)
  starting transfers between devices: 79.3 us -> 73.8 us
    ppermute x4, starting transfers between devices: 13.2 us -> 9.75 us  [mix(): lax.ppermute(here, 'lat', forward)]
  transfers between devices with their start and end apart: 32 -> 32, of which waited for: 10 -> 10; matrix products, arithmetic and copies ran while one was open for 1% -> 1% of each run, Pallas kernels for 31% -> 32%
where the time goes in v5:
time: 243 us; the launch traced here: 241 us
  Pallas kernels  112 us (46%)
  starting transfers between devices  73.8 us (30%)
  waiting for transfers between devices  45 us (19%)
  local copies, waits for them, and re-layouts  9.28 us (4%)
    ppermute x19, waiting for transfers between devices, swap(): lax.ppermute(pieces[k], axis, [(i, i ^ k) for i in range(count)])  32.6 us
    ppermute x19, starting transfers between devices, swap(): lax.ppermute(pieces[k], axis, [(i, i ^ k) for i in range(count)])  31.4 us
    pallas_call x3, Pallas kernels, sort_obs(): pl.pallas_call(functools.partial(sort_obs_kernel, begin), out_shape=[jax....  28.1 us
    all_to_all x5, starting transfers between devices, turn_over(): return lax.all_to_all(block, axis, split_axis=0, concat_axis=0, tiled=True)  27.5 us
    pallas_call x4, Pallas kernels, conv(): pl.pallas_call(conv_kernel, out_shape=[jax.ShapeDtypeStruct((total // par...  23.4 us
    pallas_call x1, Pallas kernels, observe(): pl.pallas_call(functools.partial(observe_kernel, parts, turns, width), ou...  21.3 us
    pallas_call x2, Pallas kernels, unsort_obs(): pl.pallas_call(functools.partial(unsort_obs_kernel, begin, count), out_sh...  13.6 us
    all_to_all x5, waiting for transfers between devices, turn_over(): return lax.all_to_all(block, axis, split_axis=0, concat_axis=0, tiled=True)  12.5 us
  transfers between devices with their start and end apart: 32, of which 10 were waited for; matrix products, arithmetic and copies ran while one was open for 1% of the time, Pallas kernels for 32%

profile of v5, /device:TPU:0, one launch (start us, length us, event | category | flops | bytes accessed | tf_op | source)
XLA Modules:
  0.0 241.2 jit_solution(16046098734270760992)
XLA Ops:
  0.6 3.3 %split_rows.1 = (bf16[64,1536]{1,0:T(8,128)(2,1)}, bf16[64,1536]{1,0:T(8,128)(2,1)}, bf16[64,1536]{1,0:T(8,128)(2,1)}, bf16[64,1536]{1,0:T(8,128)(2,1)}, bf16[256,1536]{1,0:T(8,128)(2,1)}) custom-call(s32[1]{0:T(128)} %bitcast.place_ref, bf16[64,8,1440]{2,1,0:T(8,128)(2,1)} %state_ref.1), custom_call_target="tpu_custom_call" | custom-call | flops 1000 | bytes 1000 | tf_op jit(solution)/shard_map/split_rows/pallas_call | solution.py:67
  3.9 3.6 %pack_obs.1 = bf16[8,80,1024]{2,1,0:T(8,128)(2,1)} custom-call(s32[1,8]{1,0:T(1,128)} %counts_ref, f32[512,1024]{1,0:T(8,128)} %bitcast.21, bf16[4,1,8,1024]{3,2,1,0:T(8,128)(2,1)} %weights_ref.1, s32[1,8,1024]{2,1,0:T(8,128)} %cells_ref.1), custom_call_target="tpu_custom_call" | custom-call | flops 1000 | bytes 1000 | tf_op jit(solution)/shard_map/pack_obs/pallas_call | solution.py:204
  7.5 5.3 %all-to-all-start = ((bf16[8,80,1024]{2,1,0:T(8,128)(2,1)}), bf16[8,80,1024]{2,1,0:T(8,128)(2,1)S(1)}, u32[]{:S(2)}, u32[]{:S(2)}) async-start(bf16[8,80,1024]{2,1,0:T(8,128)(2,1)} %pack_obs.1), calls=%async_computation | async-start | bytes 2621440 | tf_op jit(solution)/shard_map/all_to_all | solution.py:561
  12.8 1.6 collective-permute-start
  14.5 2.6 %collective-permute-start.1 = (bf16[64,1536]{1,0:T(8,128)(2,1)S(1)}, bf16[64,1536]{1,0:T(8,128)(2,1)S(1)}, u32[]{:S(2)}, u32[]{:S(2)}) collective-permute-start(bf16[64,1536]{1,0:T(8,128)(2,1)S(1)} %copy-done.31), channel_id=1, source_target_pairs={{0,2},{1,3},{2,0},{3,1},{4,6},{5,7},{6,4},{7,5},{8,10},{9,11},{10,... | collective-permute-start | bytes 589832 | tf_op jit(solution)/shard_map/ppermute | solution.py:567
  17.3 6.6 %collective-permute-done.refs_1_ = bf16[64,1536]{1,0:T(8,128)(2,1)S(1)} collective-permute-done((bf16[64,1536]{1,0:T(8,128)(2,1)S(1)}, bf16[64,1536]{1,0:T(8,128)(2,1)S(1)}, u32[]{:S(2)}, u32[]{:S(2)}) %collective-permute-start) | collective-permute-done | bytes 196640 | tf_op jit(solution)/shard_map/ppermute | solution.py:567
  23.9 7.7 %collective-permute-done.1.refs_2_ = bf16[64,1536]{1,0:T(8,128)(2,1)S(1)} collective-permute-done((bf16[64,1536]{1,0:T(8,128)(2,1)S(1)}, bf16[64,1536]{1,0:T(8,128)(2,1)S(1)}, u32[]{:S(2)}, u32[]{:S(2)}) %collective-permute-start.1) | collective-permute-done | bytes 196640 | tf_op jit(solution)/shard_map/ppermute | solution.py:567
  31.6 6.3 %all-to-all-start.1 = ((bf16[4,64,1536]{2,1,0:T(8,128)(2,1)}), bf16[4,64,1536]{2,1,0:T(8,128)(2,1)S(1)}, u32[]{:S(2)}, u32[]{:S(2)}) async-start(bf16[4,64,1536]{2,1,0:T(8,128)(2,1)} %bitcast.4), calls=%async_computation.1 | async-start | bytes 1572864 | tf_op jit(solution)/shard_map/all_to_all | solution.py:561
  37.9 2.1 assemble.2.here_ref
  40.0 1.3 collective-permute-start.3
  41.4 1.3 collective-permute-start.4
  42.7 7.5 %sort_obs.3 = (bf16[1,80,2048]{2,1,0:T(8,128)(2,1)}, s32[1,1,2048]{2,1,0:T(1,128)}, s32[8]{0:T(128)}, s32[8]{0:T(128)}) custom-call(s32[1]{0:T(128)} %bitcast.1.place_ref, bf16[8,80,1024]{2,1,0:T(8,128)(2,1)} %copy-done), custom_call_target="tpu_custom_call" | custom-call | flops 1000 | bytes 1000 | tf_op jit(solution)/shard_map/sort_obs/pallas_call | solution.py:254
  50.2 7.3 %all-to-all-done.1 = bf16[4,64,1536]{2,1,0:T(8,128)(2,1)S(1)} async-done(((bf16[4,64,1536]{2,1,0:T(8,128)(2,1)}), bf16[4,64,1536]{2,1,0:T(8,128)(2,1)S(1)}, u32[]{:S(2)}, u32[]{:S(2)}) %all-to-all-start.1) | async-done | bytes 786464 | tf_op jit(solution)/shard_map/all_to_all | solution.py:561
  57.5 2.2 collective-permute-start.5
  59.7 1.3 collective-permute-start.6
  61.0 0.8 copy-done.27
  62.1 5.9 %conv.4 = bf16[256,1536]{1,0:T(8,128)(2,1)} custom-call(s32[1]{0:T(128)} %bitcast.place_ref, bf16[3,768,256]{2,1,0:T(8,128)(2,1)} %bitcast.23, bf16[256,1536]{1,0:T(8,128)(2,1)} %copy-done.27, bf16[256,1536]{1,0:T(8,128)(2,1)} %assemble.2.here_ref, bf16[256,1536]{1,0:T(8,128)(2,1)} %copy-done.29), custom_call_target="tpu_custom_call" | custom-call | flops 7000000000 | bytes 1000 | tf_op jit(solution)/shard_map/conv/pallas_call | solution.py:164
  68.1 3.7 %all-to-all-start.2 = ((bf16[4,64,1536]{2,1,0:T(8,128)(2,1)}), bf16[4,64,1536]{2,1,0:T(8,128)(2,1)S(1)}, u32[]{:S(2)}, u32[]{:S(2)}) async-start(bf16[4,64,1536]{2,1,0:T(8,128)(2,1)} %bitcast.35), calls=%async_computation.2 | async-start | bytes 1572864 | tf_op jit(solution)/shard_map/all_to_all | solution.py:561
  71.7 7.5 %sort_obs.4 = (bf16[1,80,2048]{2,1,0:T(8,128)(2,1)}, s32[1,1,2048]{2,1,0:T(1,128)}, s32[8]{0:T(128)}, s32[8]{0:T(128)}) custom-call(s32[1]{0:T(128)} %bitcast.1.place_ref, bf16[8,80,1024]{2,1,0:T(8,128)(2,1)} %copy-done), custom_call_target="tpu_custom_call" | custom-call | flops 1000 | bytes 1000 | tf_op jit(solution)/shard_map/sort_obs/pallas_call | solution.py:254
  79.3 5.8 %conv.5 = (bf16[64,1536]{1,0:T(8,128)(2,1)}, bf16[64,1536]{1,0:T(8,128)(2,1)}, bf16[64,1536]{1,0:T(8,128)(2,1)}, bf16[64,1536]{1,0:T(8,128)(2,1)}) custom-call(s32[1]{0:T(128)} %bitcast.place_ref, bf16[3,768,256]{2,1,0:T(8,128)(2,1)} %bitcast.24, bf16[256,1536]{1,0:T(8,128)(2,1)} %collective-permute-done.5.below_ref, bf16[256,1536]{1,0:T(8,128)(2,1)} %bitcast.33, ...), custom_call_target="tpu_custom_call" | custom-call | flops 7000000000 | bytes 1000 | tf_op jit(solution)/shard_map/conv/pallas_call | solution.py:164
  85.1 1.8 collective-permute-start.7
  86.9 2.4 collective-permute-start.8
  89.5 0.7 copy.9.bias_ref
  90.2 13.1 %sort_obs.5 = (bf16[2,80,2048]{2,1,0:T(8,128)(2,1)}, s32[2,1,2048]{2,1,0:T(1,128)}, s32[16]{0:T(128)}, s32[16]{0:T(128)}) custom-call(s32[1]{0:T(128)} %bitcast.1.place_ref, bf16[8,80,1024]{2,1,0:T(8,128)(2,1)} %copy-done), custom_call_target="tpu_custom_call" | custom-call | flops 1000 | bytes 1000 | tf_op jit(solution)/shard_map/sort_obs/pallas_call | solution.py:254
  103.3 0.9 copy-done.1
  104.2 3.7 %activate.2 = (bf16[3072,128]{1,0:T(8,128)(2,1)}, f32[256,1536]{1,0:T(8,128)}) custom-call(s32[1]{0:T(128)} %bitcast.place_ref, f32[64,1]{1,0:T(8,128)} %copy.9.bias_ref, bf16[256,1536]{1,0:T(8,128)(2,1)} %bitcast.19), custom_call_target="tpu_custom_call" | custom-call | flops 1000 | bytes 1000 | tf_op jit(solution)/shard_map/activate/pallas_call | solution.py:365
  107.9 0.6 copy-done.6
  108.6 0.7 copy-done.8
  109.3 3.8 %activate.3 = (bf16[3072,128]{1,0:T(8,128)(2,1)}, f32[256,1536]{1,0:T(8,128)}) custom-call(s32[1]{0:T(128)} %bitcast.place_ref, f32[64,1]{1,0:T(8,128)} %copy.9.bias_ref, bf16[64,1536]{1,0:T(8,128)(2,1)} %get-tuple-element.91.refs_0_, bf16[64,1536]{1,0:T(8,128)(2,1)} %copy-done.6, bf16[64,1536]{1,0:T(8,128)(2,1)} %copy-done.7, bf16[64,1536]{1,0:T(8,128)(2,1)} %copy-done.8), custom_call_target="tpu_custom_call" | custom-call | flops 1000 | bytes 1000 | tf_op jit(solution)/shard_map/activate/pallas_call | solution.py:365
  113.0 21.3 %observe.1 = (bf16[64,1536]{1,0:T(8,128)(2,1)}, bf16[64,1536]{1,0:T(8,128)(2,1)}, bf16[64,1536]{1,0:T(8,128)(2,1)}, bf16[64,1536]{1,0:T(8,128)(2,1)}, bf16[256,1...) custom-call(s32[1]{0:T(128)} %bitcast.place_ref, s32[8]{0:T(128)} %get-tuple-element.77.refs_0_, ...), custom_call_target="tpu_custom_call" | custom-call | flops 1000 | bytes 1000 | tf_op jit(solution)/shard_map/observe/pallas_call | solution.py:534
  134.3 1.0 collective-permute-start.10
  135.3 3.3 %collective-permute-start.11 = (bf16[64,1536]{1,0:T(8,128)(2,1)}, bf16[64,1536]{1,0:T(8,128)(2,1)S(1)}, u32[]{:S(2)}, u32[]{:S(2)}) collective-permute-start(bf16[64,1536]{1,0:T(8,128)(2,1)} %get-tuple-element.107), channel_id=1, source_target_pairs={{0,2},{1,3},{2,0},{3,1},{4,6},{5,7},{6,4},{7,5},{8,10},{9,11},{10,... | collective-permute-start | bytes 589832 | tf_op jit(solution)/shard_map/ppermute | solution.py:567
  138.8 1.5 collective-permute-done.10.refs_1_
  140.3 3.9 %collective-permute-done.11.refs_2_ = bf16[64,1536]{1,0:T(8,128)(2,1)S(1)} collective-permute-done((bf16[64,1536]{1,0:T(8,128)(2,1)}, bf16[64,1536]{1,0:T(8,128)(2,1)S(1)}, u32[]{:S(2)}, u32[]{:S(2)}) %collective-permute-start.11) | collective-permute-done | bytes 196640 | tf_op jit(solution)/shard_map/ppermute | solution.py:567
  144.2 5.6 %collective-permute-done.12.refs_3_ = bf16[64,1536]{1,0:T(8,128)(2,1)S(1)} collective-permute-done((bf16[64,1536]{1,0:T(8,128)(2,1)}, bf16[64,1536]{1,0:T(8,128)(2,1)S(1)}, u32[]{:S(2)}, u32[]{:S(2)}) %collective-permute-start.12) | collective-permute-done | bytes 196640 | tf_op jit(solution)/shard_map/ppermute | solution.py:567
  149.8 8.5 %all-to-all-start.3 = ((bf16[4,64,1536]{2,1,0:T(8,128)(2,1)}), bf16[4,64,1536]{2,1,0:T(8,128)(2,1)S(1)}, u32[]{:S(2)}, u32[]{:S(2)}) async-start(bf16[4,64,1536]{2,1,0:T(8,128)(2,1)} %bitcast.34), calls=%async_computation.3 | async-start | bytes 1572864 | tf_op jit(solution)/shard_map/all_to_all | solution.py:561
  158.3 2.2 assemble.3.here_ref
  160.5 4.2 %collective-permute-start.13 = (bf16[256,1536]{1,0:T(8,128)(2,1)}, bf16[256,1536]{1,0:T(8,128)(2,1)}, u32[]{:S(2)}, u32[]{:S(2)}) collective-permute-start(bf16[256,1536]{1,0:T(8,128)(2,1)} %assemble.3.here_ref), channel_id=1, source_target_pairs={{0,4},{4,8},{8,12},{12,16},{16,20},{20,24},{24,28},{1,5},{5,9},{9,... | collective-permute-start | bytes 2359304 | tf_op jit(solution)/shard_map/ppermute | solution.py:585
  164.7 1.3 collective-permute-start.14
  166.1 1.5 copy.11
  167.6 6.8 %unsort_obs.2 = (bf16[64,1024]{1,0:T(8,128)(2,1)}, bf16[64,1024]{1,0:T(8,128)(2,1)}, bf16[64,1024]{1,0:T(8,128)(2,1)}, bf16[64,1024]{1,0:T(8,128)(2,1)}) custom-call(bf16[4,64,2048]{2,1,0:T(8,128)(2,1)} %get-tuple-element.118.sorted_ref, s32[1,1,2048]{2,1,0:T(1,128)} %get-tuple-element.81.refs_0_, s32[1,1,2048]{2,1,0:T(1,128)} %get-tuple-element.88.refs_1_), custom_call_target="tpu_custom_call" | custom-call | flops 1000 | bytes 1000 | tf_op jit(solution)/shard_map/unsort_obs/pallas_call | solution.py:293
  174.4 5.1 %all-to-all-done.3 = bf16[4,64,1536]{2,1,0:T(8,128)(2,1)S(1)} async-done(((bf16[4,64,1536]{2,1,0:T(8,128)(2,1)}), bf16[4,64,1536]{2,1,0:T(8,128)(2,1)S(1)}, u32[]{:S(2)}, u32[]{:S(2)}) %all-to-all-start.3) | async-done | bytes 786464 | tf_op jit(solution)/shard_map/all_to_all | solution.py:561
  179.5 2.1 collective-permute-start.15
  181.6 1.3 collective-permute-start.16
  183.0 5.9 %conv.6 = bf16[256,1536]{1,0:T(8,128)(2,1)} custom-call(s32[1]{0:T(128)} %bitcast.place_ref, bf16[3,768,256]{2,1,0:T(8,128)(2,1)} %bitcast.25, bf16[256,1536]{1,0:T(8,128)(2,1)} %collective-permute-done.13.below_ref, bf16[256,1536]{1,0:T(8,128)(2,1)} %assemble.3.here_ref, bf16[256,1536]{1,0:T(8,128)(2,1)} %collective-permute-done.14.above_ref), custom_call_target="tpu_custom_call" | custom-call | flops 7000000000 | bytes 1000 | tf_op jit(solution)/shard_map/conv/pallas_call | solution.py:164
  188.9 3.8 %all-to-all-start.4 = ((bf16[4,64,1536]{2,1,0:T(8,128)(2,1)}), bf16[4,64,1536]{2,1,0:T(8,128)(2,1)S(1)}, u32[]{:S(2)}, u32[]{:S(2)}) async-start(bf16[4,64,1536]{2,1,0:T(8,128)(2,1)} %bitcast.27), calls=%async_computation.4 | async-start | bytes 1572864 | tf_op jit(solution)/shard_map/all_to_all | solution.py:561
  192.6 6.8 %unsort_obs.3 = (bf16[64,1024]{1,0:T(8,128)(2,1)}, bf16[64,1024]{1,0:T(8,128)(2,1)}, bf16[64,1024]{1,0:T(8,128)(2,1)}, bf16[64,1024]{1,0:T(8,128)(2,1)}) custom-call(bf16[4,64,2048]{2,1,0:T(8,128)(2,1)} %get-tuple-element.118.sorted_ref, s32[2,1,2048]{2,1,0:T(1,128)} %get-tuple-element.119.refs_0_), custom_call_target="tpu_custom_call" | custom-call | flops 1000 | bytes 1000 | tf_op jit(solution)/shard_map/unsort_obs/pallas_call | solution.py:293
  199.5 0.9 copy-done.26
  200.4 0.9 copy-done.28
  201.3 5.8 %conv.7 = (bf16[64,1536]{1,0:T(8,128)(2,1)}, bf16[64,1536]{1,0:T(8,128)(2,1)}, bf16[64,1536]{1,0:T(8,128)(2,1)}, bf16[64,1536]{1,0:T(8,128)(2,1)}) custom-call(s32[1]{0:T(128)} %bitcast.place_ref, bf16[3,768,256]{2,1,0:T(8,128)(2,1)} %bitcast.26, bf16[256,1536]{1,0:T(8,128)(2,1)} %copy-done.26, bf16[256,1536]{1,0:T(8,128)(2,1)} %bitcast.30, ...), custom_call_target="tpu_custom_call" | custom-call | flops 7000000000 | bytes 1000 | tf_op jit(solution)/shard_map/conv/pallas_call | solution.py:164
  207.1 4.9 %collective-permute-start.17 = (bf16[64,1024]{1,0:T(8,128)(2,1)S(1)}, bf16[64,1024]{1,0:T(8,128)(2,1)S(1)}, u32[]{:S(2)}, u32[]{:S(2)}) collective-permute-start(bf16[64,1024]{1,0:T(8,128)(2,1)S(1)} %copy-done.37), channel_id=1, source_target_pairs={{0,4},{4,0},{8,12},{12,8},{16,20},{20,16},{24,28},{28,24},{1,5},{5... | collective-permute-start | bytes 393224 | tf_op jit(solution)/shard_map/ppermute | solution.py:567
  211.9 1.9 collective-permute-start.18
  214.3 1.2 collective-permute-start.21
  215.5 1.7 collective-permute-start.24
  217.1 1.1 collective-permute-done.18.refs_2_
  218.3 2.5 %collective-permute-start.25 = (bf16[64,1536]{1,0:T(8,128)(2,1)}, bf16[64,1536]{1,0:T(8,128)(2,1)S(1)}, u32[]{:S(2)}, u32[]{:S(2)}) collective-permute-start(bf16[64,1536]{1,0:T(8,128)(2,1)} %get-tuple-element.136), channel_id=1, source_target_pairs={{0,2},{1,3},{2,0},{3,1},{4,6},{5,7},{6,4},{7,5},{8,10},{9,11},{10,... | collective-permute-start | bytes 589832 | tf_op jit(solution)/shard_map/ppermute | solution.py:567
  220.8 2.9 %collective-permute-start.26 = (bf16[64,1536]{1,0:T(8,128)(2,1)}, bf16[64,1536]{1,0:T(8,128)(2,1)S(1)}, u32[]{:S(2)}, u32[]{:S(2)}) collective-permute-start(bf16[64,1536]{1,0:T(8,128)(2,1)} %get-tuple-element.137), channel_id=1, source_target_pairs={{0,3},{1,2},{2,1},{3,0},{4,7},{5,6},{6,5},{7,4},{8,11},{9,10},{10,... | collective-permute-start | bytes 589832 | tf_op jit(solution)/shard_map/ppermute | solution.py:567
  223.7 0.8 collective-permute-start.22
  224.5 1.8 collective-permute-start.23
  226.3 4.7 %collective-permute-done.22.refs_6_ = bf16[64,1024]{1,0:T(8,128)(2,1)S(1)} collective-permute-done((bf16[64,1024]{1,0:T(8,128)(2,1)S(1)}, bf16[64,1024]{1,0:T(8,128)(2,1)S(1)}, u32[]{:S(2)}, u32[]{:S(2)}) %collective-permute-start.22) | collective-permute-done | bytes 131104 | tf_op jit(solution)/shard_map/ppermute | solution.py:567
  231.0 1.4 collective-permute-done.23.refs_7_
  232.4 0.6 copy-done.24
  233.1 3.4 %unpack_obs.1 = f32[512,1024]{1,0:T(8,128)} custom-call(s32[1]{0:T(128)} %bitcast.1.place_ref, bf16[64,1024]{1,0:T(8,128)(2,1)} %get-tuple-element.126.refs_0_, bf16[64,1024]{1,0:T(8,128)(2,1)} %copy-done.18, bf16[64,1024]{1,0:T(8,128)(2,1)} %copy-done.19, bf16[64,1024]{1,0:T(8,128)(2,1)} %copy-done.20, bf16[64,1024]{1,0:T(8,128)(2,1)} %copy-done.21, ...), custom_call_target="tpu_custom_call" | custom-call | flops 1000 | bytes 1000 | tf_op jit(solution)/shard_map/unpack_obs/pallas_call | solution.py:320
  237.6 3.6 %join_rows.1 = bf16[64,8,1440]{2,1,0:T(8,128)(2,1)} custom-call(s32[1]{0:T(128)} %bitcast.place_ref, bf16[256,1536]{1,0:T(8,128)(2,1)} %bitcast.20, bf16[64,1536]{1,0:T(8,128)(2,1)} %get-tuple-element.125.refs_1_, bf16[64,1536]{1,0:T(8,128)(2,1)} %copy-done.15, bf16[64,1536]{1,0:T(8,128)(2,1)} %copy-done.16, bf16[64,1536]{1,0:T(8,128)(2,1)} %copy-done.17), custom_call_target="tpu_custom_call" | custom-call | flops 1000 | bytes 1000 | tf_op jit(solution)/shard_map/join_rows/pallas_call | solution.py:103
  (101 shorter events, 2.8 us)
Async XLA Ops:
  7.5 5.3 %copy-start.32 = (bf16[64,1536]{1,0:T(8,128)(2,1)S(1)}, bf16[64,1536]{1,0:T(8,128)(2,1)}, u32[]{:S(2)}) copy-start(bf16[64,1536]{1,0:T(8,128)(2,1)} %get-tuple-element.72) | copy-start | bytes 589828
  7.5 7.0 %copy-start.31 = (bf16[64,1536]{1,0:T(8,128)(2,1)S(1)}, bf16[64,1536]{1,0:T(8,128)(2,1)}, u32[]{:S(2)}) copy-start(bf16[64,1536]{1,0:T(8,128)(2,1)} %get-tuple-element.73) | copy-start | bytes 589828
  7.5 9.6 %copy-start.30 = (bf16[64,1536]{1,0:T(8,128)(2,1)S(1)}, bf16[64,1536]{1,0:T(8,128)(2,1)}, u32[]{:S(2)}) copy-start(bf16[64,1536]{1,0:T(8,128)(2,1)} %get-tuple-element.74) | copy-start | bytes 589828
  7.5 24.1 %all-to-all-start = ((bf16[8,80,1024]{2,1,0:T(8,128)(2,1)}), bf16[8,80,1024]{2,1,0:T(8,128)(2,1)S(1)}, u32[]{:S(2)}, u32[]{:S(2)}) async-start(bf16[8,80,1024]{2,1,0:T(8,128)(2,1)} %pack_obs.1), calls=%async_computation | async-start | bytes 2621440 | tf_op jit(solution)/shard_map/all_to_all | solution.py:561
  12.8 11.1 %collective-permute-start = (bf16[64,1536]{1,0:T(8,128)(2,1)S(1)}, bf16[64,1536]{1,0:T(8,128)(2,1)S(1)}, u32[]{:S(2)}, u32[]{:S(2)}) collective-permute-start(bf16[64,1536]{1,0:T(8,128)(2,1)S(1)} %copy-done.32), channel_id=1, source_target_pairs={{0,1},{1,0},{2,3},{3,2},{4,5},{5,4},{6,7},{7,6},{8,9},{9,8},{10,11... | collective-permute-start | bytes 589832 | tf_op jit(solution)/shard_map/ppermute | solution.py:567
  14.5 17.1 %collective-permute-start.1 = (bf16[64,1536]{1,0:T(8,128)(2,1)S(1)}, bf16[64,1536]{1,0:T(8,128)(2,1)S(1)}, u32[]{:S(2)}, u32[]{:S(2)}) collective-permute-start(bf16[64,1536]{1,0:T(8,128)(2,1)S(1)} %copy-done.31), channel_id=1, source_target_pairs={{0,2},{1,3},{2,0},{3,1},{4,6},{5,7},{6,4},{7,5},{8,10},{9,11},{10,... | collective-permute-start | bytes 589832 | tf_op jit(solution)/shard_map/ppermute | solution.py:567
  17.1 14.5 %collective-permute-start.2 = (bf16[64,1536]{1,0:T(8,128)(2,1)S(1)}, bf16[64,1536]{1,0:T(8,128)(2,1)S(1)}, u32[]{:S(2)}, u32[]{:S(2)}) collective-permute-start(bf16[64,1536]{1,0:T(8,128)(2,1)S(1)} %copy-done.30), channel_id=1, source_target_pairs={{0,3},{1,2},{2,1},{3,0},{4,7},{5,6},{6,5},{7,4},{8,11},{9,10},{10,... | collective-permute-start | bytes 589832 | tf_op jit(solution)/shard_map/ppermute | solution.py:567
  23.9 14.0 %copy-start.9 = (bf16[64,1536]{1,0:T(8,128)(2,1)}, bf16[64,1536]{1,0:T(8,128)(2,1)S(1)}, u32[]{:S(2)}) copy-start(bf16[64,1536]{1,0:T(8,128)(2,1)S(1)} %collective-permute-done.refs_1_) | copy-start | bytes 589828
  31.6 6.3 %copy-start.10 = (bf16[64,1536]{1,0:T(8,128)(2,1)}, bf16[64,1536]{1,0:T(8,128)(2,1)S(1)}, u32[]{:S(2)}) copy-start(bf16[64,1536]{1,0:T(8,128)(2,1)S(1)} %collective-permute-done.1.refs_2_) | copy-start | bytes 589828
  31.6 6.3 %copy-start.11 = (bf16[64,1536]{1,0:T(8,128)(2,1)}, bf16[64,1536]{1,0:T(8,128)(2,1)S(1)}, u32[]{:S(2)}) copy-start(bf16[64,1536]{1,0:T(8,128)(2,1)S(1)} %collective-permute-done.2.refs_3_) | copy-start | bytes 589828
  31.6 8.4 %copy-start = (bf16[8,80,1024]{2,1,0:T(8,128)(2,1)}, bf16[8,80,1024]{2,1,0:T(8,128)(2,1)S(1)}, u32[]{:S(2)}) copy-start(bf16[8,80,1024]{2,1,0:T(8,128)(2,1)S(1)} %all-to-all-done.obs_ref) | copy-start | bytes 3932164
  31.6 25.9 %all-to-all-start.1 = ((bf16[4,64,1536]{2,1,0:T(8,128)(2,1)}), bf16[4,64,1536]{2,1,0:T(8,128)(2,1)S(1)}, u32[]{:S(2)}, u32[]{:S(2)}) async-start(bf16[4,64,1536]{2,1,0:T(8,128)(2,1)} %bitcast.4), calls=%async_computation.1 | async-start | bytes 1572864 | tf_op jit(solution)/shard_map/all_to_all | solution.py:561
  40.0 20.9 %collective-permute-start.3 = (bf16[256,1536]{1,0:T(8,128)(2,1)}, bf16[256,1536]{1,0:T(8,128)(2,1)S(1)}, u32[]{:S(2)}, u32[]{:S(2)}) collective-permute-start(bf16[256,1536]{1,0:T(8,128)(2,1)} %assemble.2.here_ref), channel_id=1, source_target_pairs={{0,4},{4,8},{8,12},{12,16},{16,20},{20,24},{24,28},{1,5},{5,9},{9,... | collective-permute-start | bytes 2359304 | tf_op jit(solution)/shard_map/ppermute | solution.py:585
  41.4 19.6 %collective-permute-start.4 = (bf16[256,1536]{1,0:T(8,128)(2,1)}, bf16[256,1536]{1,0:T(8,128)(2,1)S(1)}, u32[]{:S(2)}, u32[]{:S(2)}) collective-permute-start(bf16[256,1536]{1,0:T(8,128)(2,1)} %assemble.2.here_ref), channel_id=1, source_target_pairs={{4,0},{8,4},{12,8},{16,12},{20,16},{24,20},{28,24},{5,1},{9,5},{13... | collective-permute-start | bytes 2359304 | tf_op jit(solution)/shard_map/ppermute | solution.py:585
  57.5 10.6 %copy-start.5 = (bf16[4,64,1536]{2,1,0:T(8,128)(2,1)}, bf16[4,64,1536]{2,1,0:T(8,128)(2,1)S(1)}, u32[]{:S(2)}) copy-start(bf16[4,64,1536]{2,1,0:T(8,128)(2,1)S(1)} %all-to-all-done.1) | copy-start | bytes 2359300
  57.5 21.8 %collective-permute-start.5 = (bf16[256,1536]{1,0:T(8,128)(2,1)S(1)}, bf16[256,1536]{1,0:T(8,128)(2,1)}, u32[]{:S(2)}, u32[]{:S(2)}) collective-permute-start(bf16[256,1536]{1,0:T(8,128)(2,1)S(1)} %bitcast.31), channel_id=1, source_target_pairs={{0,4},{4,8},{8,12},{12,16},{16,20},{20,24},{24,28},{1,5},{5,9},{9,... | collective-permute-start | bytes 2359304 | tf_op jit(solution)/shard_map/ppermute | solution.py:585
  59.7 19.6 %collective-permute-start.6 = (bf16[256,1536]{1,0:T(8,128)(2,1)S(1)}, bf16[256,1536]{1,0:T(8,128)(2,1)}, u32[]{:S(2)}, u32[]{:S(2)}) collective-permute-start(bf16[256,1536]{1,0:T(8,128)(2,1)S(1)} %bitcast.32), channel_id=1, source_target_pairs={{4,0},{8,4},{12,8},{16,12},{20,16},{24,20},{28,24},{5,1},{9,5},{13... | collective-permute-start | bytes 2359304 | tf_op jit(solution)/shard_map/ppermute | solution.py:585
  61.0 0.9 copy-start.27
  61.0 1.1 copy-start.29
  68.1 35.2 %all-to-all-start.2 = ((bf16[4,64,1536]{2,1,0:T(8,128)(2,1)}), bf16[4,64,1536]{2,1,0:T(8,128)(2,1)S(1)}, u32[]{:S(2)}, u32[]{:S(2)}) async-start(bf16[4,64,1536]{2,1,0:T(8,128)(2,1)} %bitcast.35), calls=%async_computation.2 | async-start | bytes 1572864 | tf_op jit(solution)/shard_map/all_to_all | solution.py:561
  79.3 10.2 %copy-start.25 = (f32[64]{0:T(128)S(1)}, f32[64]{0:T(128)}, u32[]{:S(2)}) copy-start(f32[64]{0:T(128)} %param.9) | copy-start | bytes 772
  85.1 22.7 %collective-permute-start.7 = (bf16[64,1536]{1,0:T(8,128)(2,1)}, bf16[64,1536]{1,0:T(8,128)(2,1)S(1)}, u32[]{:S(2)}, u32[]{:S(2)}) collective-permute-start(bf16[64,1536]{1,0:T(8,128)(2,1)} %get-tuple-element.98), channel_id=1, source_target_pairs={{0,1},{1,0},{2,3},{3,2},{4,5},{5,4},{6,7},{7,6},{8,9},{9,8},{10,11... | collective-permute-start | bytes 589832 | tf_op jit(solution)/shard_map/ppermute | solution.py:567
  86.9 20.9 %collective-permute-start.8 = (bf16[64,1536]{1,0:T(8,128)(2,1)}, bf16[64,1536]{1,0:T(8,128)(2,1)S(1)}, u32[]{:S(2)}, u32[]{:S(2)}) collective-permute-start(bf16[64,1536]{1,0:T(8,128)(2,1)} %get-tuple-element.99), channel_id=1, source_target_pairs={{0,2},{1,3},{2,0},{3,1},{4,6},{5,7},{6,4},{7,5},{8,10},{9,11},{10,... | collective-permute-start | bytes 589832 | tf_op jit(solution)/shard_map/ppermute | solution.py:567
  89.3 18.6 %collective-permute-start.9 = (bf16[64,1536]{1,0:T(8,128)(2,1)}, bf16[64,1536]{1,0:T(8,128)(2,1)S(1)}, u32[]{:S(2)}, u32[]{:S(2)}) collective-permute-start(bf16[64,1536]{1,0:T(8,128)(2,1)} %get-tuple-element.100), channel_id=1, source_target_pairs={{0,3},{1,2},{2,1},{3,0},{4,7},{5,6},{6,5},{7,4},{8,11},{9,10},{10,... | collective-permute-start | bytes 589832 | tf_op jit(solution)/shard_map/ppermute | solution.py:567
  103.3 0.9 copy-start.1
  134.3 5.9 %collective-permute-start.10 = (bf16[64,1536]{1,0:T(8,128)(2,1)}, bf16[64,1536]{1,0:T(8,128)(2,1)S(1)}, u32[]{:S(2)}, u32[]{:S(2)}) collective-permute-start(bf16[64,1536]{1,0:T(8,128)(2,1)} %get-tuple-element.106), channel_id=1, source_target_pairs={{0,1},{1,0},{2,3},{3,2},{4,5},{5,4},{6,7},{7,6},{8,9},{9,8},{10,11... | collective-permute-start | bytes 589832 | tf_op jit(solution)/shard_map/ppermute | solution.py:567
  135.3 8.9 %collective-permute-start.11 = (bf16[64,1536]{1,0:T(8,128)(2,1)}, bf16[64,1536]{1,0:T(8,128)(2,1)S(1)}, u32[]{:S(2)}, u32[]{:S(2)}) collective-permute-start(bf16[64,1536]{1,0:T(8,128)(2,1)} %get-tuple-element.107), channel_id=1, source_target_pairs={{0,2},{1,3},{2,0},{3,1},{4,6},{5,7},{6,4},{7,5},{8,10},{9,11},{10,... | collective-permute-start | bytes 589832 | tf_op jit(solution)/shard_map/ppermute | solution.py:567
  138.6 11.2 %collective-permute-start.12 = (bf16[64,1536]{1,0:T(8,128)(2,1)}, bf16[64,1536]{1,0:T(8,128)(2,1)S(1)}, u32[]{:S(2)}, u32[]{:S(2)}) collective-permute-start(bf16[64,1536]{1,0:T(8,128)(2,1)} %get-tuple-element.108), channel_id=1, source_target_pairs={{0,3},{1,2},{2,1},{3,0},{4,7},{5,6},{6,5},{7,4},{8,11},{9,10},{10,... | collective-permute-start | bytes 589832 | tf_op jit(solution)/shard_map/ppermute | solution.py:567
  140.3 18.1 %copy-start.12 = (bf16[64,1536]{1,0:T(8,128)(2,1)}, bf16[64,1536]{1,0:T(8,128)(2,1)S(1)}, u32[]{:S(2)}) copy-start(bf16[64,1536]{1,0:T(8,128)(2,1)S(1)} %collective-permute-done.10.refs_1_) | copy-start | bytes 589828
  144.2 14.1 %copy-start.13 = (bf16[64,1536]{1,0:T(8,128)(2,1)}, bf16[64,1536]{1,0:T(8,128)(2,1)S(1)}, u32[]{:S(2)}) copy-start(bf16[64,1536]{1,0:T(8,128)(2,1)S(1)} %collective-permute-done.11.refs_2_) | copy-start | bytes 589828
  149.8 8.5 %copy-start.14 = (bf16[64,1536]{1,0:T(8,128)(2,1)}, bf16[64,1536]{1,0:T(8,128)(2,1)S(1)}, u32[]{:S(2)}) copy-start(bf16[64,1536]{1,0:T(8,128)(2,1)S(1)} %collective-permute-done.12.refs_3_) | copy-start | bytes 589828
  149.8 16.1 %copy-start.3 = (bf16[3,3,256,256]{3,2,1,0:T(8,128)(2,1)S(1)}, bf16[3,3,256,256]{3,2,1,0:T(8,128)(2,1)}, u32[]{:S(2)}) copy-start(bf16[3,3,256,256]{3,2,1,0:T(8,128)(2,1)} %param.8) | copy-start | bytes 3538948
  149.8 29.7 %all-to-all-start.3 = ((bf16[4,64,1536]{2,1,0:T(8,128)(2,1)}), bf16[4,64,1536]{2,1,0:T(8,128)(2,1)S(1)}, u32[]{:S(2)}, u32[]{:S(2)}) async-start(bf16[4,64,1536]{2,1,0:T(8,128)(2,1)} %bitcast.34), calls=%async_computation.3 | async-start | bytes 1572864 | tf_op jit(solution)/shard_map/all_to_all | solution.py:561
  160.5 22.4 %collective-permute-start.13 = (bf16[256,1536]{1,0:T(8,128)(2,1)}, bf16[256,1536]{1,0:T(8,128)(2,1)}, u32[]{:S(2)}, u32[]{:S(2)}) collective-permute-start(bf16[256,1536]{1,0:T(8,128)(2,1)} %assemble.3.here_ref), channel_id=1, source_target_pairs={{0,4},{4,8},{8,12},{12,16},{16,20},{20,24},{24,28},{1,5},{5,9},{9,... | collective-permute-start | bytes 2359304 | tf_op jit(solution)/shard_map/ppermute | solution.py:585
  164.7 18.3 %collective-permute-start.14 = (bf16[256,1536]{1,0:T(8,128)(2,1)}, bf16[256,1536]{1,0:T(8,128)(2,1)}, u32[]{:S(2)}, u32[]{:S(2)}) collective-permute-start(bf16[256,1536]{1,0:T(8,128)(2,1)} %assemble.3.here_ref), channel_id=1, source_target_pairs={{4,0},{8,4},{12,8},{16,12},{20,16},{24,20},{28,24},{5,1},{9,5},{13... | collective-permute-start | bytes 2359304 | tf_op jit(solution)/shard_map/ppermute | solution.py:585
  179.5 9.3 %copy-start.4 = (bf16[4,64,1536]{2,1,0:T(8,128)(2,1)}, bf16[4,64,1536]{2,1,0:T(8,128)(2,1)S(1)}, u32[]{:S(2)}) copy-start(bf16[4,64,1536]{2,1,0:T(8,128)(2,1)S(1)} %all-to-all-done.3) | copy-start | bytes 2359300
  179.5 19.9 %collective-permute-start.15 = (bf16[256,1536]{1,0:T(8,128)(2,1)S(1)}, bf16[256,1536]{1,0:T(8,128)(2,1)S(1)}, u32[]{:S(2)}, u32[]{:S(2)}) collective-permute-start(bf16[256,1536]{1,0:T(8,128)(2,1)S(1)} %bitcast.28), channel_id=1, source_target_pairs={{0,4},{4,8},{8,12},{12,16},{16,20},{20,24},{24,28},{1,5},{5,9},{9,... | collective-permute-start | bytes 2359304 | tf_op jit(solution)/shard_map/ppermute | solution.py:585
  181.6 17.9 %collective-permute-start.16 = (bf16[256,1536]{1,0:T(8,128)(2,1)S(1)}, bf16[256,1536]{1,0:T(8,128)(2,1)S(1)}, u32[]{:S(2)}, u32[]{:S(2)}) collective-permute-start(bf16[256,1536]{1,0:T(8,128)(2,1)S(1)} %bitcast.29), channel_id=1, source_target_pairs={{4,0},{8,4},{12,8},{16,12},{20,16},{24,20},{28,24},{5,1},{9,5},{13... | collective-permute-start | bytes 2359304 | tf_op jit(solution)/shard_map/ppermute | solution.py:585
  188.9 47.7 %all-to-all-start.4 = ((bf16[4,64,1536]{2,1,0:T(8,128)(2,1)}), bf16[4,64,1536]{2,1,0:T(8,128)(2,1)S(1)}, u32[]{:S(2)}, u32[]{:S(2)}) async-start(bf16[4,64,1536]{2,1,0:T(8,128)(2,1)} %bitcast.27), calls=%async_computation.4 | async-start | bytes 1572864 | tf_op jit(solution)/shard_map/all_to_all | solution.py:561
  199.4 7.6 %copy-start.37 = (bf16[64,1024]{1,0:T(8,128)(2,1)S(1)}, bf16[64,1024]{1,0:T(8,128)(2,1)}, u32[]{:S(2)}) copy-start(bf16[64,1024]{1,0:T(8,128)(2,1)} %get-tuple-element.127) | copy-start | bytes 393220
  199.4 12.5 %copy-start.34 = (bf16[64,1024]{1,0:T(8,128)(2,1)S(1)}, bf16[64,1024]{1,0:T(8,128)(2,1)}, u32[]{:S(2)}) copy-start(bf16[64,1024]{1,0:T(8,128)(2,1)} %get-tuple-element.128) | copy-start | bytes 393220
  199.4 14.4 %copy-start.33 = (bf16[64,1024]{1,0:T(8,128)(2,1)S(1)}, bf16[64,1024]{1,0:T(8,128)(2,1)}, u32[]{:S(2)}) copy-start(bf16[64,1024]{1,0:T(8,128)(2,1)} %get-tuple-element.129) | copy-start | bytes 393220
  199.4 14.4 %copy-start.39 = (bf16[64,1024]{1,0:T(8,128)(2,1)S(1)}, bf16[64,1024]{1,0:T(8,128)(2,1)}, u32[]{:S(2)}) copy-start(bf16[64,1024]{1,0:T(8,128)(2,1)} %get-tuple-element.130) | copy-start | bytes 393220
  199.4 14.8 %copy-start.38 = (bf16[64,1024]{1,0:T(8,128)(2,1)S(1)}, bf16[64,1024]{1,0:T(8,128)(2,1)}, u32[]{:S(2)}) copy-start(bf16[64,1024]{1,0:T(8,128)(2,1)} %get-tuple-element.131) | copy-start | bytes 393220
  199.4 24.2 %copy-start.36 = (bf16[64,1024]{1,0:T(8,128)(2,1)S(1)}, bf16[64,1024]{1,0:T(8,128)(2,1)}, u32[]{:S(2)}) copy-start(bf16[64,1024]{1,0:T(8,128)(2,1)} %get-tuple-element.132) | copy-start | bytes 393220
  199.5 25.0 %copy-start.35 = (bf16[64,1024]{1,0:T(8,128)(2,1)S(1)}, bf16[64,1024]{1,0:T(8,128)(2,1)}, u32[]{:S(2)}) copy-start(bf16[64,1024]{1,0:T(8,128)(2,1)} %get-tuple-element.133) | copy-start | bytes 393220
  200.4 0.9 copy-start.28
  207.1 8.4 %collective-permute-start.17 = (bf16[64,1024]{1,0:T(8,128)(2,1)S(1)}, bf16[64,1024]{1,0:T(8,128)(2,1)S(1)}, u32[]{:S(2)}, u32[]{:S(2)}) collective-permute-start(bf16[64,1024]{1,0:T(8,128)(2,1)S(1)} %copy-done.37), channel_id=1, source_target_pairs={{0,4},{4,0},{8,12},{12,8},{16,20},{20,16},{24,28},{28,24},{1,5},{5... | collective-permute-start | bytes 393224 | tf_op jit(solution)/shard_map/ppermute | solution.py:567
  211.9 6.3 %collective-permute-start.18 = (bf16[64,1024]{1,0:T(8,128)(2,1)S(1)}, bf16[64,1024]{1,0:T(8,128)(2,1)S(1)}, u32[]{:S(2)}, u32[]{:S(2)}) collective-permute-start(bf16[64,1024]{1,0:T(8,128)(2,1)S(1)} %copy-done.34), channel_id=1, source_target_pairs={{0,8},{4,12},{8,0},{12,4},{16,24},{20,28},{24,16},{28,20},{1,9},{5... | collective-permute-start | bytes 393224 | tf_op jit(solution)/shard_map/ppermute | solution.py:567
  213.8 6.9 %collective-permute-start.19 = (bf16[64,1024]{1,0:T(8,128)(2,1)S(1)}, bf16[64,1024]{1,0:T(8,128)(2,1)S(1)}, u32[]{:S(2)}, u32[]{:S(2)}) collective-permute-start(bf16[64,1024]{1,0:T(8,128)(2,1)S(1)} %copy-done.33), channel_id=1, source_target_pairs={{0,12},{4,8},{8,4},{12,0},{16,28},{20,24},{24,20},{28,16},{1,13},{... | collective-permute-start | bytes 393224 | tf_op jit(solution)/shard_map/ppermute | solution.py:567
  213.8 9.8 %collective-permute-start.20 = (bf16[64,1024]{1,0:T(8,128)(2,1)S(1)}, bf16[64,1024]{1,0:T(8,128)(2,1)S(1)}, u32[]{:S(2)}, u32[]{:S(2)}) collective-permute-start(bf16[64,1024]{1,0:T(8,128)(2,1)S(1)} %copy-done.39), channel_id=1, source_target_pairs={{0,16},{4,20},{8,24},{12,28},{16,0},{20,4},{24,8},{28,12},{1,17},{... | collective-permute-start | bytes 393224 | tf_op jit(solution)/shard_map/ppermute | solution.py:567
  214.3 10.2 %collective-permute-start.21 = (bf16[64,1024]{1,0:T(8,128)(2,1)S(1)}, bf16[64,1024]{1,0:T(8,128)(2,1)S(1)}, u32[]{:S(2)}, u32[]{:S(2)}) collective-permute-start(bf16[64,1024]{1,0:T(8,128)(2,1)S(1)} %copy-done.38), channel_id=1, source_target_pairs={{0,20},{4,16},{8,28},{12,24},{16,4},{20,0},{24,12},{28,8},{1,21},{... | collective-permute-start | bytes 393224 | tf_op jit(solution)/shard_map/ppermute | solution.py:567
  215.5 16.9 %copy-start.18 = (bf16[64,1024]{1,0:T(8,128)(2,1)}, bf16[64,1024]{1,0:T(8,128)(2,1)S(1)}, u32[]{:S(2)}) copy-start(bf16[64,1024]{1,0:T(8,128)(2,1)S(1)} %collective-permute-done.17.refs_1_) | copy-start | bytes 393220
  215.5 21.0 %collective-permute-start.24 = (bf16[64,1536]{1,0:T(8,128)(2,1)}, bf16[64,1536]{1,0:T(8,128)(2,1)S(1)}, u32[]{:S(2)}, u32[]{:S(2)}) collective-permute-start(bf16[64,1536]{1,0:T(8,128)(2,1)} %get-tuple-element.135), channel_id=1, source_target_pairs={{0,1},{1,0},{2,3},{3,2},{4,5},{5,4},{6,7},{7,6},{8,9},{9,8},{10,11... | collective-permute-start | bytes 589832 | tf_op jit(solution)/shard_map/ppermute | solution.py:567
  218.3 14.1 %copy-start.19 = (bf16[64,1024]{1,0:T(8,128)(2,1)}, bf16[64,1024]{1,0:T(8,128)(2,1)S(1)}, u32[]{:S(2)}) copy-start(bf16[64,1024]{1,0:T(8,128)(2,1)S(1)} %collective-permute-done.18.refs_2_) | copy-start | bytes 393220
  218.3 18.2 %collective-permute-start.25 = (bf16[64,1536]{1,0:T(8,128)(2,1)}, bf16[64,1536]{1,0:T(8,128)(2,1)S(1)}, u32[]{:S(2)}, u32[]{:S(2)}) collective-permute-start(bf16[64,1536]{1,0:T(8,128)(2,1)} %get-tuple-element.136), channel_id=1, source_target_pairs={{0,2},{1,3},{2,0},{3,1},{4,6},{5,7},{6,4},{7,5},{8,10},{9,11},{10,... | collective-permute-start | bytes 589832 | tf_op jit(solution)/shard_map/ppermute | solution.py:567
  220.8 11.6 %copy-start.20 = (bf16[64,1024]{1,0:T(8,128)(2,1)}, bf16[64,1024]{1,0:T(8,128)(2,1)S(1)}, u32[]{:S(2)}) copy-start(bf16[64,1024]{1,0:T(8,128)(2,1)S(1)} %collective-permute-done.19.refs_3_) | copy-start | bytes 393220
  220.8 15.8 %collective-permute-start.26 = (bf16[64,1536]{1,0:T(8,128)(2,1)}, bf16[64,1536]{1,0:T(8,128)(2,1)S(1)}, u32[]{:S(2)}, u32[]{:S(2)}) collective-permute-start(bf16[64,1536]{1,0:T(8,128)(2,1)} %get-tuple-element.137), channel_id=1, source_target_pairs={{0,3},{1,2},{2,1},{3,0},{4,7},{5,6},{6,5},{7,4},{8,11},{9,10},{10,... | collective-permute-start | bytes 589832 | tf_op jit(solution)/shard_map/ppermute | solution.py:567
  223.7 8.7 %copy-start.21 = (bf16[64,1024]{1,0:T(8,128)(2,1)}, bf16[64,1024]{1,0:T(8,128)(2,1)S(1)}, u32[]{:S(2)}) copy-start(bf16[64,1024]{1,0:T(8,128)(2,1)S(1)} %collective-permute-done.20.refs_4_) | copy-start | bytes 393220
  223.7 7.3 %collective-permute-start.22 = (bf16[64,1024]{1,0:T(8,128)(2,1)S(1)}, bf16[64,1024]{1,0:T(8,128)(2,1)S(1)}, u32[]{:S(2)}, u32[]{:S(2)}) collective-permute-start(bf16[64,1024]{1,0:T(8,128)(2,1)S(1)} %copy-done.36), channel_id=1, source_target_pairs={{0,24},{4,28},{8,16},{12,20},{16,8},{20,12},{24,0},{28,4},{1,25},{... | collective-permute-start | bytes 393224 | tf_op jit(solution)/shard_map/ppermute | solution.py:567
  224.5 7.9 %copy-start.22 = (bf16[64,1024]{1,0:T(8,128)(2,1)}, bf16[64,1024]{1,0:T(8,128)(2,1)S(1)}, u32[]{:S(2)}) copy-start(bf16[64,1024]{1,0:T(8,128)(2,1)S(1)} %collective-permute-done.21.refs_5_) | copy-start | bytes 393220
  224.5 7.9 %collective-permute-start.23 = (bf16[64,1024]{1,0:T(8,128)(2,1)S(1)}, bf16[64,1024]{1,0:T(8,128)(2,1)S(1)}, u32[]{:S(2)}, u32[]{:S(2)}) collective-permute-start(bf16[64,1024]{1,0:T(8,128)(2,1)S(1)} %copy-done.35), channel_id=1, source_target_pairs={{0,28},{4,24},{8,20},{12,16},{16,12},{20,8},{24,4},{28,0},{1,29},{... | collective-permute-start | bytes 393224 | tf_op jit(solution)/shard_map/ppermute | solution.py:567
  231.0 1.4 copy-start.23
  236.5 1.0 copy-start.2
  (8 other events, 5.8 us)
